TPU v7x, 32 devices: a whole 2x2x4 slice. The times are simulated.
32 devices in a mesh: dp: 8 (over z, x), tensor: 4 (over y, core).
Axes of the slice: x: 2, y: 2, z: 4, core: 2. Of those that a mesh axis runs over, the one named last changes fastest.
Arguments:
- tokens: bfloat16 [16384, 480], P(('dp', 'tensor')), may hold values from -6 to 6
- cotangent: bfloat16 [16384, 480], P(('dp', 'tensor')), may hold values from -6 to 6
- lengths: int32 [32], P('dp'), may hold values from 64 to 512, as said below
- clusters: int32 [32], P('dp'), may hold values from 0 to 63
- cluster_weight: float32 [64], replicated, may hold values from 0.5 to 2
- qkv_master: float32 [4, 172800], P('tensor', 'dp'), may hold values from -0.25 to 0.25
- qkv_moment: float32 [4, 172800], P('tensor', 'dp'), may hold values from -160 to 160
- qkv_square: float32 [4, 172800], P('tensor', 'dp'), may hold values from 737.28 to 2949.12
- qkv_ema: float32 [4, 172800], P('tensor', 'dp'), may hold values from -0.25 to 0.25
- out_master: float32 [4, 57600], P('tensor', 'dp'), may hold values from -1.5 to 1.5
- out_moment: float32 [4, 57600], P('tensor', 'dp'), may hold values from -56 to 56
- out_square: float32 [4, 57600], P('tensor', 'dp'), may hold values from 81.92 to 327.68
- out_ema: float32 [4, 57600], P('tensor', 'dp'), may hold values from -1.5 to 1.5
- up_master: float32 [921600], P(('dp', 'tensor')), may hold values from -0.25 to 0.25
- up_moment: float32 [921600], P(('dp', 'tensor')), may hold values from -160 to 160
- up_square: float32 [921600], P(('dp', 'tensor')), may hold values from 737.28 to 2949.12
- up_ema: float32 [921600], P(('dp', 'tensor')), may hold values from -0.25 to 0.25
- down_master: float32 [921600], P(('dp', 'tensor')), may hold values from -0.125 to 0.125
- down_moment: float32 [921600], P(('dp', 'tensor')), may hold values from -320 to 320
- down_square: float32 [921600], P(('dp', 'tensor')), may hold values from 2949.12 to 11796.48
- down_ema: float32 [921600], P(('dp', 'tensor')), may hold values from -0.125 to 0.125
- norm_master: float32 [4, 480], replicated
- norm_moment: float32 [4, 480], replicated, may hold values from -512 to 512
- norm_square: float32 [4, 480], replicated, may hold values from 8192 to 32768
- norm_ema: float32 [4, 480], replicated
Outputs:
- layer_out: float32 [16384, 480], P(('dp', 'tensor'))
- tokens_grad: float32 [16384, 480], P(('dp', 'tensor'))
- qkv_new: float32 [4, 172800], P('tensor', 'dp')
- qkv_moment_new: float32 [4, 172800], P('tensor', 'dp')
- qkv_square_new: float32 [4, 172800], P('tensor', 'dp')
- qkv_ema_new: float32 [4, 172800], P('tensor', 'dp')
- out_new: float32 [4, 57600], P('tensor', 'dp')
- out_moment_new: float32 [4, 57600], P('tensor', 'dp')
- out_square_new: float32 [4, 57600], P('tensor', 'dp')
- out_ema_new: float32 [4, 57600], P('tensor', 'dp')
- up_new: float32 [921600], P(('dp', 'tensor'))
- up_moment_new: float32 [921600], P(('dp', 'tensor'))
- up_square_new: float32 [921600], P(('dp', 'tensor'))
- up_ema_new: float32 [921600], P(('dp', 'tensor'))
- down_new: float32 [921600], P(('dp', 'tensor'))
- down_moment_new: float32 [921600], P(('dp', 'tensor'))
- down_square_new: float32 [921600], P(('dp', 'tensor'))
- down_ema_new: float32 [921600], P(('dp', 'tensor'))
- norm_new: float32 [4, 480], replicated
- norm_moment_new: float32 [4, 480], replicated
- norm_square_new: float32 [4, 480], replicated
- norm_ema_new: float32 [4, 480], replicated
Inputs may be any that keep to these rules, and one draw needn't show every extreme that they name: `lengths`: protein 0 has length 512; token slots at positions >= a protein's length are padding.
All inputs are finite; a program needn't handle non-finite values.
Results may differ from a plain program's by a relative error of at most 0.009.
The roundings to bfloat16 on the way count: a program that leaves them out, or rounds other values in their place, can miss the bound.
Values may be sent and summed in bfloat16 or wider, within the bound.
A program may use at most 256 MiB of HBM per device.

v0:
```python
import jax
import jax.numpy as jnp
from jax import lax
from jax.sharding import PartitionSpec as P

D = 480
HEAD = 24
FF = 1920
MAXLEN = 512
QBLK = 512


norm_eps = 1e-05
beta_one = 0.5
beta_two = 0.5
adam_eps = 1e-08
decay_rate = 0.01
average_keep = 0.75
rope_base = 10000.0
masked_score = -1e30


def norm_rows(values, gain, shift):
    middle = jnp.mean(values, axis=-1, keepdims=True)
    centered = values - middle
    spread = jnp.mean(centered * centered, axis=-1, keepdims=True)
    inverse = lax.rsqrt(spread + norm_eps)
    plain = centered * inverse
    return (plain * gain + shift, plain, inverse)


def norm_back(upstream, plain, inverse, gain):
    gain_grad = jnp.sum(upstream * plain, axis=0)
    shift_grad = jnp.sum(upstream, axis=0)
    scaled = upstream * gain
    first_term = jnp.mean(scaled, axis=-1, keepdims=True)
    second_term = jnp.mean(scaled * plain, axis=-1, keepdims=True)
    return (inverse * (scaled - first_term - plain * second_term), gain_grad, shift_grad)


def gelu_value(inputs):
    return 0.5 * inputs * (1.0 + lax.erf(inputs * 0.7071067811865476))


def gelu_slope(inputs):
    return (
        0.5 * (1.0 + lax.erf(inputs * 0.7071067811865476))
        + inputs * jnp.exp(-0.5 * inputs * inputs) * 0.3989422804014327
    )


def rope_tables(count):
    position = (lax.iota(jnp.int32, count) % MAXLEN).astype(jnp.float32)
    exponent = jnp.arange(HEAD // 2, dtype=jnp.float32) * (2.0 / HEAD)
    inverse_freq = rope_base ** (-exponent)
    angle = position[:, None] * inverse_freq[None, :]
    cosine = jnp.cos(angle)
    sine_table = jnp.sin(angle)
    return (jnp.concatenate([cosine, cosine], -1), jnp.concatenate([sine_table, sine_table], -1))


def rotate(block, cosine, sine_table):
    half_size = HEAD // 2
    turned = jnp.concatenate([-block[..., half_size:], block[..., :half_size]], -1)
    return block * cosine[:, None, :] + turned * sine_table[:, None, :]


def unrotate(grad_block, cosine, sine_table):
    half_size = HEAD // 2
    scaled = grad_block * sine_table[:, None, :]
    turned = jnp.concatenate([scaled[..., half_size:], -scaled[..., :half_size]], -1)
    return grad_block * cosine[:, None, :] + turned


def scores_block(query_block, key_rows, length):
    product = jnp.einsum(
        "qhe,khe->hqk", query_block, key_rows, preferred_element_type=jnp.float32
    ) * HEAD ** (-0.5)
    usable = lax.iota(jnp.int32, key_rows.shape[0]) < length
    return jnp.where(usable[None, None, :], product, masked_score)


def forward_blocks(queries, key_rows, vectors, length):
    head_count = queries.shape[1]

    def forward_one_block(counter, query_block):
        scores = scores_block(query_block, key_rows, length)
        largest = jnp.max(scores, axis=-1, keepdims=True)
        exponent = jnp.exp(scores - largest)
        summed = jnp.sum(exponent, axis=-1, keepdims=True)
        probability = (exponent / summed).astype(jnp.bfloat16)
        result = jnp.einsum(
            "hqk,khe->qhe", probability, vectors, preferred_element_type=jnp.float32
        )
        return (counter, (result, (largest + jnp.log(summed))[..., 0]))

    blocks = queries.reshape(MAXLEN // QBLK, QBLK, head_count, HEAD)
    unused, outputs = lax.scan(forward_one_block, 0, blocks)
    return (outputs[0].reshape(MAXLEN, head_count, HEAD), outputs[1])


def backward_blocks(queries, key_rows, vectors, logsum, grad_rows, length):
    head_count = queries.shape[1]
    scale = HEAD ** (-0.5)

    def backward_one_block(totals, inputs):
        query_block, lse_block, grad_block = inputs
        scores = scores_block(query_block, key_rows, length)
        probability = jnp.exp(scores - lse_block[..., None])
        prob_low = probability.astype(jnp.bfloat16)
        grad_prob = jnp.einsum(
            "qhe,khe->hqk", grad_block, vectors, preferred_element_type=jnp.float32
        )
        centre = jnp.sum(probability * grad_prob, axis=-1, keepdims=True)
        grad_score = (probability * (grad_prob - centre)).astype(jnp.bfloat16)
        grad_query = (
            jnp.einsum("hqk,khe->qhe", grad_score, key_rows, preferred_element_type=jnp.float32)
            * scale
        )
        key_total = (
            totals[0]
            + jnp.einsum(
                "hqk,qhe->khe", grad_score, query_block, preferred_element_type=jnp.float32
            )
            * scale
        )
        value_total = totals[1] + jnp.einsum(
            "hqk,qhe->khe", prob_low, grad_block, preferred_element_type=jnp.float32
        )
        return ((key_total, value_total), grad_query)

    block_shape = (MAXLEN // QBLK, QBLK, head_count, HEAD)
    zero_keys = jnp.zeros((key_rows.shape[0], head_count, HEAD), jnp.float32)
    sums, query_grads = lax.scan(
        backward_one_block,
        (zero_keys, zero_keys),
        (queries.reshape(block_shape), logsum, grad_rows.reshape(block_shape)),
    )
    return (query_grads.reshape(MAXLEN, head_count, HEAD), sums[0], sums[1])


def attend_forward(inputs):
    queries, key_rows, vectors, length = inputs
    return forward_blocks(queries, key_rows, vectors, length)


def attend_backward(inputs):
    queries, key_rows, vectors, logsum, grad_rows, length = inputs
    return backward_blocks(queries, key_rows, vectors, logsum, grad_rows, length)


def adam_step(master, moment, square, average, grad, rate):
    moment_new = beta_one * moment + (1.0 - beta_one) * grad
    square_new = beta_two * square + (1.0 - beta_two) * grad * grad
    update = moment_new / (jnp.sqrt(square_new) + adam_eps) + decay_rate * master
    fresh = master - rate * update
    average_new = average_keep * average + (1.0 - average_keep) * fresh
    return (fresh, moment_new, square_new, average_new)


def on_device(
    tokens,
    cotangent,
    lengths,
    clusters,
    cluster_weight,
    qkv_master,
    qkv_moment,
    qkv_square,
    qkv_ema,
    out_master,
    out_moment,
    out_square,
    out_ema,
    up_master,
    up_moment,
    up_square,
    up_ema,
    down_master,
    down_moment,
    down_square,
    down_ema,
    norm_master,
    norm_moment,
    norm_square,
    norm_ema,
):
    local_rows = tokens.shape[0]
    tensor_count = lax.axis_size("tensor")
    group_rows = local_rows * tensor_count
    protein_count = lengths.shape[0]
    head_pieces = (
        lax.all_gather(qkv_master.astype(jnp.bfloat16), "dp", axis=1, tiled=True),
        lax.all_gather(out_master.astype(jnp.bfloat16), "dp", axis=1, tiled=True),
    )
    joined_weight = head_pieces[0].reshape(D, -1)
    out_weight = head_pieces[1].reshape(-1, D)
    dense_pieces = (
        lax.all_gather(up_master.astype(jnp.bfloat16), ("dp", "tensor"), axis=0, tiled=True),
        lax.all_gather(down_master.astype(jnp.bfloat16), ("dp", "tensor"), axis=0, tiled=True),
    )
    up_weight = dense_pieces[0].reshape(D, FF)
    down_weight = dense_pieces[1].reshape(FF, D)
    head_width = out_weight.shape[0]
    head_count = head_width // HEAD
    tok_float = tokens.astype(jnp.float32)
    normed_one, plain_one, inverse_one = norm_rows(tok_float, norm_master[0], norm_master[1])
    act_one = normed_one.astype(jnp.bfloat16)
    group_act = lax.all_gather(act_one, "tensor", axis=0, tiled=True)
    joined_rows = jnp.dot(group_act, joined_weight, preferred_element_type=jnp.float32)
    cosine, sine_table = rope_tables(group_rows)
    queries = rotate(
        joined_rows[:, :head_width].reshape(group_rows, head_count, HEAD), cosine, sine_table
    ).astype(jnp.bfloat16)
    key_rows = rotate(
        joined_rows[:, head_width : 2 * head_width].reshape(group_rows, head_count, HEAD),
        cosine,
        sine_table,
    ).astype(jnp.bfloat16)
    vectors = (
        joined_rows[:, 2 * head_width :].reshape(group_rows, head_count, HEAD).astype(jnp.bfloat16)
    )
    block_shape = (protein_count, MAXLEN, head_count, HEAD)
    query_four = queries.reshape(block_shape)
    key_four = key_rows.reshape(block_shape)
    value_four = vectors.reshape(block_shape)
    attn_rows, logsum = lax.map(attend_forward, (query_four, key_four, value_four, lengths))
    attended = attn_rows.reshape(group_rows, head_width).astype(jnp.bfloat16)
    sliced = attended
    projected = lax.psum_scatter(
        jnp.dot(sliced, out_weight, preferred_element_type=jnp.float32),
        "tensor",
        scatter_dimension=0,
        tiled=True,
    )
    residual = tok_float + projected
    normed_two, plain_two, inverse_two = norm_rows(residual, norm_master[2], norm_master[3])
    act_two = normed_two.astype(jnp.bfloat16)
    upper_pre = jnp.dot(act_two, up_weight, preferred_element_type=jnp.float32)
    active = gelu_value(upper_pre).astype(jnp.bfloat16)
    layer_out = residual + jnp.dot(active, down_weight, preferred_element_type=jnp.float32)
    row_index = lax.axis_index("tensor") * local_rows + lax.iota(jnp.int32, local_rows)
    owner_hit = (row_index // MAXLEN)[:, None] == lax.iota(jnp.int32, protein_count)[None, :]
    cluster_hit = (
        clusters[:, None] == lax.iota(jnp.int32, cluster_weight.shape[0])[None, :]
    ).astype(jnp.float32)
    protein_scale = jnp.sum(cluster_hit * cluster_weight[None, :], axis=1)
    row_length = jnp.sum(jnp.where(owner_hit, lengths[None, :], 0), axis=1)
    row_scale = jnp.sum(jnp.where(owner_hit, protein_scale[None, :], 0.0), axis=1)
    row_scale = jnp.where(row_index % MAXLEN < row_length, row_scale, 0.0)
    grad_y = cotangent.astype(jnp.float32) * row_scale[:, None]
    grad_low = grad_y.astype(jnp.bfloat16)
    d_active = jnp.dot(grad_low, down_weight.T, preferred_element_type=jnp.float32)
    d_upper = (d_active * gelu_slope(upper_pre)).astype(jnp.bfloat16)
    grad_down = jnp.dot(active.T, grad_low, preferred_element_type=jnp.float32)
    grad_up = jnp.dot(act_two.T, d_upper, preferred_element_type=jnp.float32)
    d_normed_two = jnp.dot(d_upper, up_weight.T, preferred_element_type=jnp.float32)
    d_from_norm, gain_two_grad, shift_two_grad = norm_back(
        d_normed_two, plain_two, inverse_two, norm_master[2]
    )
    d_residual = grad_y + d_from_norm
    d_res_low = d_residual.astype(jnp.bfloat16)
    group_grad = lax.all_gather(d_res_low, "tensor", axis=0, tiled=True)
    d_attended = jnp.dot(group_grad, out_weight.T, preferred_element_type=jnp.float32).astype(
        jnp.bfloat16
    )
    grad_out = jnp.dot(attended.T, group_grad, preferred_element_type=jnp.float32)
    grad_four = d_attended.reshape(block_shape)
    query_grad, key_grad, value_grad = lax.map(
        attend_backward, (query_four, key_four, value_four, logsum, grad_four, lengths)
    )
    query_grad = unrotate(query_grad.reshape(group_rows, head_count, HEAD), cosine, sine_table)
    key_grad = unrotate(key_grad.reshape(group_rows, head_count, HEAD), cosine, sine_table)
    d_joined = jnp.concatenate(
        [
            query_grad.reshape(group_rows, head_width),
            key_grad.reshape(group_rows, head_width),
            value_grad.reshape(group_rows, head_width),
        ],
        1,
    ).astype(jnp.bfloat16)
    grad_qkv = jnp.dot(group_act.T, d_joined, preferred_element_type=jnp.float32)
    sliced = d_joined
    d_normed_one = lax.psum_scatter(
        jnp.dot(sliced, joined_weight.T, preferred_element_type=jnp.float32),
        "tensor",
        scatter_dimension=0,
        tiled=True,
    )
    d_from_first, gain_one_grad, shift_one_grad = norm_back(
        d_normed_one, plain_one, inverse_one, norm_master[0]
    )
    tokens_grad = d_residual + d_from_first
    head_sums = (
        lax.psum_scatter(grad_qkv.reshape(1, -1), "dp", scatter_dimension=1, tiled=True),
        lax.psum_scatter(grad_out.reshape(1, -1), "dp", scatter_dimension=1, tiled=True),
    )
    dense_sums = (
        lax.psum_scatter(grad_up.reshape(-1), ("dp", "tensor"), scatter_dimension=0, tiled=True),
        lax.psum_scatter(grad_down.reshape(-1), ("dp", "tensor"), scatter_dimension=0, tiled=True),
    )
    norm_grad = lax.psum(
        jnp.stack([gain_one_grad, shift_one_grad, gain_two_grad, shift_two_grad], 0),
        ("dp", "tensor"),
    )
    qkv_all = adam_step(qkv_master, qkv_moment, qkv_square, qkv_ema, head_sums[0], D ** (-0.5))
    out_all = adam_step(
        out_master, out_moment, out_square, out_ema, head_sums[1], (D // 32) ** (-0.5)
    )
    up_all = adam_step(up_master, up_moment, up_square, up_ema, dense_sums[0], D ** (-0.5))
    down_all = adam_step(
        down_master, down_moment, down_square, down_ema, dense_sums[1], FF ** (-0.5)
    )
    norm_all = adam_step(norm_master, norm_moment, norm_square, norm_ema, norm_grad, 0.2)
    return (
        layer_out,
        tokens_grad,
        qkv_all[0],
        qkv_all[1],
        qkv_all[2],
        qkv_all[3],
        out_all[0],
        out_all[1],
        out_all[2],
        out_all[3],
        up_all[0],
        up_all[1],
        up_all[2],
        up_all[3],
        down_all[0],
        down_all[1],
        down_all[2],
        down_all[3],
        norm_all[0],
        norm_all[1],
        norm_all[2],
        norm_all[3],
    )


def solution(mesh):
    return jax.shard_map(
        on_device,
        mesh=mesh,
        in_specs=(
            P(("dp", "tensor"), None),
            P(("dp", "tensor"), None),
            P("dp"),
            P("dp"),
            P(),
            P("tensor", "dp"),
            P("tensor", "dp"),
            P("tensor", "dp"),
            P("tensor", "dp"),
            P("tensor", "dp"),
            P("tensor", "dp"),
            P("tensor", "dp"),
            P("tensor", "dp"),
            P(("dp", "tensor")),
            P(("dp", "tensor")),
            P(("dp", "tensor")),
            P(("dp", "tensor")),
            P(("dp", "tensor")),
            P(("dp", "tensor")),
            P(("dp", "tensor")),
            P(("dp", "tensor")),
            P(),
            P(),
            P(),
            P(),
        ),
        out_specs=(
            P(("dp", "tensor"), None),
            P(("dp", "tensor"), None),
            P("tensor", "dp"),
            P("tensor", "dp"),
            P("tensor", "dp"),
            P("tensor", "dp"),
            P("tensor", "dp"),
            P("tensor", "dp"),
            P("tensor", "dp"),
            P("tensor", "dp"),
            P(("dp", "tensor")),
            P(("dp", "tensor")),
            P(("dp", "tensor")),
            P(("dp", "tensor")),
            P(("dp", "tensor")),
            P(("dp", "tensor")),
            P(("dp", "tensor")),
            P(("dp", "tensor")),
            P(),
            P(),
            P(),
            P(),
        ),
        check_vma=False,
    )
```

profile of v0, /device:TPU:0, one launch (start us, length us, event | category | flops | bytes accessed | tf_op | source)
XLA Modules:
  0.0 2303.6 jit_solution(2817682420576331939)
XLA Ops:
  17.8 2.0 fusion.64
  23.1 66.9 %all-reduce.11.cloned.1.call-done = (bf16[172800]{0:T(1024)(128)(2,1)}, bf16[57600]{0:T(1024)(128)(2,1)}) async-done(((bf16[172800]{0:T(1024)(128)(2,1)}, bf16[57600]{0:T(1024)(128)(2,1)}), (bf16[172800]{0:T(1024)(128)(2,1)}, bf16[57600]{0:T(1024)(128)(2,1)})) %all-reduce.11.cloned.1.call-update) | async-done | bytes 460816
  90.1 1.9 reshape.302
  92.0 1.8 reshape.307
  93.9 2.5 fusion.118
  97.8 1.6 reshape.303
  100.5 2.3 concatenate.43
  102.8 2.2 concatenate.44
  109.0 2.1 fusion.78
  111.4 20.9 while.10
  132.7 2.6 fusion.119
  135.8 40.9 %reduce.2 = bf16[32,28800]{1,0:T(8,128)(2,1)} reduce(bf16[32,1,28800]{2,1,0:T(2,128)(2,1)} %all-gather.11.cloned.1.call-done, bf16[]{:T(256)} %constant.209), dimensions={1}, to_apply=%all-gather.reduce_sub_computation | reduce | bytes 3686402 | tf_op jit(solution)/shard_map/all_gather | solution.py:199
  176.7 5.2 reshape.308
  181.9 40.8 %reduce.3 = bf16[32,28800]{1,0:T(8,128)(2,1)} reduce(bf16[32,1,28800]{2,1,0:T(2,128)(2,1)} %all-gather.13.cloned.1.call-done, bf16[]{:T(256)} %constant.209), dimensions={1}, to_apply=%all-gather.1.reduce_sub_computation | reduce | bytes 3686402 | tf_op jit(solution)/shard_map/all_gather | solution.py:200
  222.7 14.1 reshape.309
  238.4 4.7 multiply_convert_fusion.1
  243.1 2.4 fusion.56
  245.6 2.1 multiply_reduce_fusion.1
  251.3 19.4 all-gather.9.cloned.1.call-done
  270.7 2.3 fusion.120
  273.0 41.7 %reshape.343 = f32[1,57600]{0,1:T(8,128)} reshape(f32[120,480]{1,0:T(8,128)S(1)} %fusion.120) | data formatting | bytes 460800 | tf_op jit(solution)/shard_map/reshape | solution.py:296
  314.7 4.6 fusion.106
  319.3 4.7 reshape.318
  324.1 4.7 fusion.82
  328.7 6.1 reshape.319
  335.7 2.0 convolution_convert_fusion
  340.7 99.8 %while.27 = (s32[]{:T(128)}, f32[4,512,5,24]{1,0,3,2:T(4,128)}, f32[4,512,5,24]{1,0,3,2:T(4,128)}, bf16[4,512,5,24]{1,3,2,0:T(8,128)(2,1)}, bf16[4,512,5,24]{1,3...) while((s32[]{:T(128)}, f32[4,512,5,24]{1,0,3,2:T(4,128)}, ...), condition=%wide.region_16.17_spmd, body=%wide.region_14.16_spmd.sunk | while | flops 334354432 | bytes 42974368 | solution.py:269
  343.1 2.0 fusion.172
  345.1 2.7 multiply_reduce_fusion.7
  347.8 1.7 multiply_convert_fusion.3
  351.3 7.3 dynamic_update_slice.37
  358.6 7.3 dynamic_update_slice.36
  368.0 1.9 fusion.172
  370.0 2.7 multiply_reduce_fusion.7
  372.7 1.7 multiply_convert_fusion.3
  376.2 7.3 dynamic_update_slice.37
  383.5 7.3 dynamic_update_slice.36
  392.9 1.9 fusion.172
  394.9 2.7 multiply_reduce_fusion.7
  397.6 1.7 multiply_convert_fusion.3
  401.1 7.3 dynamic_update_slice.37
  408.4 7.3 dynamic_update_slice.36
  417.8 1.9 fusion.172
  419.8 2.7 multiply_reduce_fusion.7
  422.5 1.7 multiply_convert_fusion.3
  426.0 7.3 dynamic_update_slice.37
  433.3 7.2 dynamic_update_slice.36
  442.8 2.8 reshape.314
  445.9 2.9 reshape.312
  448.8 1.5 copy.138
  450.3 1.8 broadcast_multiply_fusion.1
  455.7 37.9 %reshape.342 = f32[1,172800]{0,1:T(8,128)} reshape(f32[480,360]{1,0:T(8,128)S(1)} %fusion.80) | data formatting | bytes 1382400 | tf_op jit(solution)/shard_map/reshape | solution.py:295
  495.2 3.9 convolution_add_fusion
  499.0 3.1 fusion.81
  502.3 341.8 %reduce-scatter.15.cloned.1.call-done = f32[7200,1]{1,0:T(8,128)} async-done(((f32[57600,1]{1,0:T(8,128)}), f32[7200,1]{1,0:T(8,128)}) %reduce-scatter.15.cloned.1.call-update) | async-done | bytes 28816
  844.1 2.7 copy.118
  847.7 1.8 multiply_add_fusion.4
  849.5 1.8 multiply_add_fusion.3
  851.4 1355.8 %reduce-scatter.13.cloned.1.call-done = f32[21600,1]{1,0:T(8,128)} async-done(((f32[172800,1]{1,0:T(8,128)}), f32[21600,1]{1,0:T(8,128)}) %reduce-scatter.13.cloned.1.call-update) | async-done | bytes 86416
  2207.3 6.4 copy.116
  2215.1 36.4 %reduce-scatter.11.cloned.1.call-done = f32[512,480]{0,1:T(8,128)} async-done(((f32[2048,480]{0,1:T(8,128)}), f32[512,480]{0,1:T(8,128)}) %reduce-scatter.11.cloned.1.call-update) | async-done | bytes 983056 | tf_op jit(solution)/shard_map/reduce_scatter | solution.py:284
  2251.5 1.7 fusion.69
  2253.2 39.4 %psum.7 = f32[4,480]{1,0:T(4,128)S(1)} all-reduce(f32[4,480]{1,0:T(4,128)S(1)} %pad_maximum_fusion.9), channel_id=1, replica_groups=mesh['dp'=8,'tensor'=4] {'dp','tensor'}, use_global_device_ids=true, to_apply=%region_28.29 | all-reduce | flops 1920 | bytes 15360 | tf_op jit(solution)/shard_map/psum | solution.py:302
  2293.2 2.8 fusion.68
  (277 shorter events, 75.0 us)
Async XLA Ops:
  8.0 11.9 copy-start.25
  8.0 12.7 copy-start.27
  8.0 82.0 %all-reduce.11.cloned.1.call-start = ((), (), s32[]{:S(2)}) async-start(), calls=%async_computation.13 | async-start | bytes 925696
  14.5 79.4 %all-gather.7.cloned.1.call-start = ((), (), s32[]{:S(2)}) async-start(), calls=%async_computation.4 | async-start | bytes 2457600 | tf_op jit(solution)/shard_map/all_gather | solution.py:209
  15.7 80.7 %copy-start.41 = (f32[512]{0:T(512)}, f32[512]{0:T(512)S(1)}, u32[]{:S(2)}) copy-start(f32[512]{0:T(512)S(1)} %broadcast_multiply_fusion.7) | copy-start | bytes 6148
  17.7 78.7 %copy-start.45 = (f32[1,480]{1,0:T(1,128)}, f32[1,480]{1,0:T(1,128)S(1)}, u32[]{:S(2)}) copy-start(f32[1,480]{1,0:T(1,128)S(1)} %get-tuple-element.332) | copy-start | bytes 5764
  17.8 78.6 %copy-start.43 = (f32[512]{0:T(512)}, f32[512]{0:T(512)S(1)}, u32[]{:S(2)}) copy-start(f32[512]{0:T(512)S(1)} %add_rsqrt_fusion.1) | copy-start | bytes 6148
  19.8 116.0 %all-gather.11.cloned.1.call-start = ((), (), s32[]{:S(2)}) async-start(), calls=%async_computation.8 | async-start | bytes 3801600 | tf_op jit(solution)/shard_map/all_gather | solution.py:199
  20.6 161.2 %all-gather.13.cloned.1.call-start = ((), (), s32[]{:S(2)}) async-start(), calls=%async_computation.9 | async-start | bytes 3801600 | tf_op jit(solution)/shard_map/all_gather | solution.py:200
  21.5 215.4 %reduce-scatter.9.cloned.1.call-start = ((), (), s32[]{:S(2)}) async-start(), calls=%async_computation.5 | async-start | bytes 4915200 | tf_op jit(solution)/shard_map/reduce_scatter | solution.py:230
  92.0 4.4 copy-start.13
  100.5 8.5 copy-start.7
  109.0 2.3 copy-start.60
  111.4 21.3 copy-start.16
  132.3 3.0 copy-start.9
  132.7 2.7 copy-start.61
  132.7 2.7 copy-start.62
  135.3 135.3 %all-gather.9.cloned.1.call-start = ((), (), s32[]{:S(2)}) async-start(), calls=%async_computation.6 | async-start | bytes 2457600 | tf_op jit(solution)/shard_map/all_gather | solution.py:263
  181.8 55.0 %copy-start = (bf16[512,480]{0,1:T(8,128)(2,1)S(1)}, bf16[512,480]{0,1:T(8,128)(2,1)}, u32[]{:S(2)}) copy-start(bf16[512,480]{0,1:T(8,128)(2,1)} %param.29) | copy-start | bytes 1474564
  238.4 4.7 copy-start.3
  238.4 4.7 copy-start.10
  243.1 2.4 copy-start.12
  245.5 2.1 copy-start.11
  247.6 2.2 copy-start.51
  247.7 2.2 copy-start.53
  249.8 594.3 %reduce-scatter.15.cloned.1.call-start = ((), (), s32[]{:S(2)}) async-start(), calls=%async_computation.11 | async-start | bytes 33177600
  314.7 533.0 %all-reduce.9.cloned.1.call-start = ((), (), s32[]{:S(2)}) async-start(), calls=%async_computation.12 | async-start | bytes 14745600
  334.8 1872.3 %reduce-scatter.13.cloned.1.call-start = ((), (), s32[]{:S(2)}) async-start(), calls=%async_computation.10 | async-start | bytes 99532800
  440.5 5.1 copy-start.6
  452.5 2.0 copy-start.2
  493.6 1757.8 %reduce-scatter.11.cloned.1.call-start = ((), (), s32[]{:S(2)}) async-start(), calls=%async_computation.7 | async-start | bytes 4915200 | tf_op jit(solution)/shard_map/reduce_scatter | solution.py:284
  495.2 3.9 copy-start.14
  495.2 3.9 copy-start.20
  495.2 3.9 copy-start.22
  495.2 3.9 copy-start.24
  502.1 344.6 %copy-start.37 = (f32[1,7200]{1,0:T(1,128)S(1)}, f32[1,7200]{1,0:T(1,128)}, u32[]{:S(2)}) copy-start(f32[1,7200]{1,0:T(1,128)} %param.38) | copy-start | bytes 86404
  502.1 344.7 %copy-start.48 = (f32[1,7200]{1,0:T(1,128)S(1)}, f32[1,7200]{1,0:T(1,128)}, u32[]{:S(2)}) copy-start(f32[1,7200]{1,0:T(1,128)} %param.41) | copy-start | bytes 86404
  502.1 344.7 %copy-start.49 = (f32[1,7200]{1,0:T(1,128)S(1)}, f32[1,7200]{1,0:T(1,128)}, u32[]{:S(2)}) copy-start(f32[1,7200]{1,0:T(1,128)} %param.40) | copy-start | bytes 86404
  502.2 344.7 %copy-start.50 = (f32[1,7200]{1,0:T(1,128)S(1)}, f32[1,7200]{1,0:T(1,128)}, u32[]{:S(2)}) copy-start(f32[1,7200]{1,0:T(1,128)} %param.39) | copy-start | bytes 86404
  502.2 345.5 %copy-start.26 = (f32[28800]{0:T(1024)S(1)}, f32[28800]{0:T(1024)}, u32[]{:S(2)}) copy-start(f32[28800]{0:T(1024)} %param.42) | copy-start | bytes 345604
  502.2 345.5 %copy-start.31 = (f32[28800]{0:T(1024)S(1)}, f32[28800]{0:T(1024)}, u32[]{:S(2)}) copy-start(f32[28800]{0:T(1024)} %param.45) | copy-start | bytes 345604
  502.2 345.5 %copy-start.32 = (f32[28800]{0:T(1024)S(1)}, f32[28800]{0:T(1024)}, u32[]{:S(2)}) copy-start(f32[28800]{0:T(1024)} %param.44) | copy-start | bytes 345604
  502.2 345.5 %copy-start.33 = (f32[28800]{0:T(1024)S(1)}, f32[28800]{0:T(1024)}, u32[]{:S(2)}) copy-start(f32[28800]{0:T(1024)} %param.43) | copy-start | bytes 345604
  502.2 347.3 %copy-start.28 = (f32[28800]{0:T(1024)S(1)}, f32[28800]{0:T(1024)}, u32[]{:S(2)}) copy-start(f32[28800]{0:T(1024)} %param.46) | copy-start | bytes 345604
  502.2 347.3 %copy-start.34 = (f32[28800]{0:T(1024)S(1)}, f32[28800]{0:T(1024)}, u32[]{:S(2)}) copy-start(f32[28800]{0:T(1024)} %param.49) | copy-start | bytes 345604
  502.2 347.3 %copy-start.35 = (f32[28800]{0:T(1024)S(1)}, f32[28800]{0:T(1024)}, u32[]{:S(2)}) copy-start(f32[28800]{0:T(1024)} %param.48) | copy-start | bytes 345604
  502.2 347.3 %copy-start.36 = (f32[28800]{0:T(1024)S(1)}, f32[28800]{0:T(1024)}, u32[]{:S(2)}) copy-start(f32[28800]{0:T(1024)} %param.47) | copy-start | bytes 345604
  2207.1 6.6 copy-start.30
  2207.1 6.6 copy-start.38
  2207.1 6.6 copy-start.39
  2207.1 6.6 copy-start.40
  2207.1 44.3 %copy-start.1 = (bf16[512,480]{0,1:T(8,128)(2,1)S(1)}, bf16[512,480]{0,1:T(8,128)(2,1)}, u32[]{:S(2)}) copy-start(bf16[512,480]{0,1:T(8,128)(2,1)} %param.29) | copy-start | bytes 1474564
  2207.2 44.3 %copy-start.42 = (f32[512]{0:T(512)S(1)}, f32[512]{0:T(512)}, u32[]{:S(2)}) copy-start(f32[512]{0:T(512)} %copy-done.41) | copy-start | bytes 6148
  2207.2 44.3 %copy-start.44 = (f32[512]{0:T(512)S(1)}, f32[512]{0:T(512)}, u32[]{:S(2)}) copy-start(f32[512]{0:T(512)} %copy-done.43) | copy-start | bytes 6148
  2207.2 44.3 %copy-start.46 = (f32[1,480]{1,0:T(1,128)S(1)}, f32[1,480]{1,0:T(1,128)}, u32[]{:S(2)}) copy-start(f32[1,480]{1,0:T(1,128)} %copy-done.45) | copy-start | bytes 5764
  2207.2 46.0 %copy-start.58 = (f32[480]{0:T(512)S(1)}, f32[480]{0:T(512)}, u32[]{:S(2)}) copy-start(f32[480]{0:T(512)} %get-tuple-element.238) | copy-start | bytes 5764
  2207.2 46.0 %copy-start.59 = (f32[480]{0:T(512)S(1)}, f32[480]{0:T(512)}, u32[]{:S(2)}) copy-start(f32[480]{0:T(512)} %get-tuple-element.245) | copy-start | bytes 5764
  2207.2 85.3 %copy-start.47 = (f32[4,480]{1,0:T(4,128)S(1)}, f32[4,480]{1,0:T(4,128)}, u32[]{:S(2)}) copy-start(f32[4,480]{1,0:T(4,128)} %param.50) | copy-start | bytes 23044
  2207.2 85.3 %copy-start.55 = (f32[4,480]{1,0:T(4,128)S(1)}, f32[4,480]{1,0:T(4,128)}, u32[]{:S(2)}) copy-start(f32[4,480]{1,0:T(4,128)} %param.53) | copy-start | bytes 23044
  2207.2 85.3 %copy-start.56 = (f32[4,480]{1,0:T(4,128)S(1)}, f32[4,480]{1,0:T(4,128)}, u32[]{:S(2)}) copy-start(f32[4,480]{1,0:T(4,128)} %param.52) | copy-start | bytes 23044
  2207.2 85.3 %copy-start.57 = (f32[4,480]{1,0:T(4,128)S(1)}, f32[4,480]{1,0:T(4,128)}, u32[]{:S(2)}) copy-start(f32[4,480]{1,0:T(4,128)} %param.51) | copy-start | bytes 23044
  2207.3 86.0 %copy-start.5 = (f32[512,480]{0,1:T(8,128)S(1)}, f32[512,480]{0,1:T(8,128)}, u32[]{:S(2)}) copy-start(f32[512,480]{0,1:T(8,128)} %copy-done.4) | copy-start | bytes 2949124
  2207.3 86.0 %copy-start.52 = (f32[512]{0:T(512)S(1)}, f32[512]{0:T(512)}, u32[]{:S(2)}) copy-start(f32[512]{0:T(512)} %copy-done.51) | copy-start | bytes 6148
  2207.3 86.0 %copy-start.54 = (f32[512]{0:T(512)S(1)}, f32[512]{0:T(512)}, u32[]{:S(2)}) copy-start(f32[512]{0:T(512)} %copy-done.53) | copy-start | bytes 6148
  (9 other events, 9.5 us)
Sparse Core Ops, SparseCore 0:
  14.6 75.4 all-reduce.10
  314.8 529.2 reduce-scatter.14
  848.0 1359.0 reduce-scatter.12
  2209.5 41.8 reduce-scatter.10
Sparse Core Ops, SparseCore 1:
  19.9 24.2 all-gather.6
  47.6 60.8 all-gather.10
  111.8 59.1 all-gather.12
  173.5 41.2 reduce-scatter.8
  249.9 20.7 all-gather.8
  334.9 472.1 all-reduce.8
where the time goes:
time: 2310 us; the launch traced here: 2300 us
  waiting for transfers between devices  1820 us (79%)
  local copies, waits for them, and re-layouts  221 us (10%)
  other arithmetic  129 us (6%)
  matrix products  73.9 us (3%)
  blocking collectives  39.4 us (2%)
    unnamed x14, waiting for transfers between devices  1760 us
    dynamic_update_slice x16, local copies, waits for them, and re-layouts, on_device(): lax.map(attend_forward, (query_four, key_four, value_four, lengths))  60.2 us
  transfers between devices with their start and end apart: 10, of which 5 were waited for; matrix products, arithmetic and copies ran while one was open for 15% of the time, Pallas kernels for 0%

commit v1 on v0

v1 whole, which is shorter than its diff:
```python
import jax
import jax.numpy as jnp
import numpy as np
from jax import lax
from jax.experimental import pallas as pl
from jax.experimental.pallas import tpu as pltpu
from jax.sharding import PartitionSpec as P

D = 480
HEAD = 24
FF = 1920
MAXLEN = 512
NDP, NTEN = 8, 4
WIDE = 512
HEADS_DEV = 5
LANES = 128
TILES = 47
UP0, DOWN0, QKV0, OUT0 = 0, 15, 31, 43
CHUNK = 384
QB = 256

norm_eps = 1e-05
beta_one = 0.5
beta_two = 0.5
adam_eps = 1e-08
decay_rate = 0.01
average_keep = 0.75
masked_score = -1e30
MESH = pl.DeviceIdType.MESH
f32, bf16 = jnp.float32, jnp.bfloat16


def mm(a, b):
    return lax.dot_general(a, b, (((1,), (0,)), ((), ())), preferred_element_type=f32)


def mm_nt(a, b):
    return lax.dot_general(a, b, (((1,), (1,)), ((), ())), preferred_element_type=f32)


def constants():
    natural = np.arange(D)
    squeeze = np.zeros((WIDE, WIDE), np.float32)
    squeeze[natural, 16 * (natural // 15) + natural % 15] = 1.0
    spread = np.zeros((CHUNK, CHUNK), np.float32)
    for third in range(3):
        lane = np.arange(120)
        spread[third * 120 + lane, third * 128 + lane] = 1.0
    position = np.arange(MAXLEN, dtype=np.float32)
    exponent = np.arange(HEAD // 2, dtype=np.float32) * np.float32(2.0 / HEAD)
    inverse = np.float32(10000.0) ** (-exponent)
    angle = (position[:, None] * inverse[None, :]).astype(np.float32).astype(np.float64)
    lane = np.arange(120)
    place = lane % HEAD
    cosine = np.zeros((MAXLEN, LANES), np.float32)
    first = np.zeros((MAXLEN, LANES), np.float32)
    second = np.zeros((MAXLEN, LANES), np.float32)
    cosine[:, :120] = np.cos(angle)[:, place % 12]
    sines = np.sin(angle)[:, place % 12]
    first[:, :120] = np.where(place < 12, -sines, 0.0)
    second[:, :120] = np.where(place >= 12, sines, 0.0)
    low = lambda v: jnp.asarray(v.astype(jnp.bfloat16))
    return (low(squeeze), low(squeeze.T), low(spread), jnp.asarray(cosine), jnp.asarray(first), jnp.asarray(second))


def gelu_parts(u):
    half = 0.5 * (1.0 + lax.erf(u * 0.7071067811865476))
    return u * half, half + u * jnp.exp(-0.5 * u * u) * 0.3989422804014327


def layer_kernel(
    lengths, clusters, weights_of, W, tok, cot, norm, squeeze, widen, spread, cosine, first, second,
    layer_out, tokens_grad, G, norm_grad,
    up_s, down_s, qkv_s, out_s, q_s, k_s, v_s, kT_s, vT_s, P_s, OT_s, att_s, dA_s, dqT_s, dk_s, dv_s,
    act1_s, act2_s, act_pad, plain1, plain2, res_s, y_s, dn_s, dres_s, dlow_s, active_s, gdown_s, x_s,
):
    me = lax.axis_index("tensor")
    length = lengths[me]
    scale_row = weights_of[clusters[me]]
    scale = HEAD ** -0.5

    sq = squeeze[...]

    def up_tile(c, carry):
        part = mm(sq, W[:, :, UP0 + c].reshape(WIDE, LANES)).astype(bf16)
        up_s[:, pl.ds(pl.multiple_of(c * LANES, LANES), LANES)] = part
        return carry

    for c in range(15):
        up_tile(c, 0)
    for t in range(NTEN):
        pieces = [W[:, t, QKV0 + 4 * c : QKV0 + 4 * c + 4].reshape(WIDE, LANES) for c in range(3)]
        plain = mm(sq, jnp.concatenate(pieces, 1)).astype(bf16)
        qkv_s[t] = mm(plain, spread[...]).astype(bf16)
        pieces = [W[:, t, OUT0 + c].reshape(LANES, LANES) for c in range(4)]
        out_s[t] = mm(squeeze[:LANES, :LANES], jnp.concatenate(pieces, 1)).astype(bf16)

    def down_rows(k, carry):
        pieces = [W[k, :, DOWN0 + 4 * c : DOWN0 + 4 * c + 4].reshape(256, LANES) for c in range(4)]
        part = mm(squeeze[:240, :256], jnp.concatenate(pieces, 1)).astype(bf16)
        down_s[pl.ds(pl.multiple_of(k * 240, 16), 240), :] = part
        return carry

    lax.fori_loop(0, 8, down_rows, 0)

    lane = lax.broadcasted_iota(jnp.int32, (1, WIDE), 1)
    real = jnp.where(lane < D, 1.0, 0.0)
    gains = norm[...]

    def norm_rows(values, gain, shift):
        middle = jnp.sum(values, axis=-1, keepdims=True) * (1.0 / D)
        centered = (values - middle) * real
        spread_ = jnp.sum(centered * centered, axis=-1, keepdims=True) * (1.0 / D)
        inverse = lax.rsqrt(spread_ + norm_eps)
        plain = centered * inverse
        return plain * gain + shift, plain, inverse

    def norm_back(dz, plain, inverse, gain):
        dg = jnp.sum(dz * plain, axis=0, keepdims=True)
        db = jnp.sum(dz, axis=0, keepdims=True)
        scaled = dz * gain
        one = jnp.sum(scaled, axis=-1, keepdims=True) * (1.0 / D)
        two = jnp.sum(scaled * plain, axis=-1, keepdims=True) * (1.0 / D)
        return inverse * (scaled - one - plain * two) * real, dg, db

    x_s[...] = jnp.zeros_like(x_s)
    x_s[:, :D] = tok[...].astype(f32)
    normed, plain, inverse1 = norm_rows(x_s[...], gains[0:1], gains[1:2])
    plain1[...] = plain
    act1_s[...] = normed.astype(bf16)
    cosv, firstv, secondv = cosine[...], first[...], second[...]
    for t in range(NTEN):
        joined = mm(act1_s[...], qkv_s[t])
        for number in range(2):
            u = joined[:, number * LANES : (number + 1) * LANES]
            r = u * cosv + pltpu.roll(u, LANES - 12, 1) * firstv + pltpu.roll(u, 12, 1) * secondv
            if number == 0:
                q_s[t] = r.astype(bf16)
            else:
                k_s[t] = r.astype(bf16)
                kT_s[t] = r.T.astype(bf16)
        v = joined[:, 2 * LANES :]
        v_s[t] = v.astype(bf16)
        vT_s[t] = v.T.astype(bf16)

    lane_id = lax.broadcasted_iota(jnp.int32, (1, LANES), 1)
    row_id = lax.broadcasted_iota(jnp.int32, (LANES, 1), 0)
    key_id = lax.broadcasted_iota(jnp.int32, (MAXLEN, 1), 0)
    usable = key_id < length

    OT_s[...] = jnp.zeros_like(OT_s)

    def forward_head(h, carry):
        t = h // HEADS_DEV
        begin = (h - t * HEADS_DEV) * HEAD
        lanes = jnp.where((lane_id >= begin) & (lane_id < begin + HEAD), 1.0, 0.0).astype(bf16)
        rows = jnp.where((row_id >= begin) & (row_id < begin + HEAD), 1.0, 0.0).astype(bf16)
        keys = k_s[t] * lanes
        values = vT_s[t] * rows
        for b in range(MAXLEN // QB):
            cols = slice(b * QB, (b + 1) * QB)
            s = mm_nt(keys, q_s[t, cols, :])
            s = jnp.where(usable, s * scale, masked_score)
            top = jnp.max(s, axis=0, keepdims=True)
            e = jnp.exp(s - top)
            total = jnp.sum(e, axis=0, keepdims=True)
            p = (e * (1.0 / total)).astype(bf16)
            P_s[h, :, cols] = p
            OT_s[t, :, cols] += mm(values, p)
        return carry

    lax.fori_loop(0, NTEN * HEADS_DEV, forward_head, 0)

    res = x_s[...]
    for t in range(NTEN):
        att_s[t] = OT_s[t].T.astype(bf16)
        res = res + mm(att_s[t], out_s[t])
    res_s[...] = res
    normed, plain, inverse2 = norm_rows(res, gains[2:3], gains[3:4])
    plain2[...] = plain
    act2_s[...] = normed.astype(bf16)
    act_pad[...] = mm_nt(widen[...], act2_s[...]).astype(bf16)

    row = lax.broadcasted_iota(jnp.int32, (MAXLEN, 1), 0)
    row_scale = jnp.where(row < length, scale_row, 0.0)
    grad = cot[...].astype(f32) * row_scale
    dres_s[...] = jnp.zeros_like(dres_s)
    dres_s[:, :D] = grad
    dlow_s[...] = dres_s[...].astype(bf16)

    y_s[...] = res_s[...]
    dn_s[...] = jnp.zeros_like(dn_s)
    eye_row = lax.broadcasted_iota(jnp.int32, (CHUNK, CHUNK), 0)
    eye_col = lax.broadcasted_iota(jnp.int32, (CHUNK, CHUNK), 1)
    eye = jnp.where(eye_row == eye_col, 1.0, 0.0).astype(bf16)
    active_s[...] = eye

    def hidden_chunk(c, carry):
        cols = pl.ds(pl.multiple_of(c * CHUNK, LANES), CHUNK)
        u = mm(act2_s[...], up_s[:, cols])
        value, slope = gelu_parts(u)
        a = value.astype(bf16)
        y_s[...] += mm(a, down_s[cols, :])
        d_active = mm_nt(dlow_s[...], down_s[cols, :])
        d_upper = (d_active * slope).astype(bf16)
        dn_s[...] += mm_nt(d_upper, up_s[:, cols])
        g_up = mm(act_pad[...], d_upper).astype(bf16)
        for part in range(3):
            G[:, :, UP0 + 3 * c + part] = g_up[:, part * LANES : (part + 1) * LANES].reshape(NDP, NTEN, 16, LANES)
        aT = mm_nt(active_s[...], a).astype(bf16)
        gdown_s[cols, :] = mm(aT, dlow_s[...]).astype(bf16)
        return carry

    lax.fori_loop(0, FF // CHUNK, hidden_chunk, 0)
    layer_out[...] = y_s[:, :D]

    def down_groups(k, carry):
        part = mm(widen[:256, :240], gdown_s[pl.ds(pl.multiple_of(k * 240, 16), 240), :]).astype(bf16)
        for c in range(4):
            G[k, :, DOWN0 + 4 * c : DOWN0 + 4 * c + 4] = part[:, c * LANES : (c + 1) * LANES].reshape(NTEN, 4, 16, LANES)
        return carry

    lax.fori_loop(0, 8, down_groups, 0)

    d_from, dg2, db2 = norm_back(dn_s[...], plain2[...], inverse2, gains[2:3])
    d_res = dres_s[...] + d_from
    dres_s[...] = d_res
    dlow_s[...] = d_res.astype(bf16)

    for t in range(NTEN):
        dA_s[t] = mm_nt(dlow_s[...], out_s[t]).astype(bf16)
        attT = mm_nt(widen[:LANES, :LANES], att_s[t]).astype(bf16)
        part = mm(attT, dlow_s[...]).astype(bf16)
        for c in range(4):
            G[:, t, OUT0 + c] = part[:, c * LANES : (c + 1) * LANES].reshape(NDP, 16, LANES)

    dqT_s[...] = jnp.zeros_like(dqT_s)
    dk_s[...] = jnp.zeros_like(dk_s)
    dv_s[...] = jnp.zeros_like(dv_s)

    def backward_head(h, carry):
        t = h // HEADS_DEV
        begin = (h - t * HEADS_DEV) * HEAD
        lanes = jnp.where((lane_id >= begin) & (lane_id < begin + HEAD), 1.0, 0.0).astype(bf16)
        rows = jnp.where((row_id >= begin) & (row_id < begin + HEAD), 1.0, 0.0).astype(bf16)
        values = v_s[t]
        keysT = kT_s[t] * rows
        for b in range(MAXLEN // QB):
            cols = slice(b * QB, (b + 1) * QB)
            dA = dA_s[t, cols, :] * lanes
            dP = mm_nt(values, dA)
            low = P_s[h, :, cols]
            p = low.astype(f32)
            centre = jnp.sum(p * dP, axis=0, keepdims=True)
            ds = (p * (dP - centre)).astype(bf16)
            dv_s[t] += mm(low, dA)
            dk_s[t] += mm(ds, q_s[t, cols, :] * lanes)
            dqT_s[t, :, cols] += mm(keysT, ds)
        return carry

    lax.fori_loop(0, NTEN * HEADS_DEV, backward_head, 0)

    act_pad[...] = mm_nt(widen[...], act1_s[...]).astype(bf16)
    dz = jnp.zeros((MAXLEN, WIDE), f32)
    for t in range(NTEN):
        pieces = []
        for number in range(2):
            g = (dqT_s[t].T if number == 0 else dk_s[t]) * scale
            r = g * cosv - pltpu.roll(g, LANES - 12, 1) * firstv - pltpu.roll(g, 12, 1) * secondv
            pieces.append(r.astype(bf16))
        pieces.append(dv_s[t].astype(bf16))
        d_joined = jnp.concatenate(pieces, 1)
        dz = dz + mm_nt(d_joined, qkv_s[t])
        natural = mm_nt(d_joined, spread[...]).astype(bf16)
        part = mm(act_pad[...], natural).astype(bf16)
        for c in range(3):
            G[:, t, QKV0 + 4 * c : QKV0 + 4 * c + 4] = part[:, c * LANES : (c + 1) * LANES].reshape(NDP, 4, 16, LANES)
    d_from, dg1, db1 = norm_back(dz, plain1[...], inverse1, gains[0:1])
    x_s[...] = dres_s[...] + d_from
    tokens_grad[...] = x_s[:, :D]
    norm_grad[...] = jnp.concatenate([dg1, db1, dg2, db2, jnp.zeros((4, WIDE), f32)], 0)


def run_layer(lengths, clusters, cluster_weight, tiles, tokens, cotangent, norm_master):
    rows = MAXLEN
    wide_norm = jnp.pad(norm_master, ((0, 0), (0, WIDE - D)))
    smem = pl.BlockSpec(memory_space=pltpu.SMEM)
    vmem = pl.BlockSpec(memory_space=pltpu.VMEM)
    head_set = (NTEN, MAXLEN, LANES)
    turned = (NTEN, LANES, MAXLEN)
    wide = (rows, WIDE)
    return pl.pallas_call(
        layer_kernel,
        out_shape=(
            jax.ShapeDtypeStruct((rows, D), f32),
            jax.ShapeDtypeStruct((rows, D), f32),
            jax.ShapeDtypeStruct((NDP, NTEN, TILES, 16, LANES), bf16),
            jax.ShapeDtypeStruct((8, WIDE), f32),
        ),
        in_specs=[smem] * 3 + [vmem] * 10,
        out_specs=[vmem] * 4,
        scratch_shapes=[
            pltpu.VMEM((WIDE, FF), bf16),
            pltpu.VMEM((FF, WIDE), bf16),
            pltpu.VMEM((NTEN, WIDE, CHUNK), bf16),
            pltpu.VMEM((NTEN, LANES, WIDE), bf16),
            pltpu.VMEM(head_set, bf16),
            pltpu.VMEM(head_set, bf16),
            pltpu.VMEM(head_set, bf16),
            pltpu.VMEM(turned, bf16),
            pltpu.VMEM(turned, bf16),
            pltpu.VMEM((NTEN * HEADS_DEV, MAXLEN, MAXLEN), bf16),
            pltpu.VMEM(turned, f32),
            pltpu.VMEM(head_set, bf16),
            pltpu.VMEM(head_set, bf16),
            pltpu.VMEM(turned, f32),
            pltpu.VMEM(head_set, f32),
            pltpu.VMEM(head_set, f32),
            pltpu.VMEM(wide, bf16),
            pltpu.VMEM(wide, bf16),
            pltpu.VMEM(wide, bf16),
            pltpu.VMEM(wide, f32),
            pltpu.VMEM(wide, f32),
            pltpu.VMEM(wide, f32),
            pltpu.VMEM(wide, f32),
            pltpu.VMEM(wide, f32),
            pltpu.VMEM(wide, f32),
            pltpu.VMEM(wide, bf16),
            pltpu.VMEM((CHUNK, CHUNK), bf16),
            pltpu.VMEM((FF, WIDE), bf16),
            pltpu.VMEM(wide, f32),
        ],
        compiler_params=pltpu.CompilerParams(vmem_limit_bytes=60 * 1024 * 1024),
        name="layer",
    )(lengths, clusters, cluster_weight, tiles, tokens, cotangent, wide_norm, *constants())


def shard_tiles(up, down, qkv, out):
    up = jnp.pad(up.reshape(15, 15, LANES), ((0, 1), (0, 0), (0, 0))).transpose(1, 0, 2)
    down = jnp.pad(down.reshape(4, 15, D), ((0, 0), (0, 1), (0, WIDE - D)))
    down = down.reshape(4, 16, 4, LANES).transpose(2, 0, 1, 3).reshape(16, 16, LANES)
    qkv = jnp.pad(qkv.reshape(4, 15, 360), ((0, 0), (0, 1), (0, CHUNK - 360)))
    qkv = qkv.reshape(4, 16, 3, LANES).transpose(2, 0, 1, 3).reshape(12, 16, LANES)
    out = jnp.pad(out.reshape(15, D), ((0, 1), (0, WIDE - D)))
    out = out.reshape(16, 4, LANES).transpose(1, 0, 2)
    return jnp.concatenate([up, down, qkv, out], 0)


def tiles_shard(tiles):
    up = tiles[UP0:DOWN0, :15].transpose(1, 0, 2).reshape(-1)
    down = tiles[DOWN0:QKV0].reshape(4, 4, 16, LANES).transpose(1, 2, 0, 3)[:, :15].reshape(60, WIDE)[:, :D].reshape(-1)
    qkv = tiles[QKV0:OUT0].reshape(3, 4, 16, LANES).transpose(1, 2, 0, 3)[:, :15].reshape(60, CHUNK)[:, :360].reshape(1, -1)
    out = tiles[OUT0:].transpose(1, 0, 2)[:15].reshape(15, WIDE)[:, :D].reshape(1, -1)
    return up, down, qkv, out


ROUTES = (
    (0, 19, (0, 1, 3, 2, 4)),
    (19, 19, (0, 1, 2, 3, 4)),
    (38, 9, (2, 3, 0, 1, 4)),
)


def place():
    dp, tensor = lax.axis_index("dp"), lax.axis_index("tensor")
    return (dp // 4, (dp // 2) % 2, dp % 2, tensor // 2, tensor % 2)


def partner(coords, dim):
    c = list(coords)
    c[dim] = 1 - c[dim]
    return (c[0] * 4 + c[1] * 2 + c[2], c[3] * 2 + c[4])


def greet(coords):
    barrier = pltpu.get_barrier_semaphore()
    for dim in range(5):
        pl.semaphore_signal(barrier, inc=1, device_id=partner(coords, dim), device_id_type=MESH)
    pl.semaphore_wait(barrier, 5)


def gather_kernel(shard, whole, send, recv, own_sem):
    coords = place()
    greet(coords)
    own = pltpu.make_async_copy(shard, whole.at[coords], own_sem)
    own.start()
    copies = [[None] * 5 for _ in ROUTES]
    for stage in range(5):
        for r, (begin, count, order) in enumerate(ROUTES):
            if stage > 0:
                copies[r][stage - 1].wait_recv()
            if stage == 1 and r == 0:
                own.wait()
            done, dim = order[:stage], order[stage]
            where = tuple(slice(None) if d in done else coords[d] for d in range(5)) + (pl.ds(begin, count),)
            copies[r][stage] = pltpu.make_async_remote_copy(
                src_ref=shard.at[pl.ds(begin, count)] if stage == 0 else whole.at[where],
                dst_ref=whole.at[where],
                send_sem=send.at[r, stage],
                recv_sem=recv.at[r, stage],
                device_id=partner(coords, dim),
                device_id_type=MESH,
            )
            copies[r][stage].start()
    for r in range(len(ROUTES)):
        copies[r][4].wait_recv()
    for r in range(len(ROUTES)):
        for stage in range(5):
            copies[r][stage].wait_send()


def gather(shard):
    n = len(ROUTES)
    whole = pl.pallas_call(
        gather_kernel,
        out_shape=jax.ShapeDtypeStruct((2, 2, 2, 2, 2, TILES, 16, LANES), bf16),
        in_specs=[pl.BlockSpec(memory_space=pltpu.VMEM)],
        out_specs=pl.BlockSpec(memory_space=pltpu.VMEM),
        scratch_shapes=[
            pltpu.SemaphoreType.DMA((n, 5)),
            pltpu.SemaphoreType.DMA((n, 5)),
            pltpu.SemaphoreType.DMA,
        ],
        compiler_params=pltpu.CompilerParams(collective_id=0, has_side_effects=True, vmem_limit_bytes=40 << 20),
        name="gather",
    )(shard)
    return whole.reshape(8, 4, TILES, 16, LANES)


def scatter_kernel(parts, norm, total, norm_total, *scratch):
    n = len(ROUTES)
    bufs = [scratch[5 * r : 5 * r + 5] for r in range(n)]
    norm_in, norm_now, send, recv, norm_send, norm_recv = scratch[5 * n :]
    coords = place()
    greet(coords)
    copies = [[None] * 5 for _ in ROUTES]
    norm_copies = [None] * 5

    def source(r, stage, coordinate):
        begin, count, order = ROUTES[r]
        order = order[::-1]
        left = [d for d in range(5) if d not in order[:stage]]
        where = tuple(coordinate if d == order[stage] else slice(None) for d in left)
        if stage == 0:
            return parts, where + (pl.ds(begin, count),)
        return bufs[r][stage - 1], where

    def send_norm(stage):
        c = pltpu.make_async_remote_copy(
            src_ref=norm if stage == 0 else norm_now.at[stage - 1],
            dst_ref=norm_in.at[stage],
            send_sem=norm_send.at[stage],
            recv_sem=norm_recv.at[stage],
            device_id=partner(coords, stage),
            device_id_type=MESH,
        )
        c.start()
        norm_copies[stage] = c

    def send_part(r, stage):
        dim = ROUTES[r][2][::-1][stage]
        ref, where = source(r, stage, 1 - coords[dim])
        c = pltpu.make_async_remote_copy(
            src_ref=ref.at[where],
            dst_ref=bufs[r][stage],
            send_sem=send.at[r, stage],
            recv_sem=recv.at[r, stage],
            device_id=partner(coords, dim),
            device_id_type=MESH,
        )
        c.start()
        copies[r][stage] = c

    send_norm(0)
    for r in range(n):
        send_part(r, 0)
    for stage in range(5):
        for r in range(n):
            begin, count, order = ROUTES[r]
            dim = order[::-1][stage]
            copies[r][stage].wait_recv()
            ref, where = source(r, stage, coords[dim])
            if stage < 4:
                buf = bufs[r][stage]
                buf[...] = buf[...] + ref[where]
                send_part(r, stage + 1)
            else:
                total[begin : begin + count] = bufs[r][stage][...].astype(f32) + ref[where].astype(f32)
        norm_copies[stage].wait_recv()
        now = norm[...] if stage == 0 else norm_now[stage - 1]
        now = now + norm_in[stage]
        if stage < 4:
            norm_now[stage] = now
            send_norm(stage + 1)
        else:
            norm_total[...] = now
    for stage in range(5):
        norm_copies[stage].wait_send()
        for r in range(n):
            copies[r][stage].wait_send()


def scatter(parts, norm):
    n = len(ROUTES)
    vmem = pl.BlockSpec(memory_space=pltpu.VMEM)
    bufs = [
        pltpu.VMEM((2,) * (4 - stage) + (count, 16, LANES), bf16)
        for begin, count, order in ROUTES
        for stage in range(5)
    ]
    return pl.pallas_call(
        scatter_kernel,
        out_shape=(
            jax.ShapeDtypeStruct((TILES, 16, LANES), f32),
            jax.ShapeDtypeStruct((8, WIDE), f32),
        ),
        in_specs=[vmem] * 2,
        out_specs=[vmem] * 2,
        scratch_shapes=bufs
        + [
            pltpu.VMEM((5, 8, WIDE), f32),
            pltpu.VMEM((4, 8, WIDE), f32),
            pltpu.SemaphoreType.DMA((n, 5)),
            pltpu.SemaphoreType.DMA((n, 5)),
            pltpu.SemaphoreType.DMA((5,)),
            pltpu.SemaphoreType.DMA((5,)),
        ],
        compiler_params=pltpu.CompilerParams(collective_id=1, has_side_effects=True, vmem_limit_bytes=40 << 20),
        name="scatter",
    )(parts.reshape(2, 2, 2, 2, 2, TILES, 16, LANES), norm)


def adam_step(master, moment, square, average, grad, rate):
    moment_new = beta_one * moment + (1.0 - beta_one) * grad
    square_new = beta_two * square + (1.0 - beta_two) * grad * grad
    update = moment_new / (jnp.sqrt(square_new) + adam_eps) + decay_rate * master
    fresh = master - rate * update
    average_new = average_keep * average + (1.0 - average_keep) * fresh
    return (fresh, moment_new, square_new, average_new)


def to_groups(up, down, qkv, out):
    up, down = up.reshape(NDP, NTEN, -1), down.reshape(NDP, NTEN, -1)
    qkv = qkv.reshape(NTEN, NDP, -1).transpose(1, 0, 2)
    out = out.reshape(NTEN, NDP, -1).transpose(1, 0, 2)
    return jax.vmap(jax.vmap(shard_tiles))(up, down, qkv, out)


def from_groups(tiles):
    up, down, qkv, out = jax.vmap(jax.vmap(tiles_shard))(tiles.astype(f32))
    qkv = qkv.reshape(NDP, NTEN, -1).transpose(1, 0, 2).reshape(NTEN, -1)
    out = out.reshape(NDP, NTEN, -1).transpose(1, 0, 2).reshape(NTEN, -1)
    return up.reshape(-1), down.reshape(-1), qkv, out


def on_device(tokens, cotangent, lengths, clusters, cluster_weight, *state):
    qkv, out, up, down, norm = (state[4 * k : 4 * k + 4] for k in range(5))
    ends = ("dp", "tensor")
    low = tuple(w[0].astype(bf16) for w in (up, down, qkv, out))
    grid = (lax.axis_size("dp"), lax.axis_size("tensor")) == (NDP, NTEN)
    if grid:
        tiles = gather(shard_tiles(*low))
    else:
        whole = [lax.all_gather(w, ends, axis=0, tiled=True) for w in low[:2]]
        for w in low[2:]:
            block = lax.all_gather(w, "dp", axis=1, tiled=True)
            whole.append(lax.all_gather(block, "tensor", axis=0, tiled=True))
        tiles = to_groups(*whole)
    layer_out, tokens_grad, parts, norm_parts = run_layer(
        lengths, clusters, cluster_weight, tiles, tokens, cotangent, norm[0]
    )
    if grid:
        total, norm_total = scatter(parts, norm_parts)
        grads = tiles_shard(total)
    else:
        whole = from_groups(parts)
        grads = [lax.psum_scatter(g, ends, scatter_dimension=0, tiled=True) for g in whole[:2]]
        for g in whole[2:]:
            block = lax.psum_scatter(g, "tensor", scatter_dimension=0, tiled=True)
            grads.append(lax.psum_scatter(block, "dp", scatter_dimension=1, tiled=True))
        norm_total = lax.psum(norm_parts, ends)
    up_grad, down_grad, qkv_grad, out_grad = grads
    results = (layer_out, tokens_grad)
    results += adam_step(*qkv, qkv_grad, D ** (-0.5))
    results += adam_step(*out, out_grad, (D // 32) ** (-0.5))
    results += adam_step(*up, up_grad, D ** (-0.5))
    results += adam_step(*down, down_grad, FF ** (-0.5))
    results += adam_step(*norm, norm_total[:4, :D], 0.2)
    return results


def solution(mesh):
    rows, both, flat = P(("dp", "tensor"), None), P("tensor", "dp"), P(("dp", "tensor"))
    state = (both,) * 8 + (flat,) * 8 + (P(),) * 4
    return jax.shard_map(
        on_device,
        mesh=mesh,
        in_specs=(rows, rows, P("dp"), P("dp"), P()) + state,
        out_specs=(rows, rows) + state,
        check_vma=False,
    )
```

time: 2310 us -> 197 us (0.09)
  waiting for transfers between devices: 1820 us -> 0 us
  local copies, waits for them, and re-layouts: 221 us -> 16.9 us
  Pallas kernels: 0 us -> 171 us
  other arithmetic: 129 us -> 7.59 us
  matrix products: 73.9 us -> 0 us
  blocking collectives: 39.4 us -> 0 us
    unnamed x14 -> x0, waiting for transfers between devices: 1760 us -> none
    pallas_call x0 -> x3, Pallas kernels: none -> 171 us  [the longest x1 80.1 us: run_layer(): pl.pallas_call(layer_kernel, out_shape=(jax.ShapeDtypeStruct((rows, D), f...]
    reshape x13, local copies, waits for them, and re-layouts: 123 us -> 1.06 us  [the longest x2 0.25 us: tiles_shard(): tiles[QKV0:OUT0].reshape(3, 4, 16, LANES).transpose(1, 2, 0, 3)[:, :15]]
    all_gather x2 -> x0, other arithmetic: 81.7 us -> none  [the longest x1 40.9 us: on_device(): lax.all_gather(up_master.astype(jnp.bfloat16), ('dp', 'tensor'), axis=0,...]
    dot_general x40 -> x0, matrix products: 73.9 us -> none  [the longest x4 10.9 us: backward_one_block(): jnp.einsum('qhe,khe->hqk', grad_block, vectors, preferred_element_type=jn...]
    dynamic_update_slice x16 -> x0, local copies, waits for them, and re-layouts: 60.2 us -> none  [on_device(): lax.map(attend_forward, (query_four, key_four, value_four, lengths))]
    psum x1 -> x0, blocking collectives: 39.4 us -> none  [on_device(): lax.psum(jnp.stack([gain_one_grad, shift_one_grad, gain_two_grad, shift_t...]
    reduce_scatter x2 -> x0, waiting for transfers between devices: 36.4 us -> none  [the longest x1 36.4 us: on_device(): lax.psum_scatter(jnp.dot(sliced, joined_weight.T, preferred_element_type=...]
  transfers between devices with their start and end apart: 10 -> 0, of which waited for: 5 -> 0; matrix products, arithmetic and copies ran while one was open for 15% -> 0% of each run, Pallas kernels for 0% -> 0%
where the time goes in v1:
time: 197 us; the launch traced here: 196 us
  Pallas kernels  171 us (87%)
  local copies, waits for them, and re-layouts  16.9 us (9%)
  other arithmetic  7.59 us (4%)
    pallas_call x1, Pallas kernels, run_layer(): pl.pallas_call(layer_kernel, out_shape=(jax.ShapeDtypeStruct((rows, D), f...  80.1 us
    pallas_call x1, Pallas kernels, scatter(): pl.pallas_call(scatter_kernel, out_shape=(jax.ShapeDtypeStruct((TILES, 16...  45.7 us
    pallas_call x1, Pallas kernels, gather(): pl.pallas_call(gather_kernel, out_shape=jax.ShapeDtypeStruct((2, 2, 2, 2,...  44.9 us
    unnamed x58, local copies, waits for them, and re-layouts  14.3 us

profile of v1, /device:TPU:0, one launch (start us, length us, event | category | flops | bytes accessed | tf_op | source)
XLA Modules:
  0.0 196.3 jit_solution(12646171552862790370)
XLA Ops:
  0.7 1.3 pad.24.norm
  2.0 0.8 convert_reduce_fusion.1
  2.8 0.1 reshape.167
  2.9 1.1 convert_reduce_fusion
  4.0 0.1 reshape.164
  4.2 0.9 convert_element_type.22
  5.2 0.9 convert_element_type.23
  6.1 0.1 reshape.161
  6.4 2.0 %copy.61.tok = bf16[512,480]{1,0:T(8,128)(2,1)} copy(bf16[512,480]{0,1:T(8,128)(2,1)} %param.31) | data formatting | bytes 983040 | tf_op args[0]
  8.4 2.0 %copy.62.cot = bf16[512,480]{1,0:T(8,128)(2,1)} copy(bf16[512,480]{0,1:T(8,128)(2,1)} %param.32) | data formatting | bytes 983040 | tf_op args[1]
  10.5 44.9 %gather.1 = bf16[2,2,2,2,2,47,16,128]{7,6,5,4,3,2,1,0:T(8,128)(2,1)S(1)} custom-call(bf16[47,16,128]{2,1,0:T(8,128)(2,1)S(1)} %pad_maximum_fusion.shard), custom_call_target="tpu_custom_call" | custom-call | tf_op jit(solution)/shard_map/gather/pallas_call | solution.py:414
  55.4 0.0 copy-start
  55.4 2.6 %copy-done = bf16[2,2,2,2,2,47,16,128]{7,6,5,4,3,2,1,0:T(8,128)(2,1)} copy-done((bf16[2,2,2,2,2,47,16,128]{7,6,5,4,3,2,1,0:T(8,128)(2,1)}, bf16[2,2,2,2,2,47,16,128]{7,6,5,4,3,2,1,0:T(8,128)(2,1)S(1)}, u32[]{:S(2)}) %copy-start) | copy-done | bytes 6160408
  58.0 80.1 %layer.1 = (f32[512,480]{1,0:T(8,128)}, f32[512,480]{1,0:T(8,128)}, bf16[8,4,47,16,128]{4,3,2,1,0:T(8,128)(2,1)}, f32[8,512]{1,0:T(8,128)}) custom-call(s32[4]{0:T(128)} %lengths.1, s32[4]{0:T(128)} %clusters.1, f32[64]{0:T(128)} %weights_of.1, bf16[8,4,47,16,128]{4,3,2,1,0:T(8,128)(2,1)} %bitcast.42, bf16[512,480]{1,0:T(8,128)(2,1)} %copy.61.tok, ...), custom_call_target="tpu_custom_call" | custom-call | tf_op jit(solution)/shard_map/layer/pallas_call | solution.py:292
  138.1 0.0 copy-start.21
  138.1 0.0 copy-start.22
  138.1 0.0 copy-start.23
  138.1 0.0 copy-start.13
  138.1 0.0 copy-start.18
  138.1 0.0 copy-start.19
  138.1 0.0 copy-start.20
  138.1 0.0 copy-start.6
  138.1 0.0 copy-start.14
  138.2 0.0 copy-start.15
  138.2 0.0 copy-start.16
  138.2 0.0 copy-start.4
  138.2 0.0 copy-start.5
  138.2 0.0 copy-start.7
  138.2 0.0 copy-start.8
  138.2 0.0 copy-start.9
  138.2 0.0 copy-start.10
  138.3 0.0 copy-start.11
  138.3 0.0 copy-start.12
  138.3 2.7 %copy.67 = f32[512,480]{0,1:T(8,128)} copy(f32[512,480]{1,0:T(8,128)} %get-tuple-element.56) | data formatting | bytes 1966080
  141.0 2.7 %copy-done.1 = bf16[8,4,47,16,128]{4,3,2,1,0:T(8,128)(2,1)S(1)} copy-done((bf16[8,4,47,16,128]{4,3,2,1,0:T(8,128)(2,1)S(1)}, bf16[8,4,47,16,128]{4,3,2,1,0:T(8,128)(2,1)}, u32[]{:S(2)}) %copy-start.1) | copy-done | bytes 6160408
  143.7 0.7 copy-done.2
  144.4 45.7 %scatter.1 = (f32[47,16,128]{2,1,0:T(8,128)S(1)}, f32[8,512]{1,0:T(8,128)S(1)}) custom-call(bf16[2,2,2,2,2,47,16,128]{7,6,5,4,3,2,1,0:T(8,128)(2,1)S(1)} %bitcast.43, f32[8,512]{1,0:T(8,128)S(1)} %copy-done.2), custom_call_target="tpu_custom_call" | custom-call | tf_op jit(solution)/shard_map/scatter/pallas_call | solution.py:511
  190.1 0.0 copy-done.17
  190.1 0.0 copy-done.21
  190.1 0.0 copy-done.22
  190.1 0.0 copy-done.23
  190.1 0.6 multiply_add_fusion.9
  190.8 0.1 reshape.175
  190.9 0.0 copy-done.13
  190.9 0.0 copy-done.18
  191.0 0.0 copy-done.19
  191.0 0.0 copy-done.20
  191.0 0.8 multiply_add_fusion.7
  191.8 0.1 copy.77
  192.0 0.2 reshape.173
  192.2 0.1 copy.76
  192.4 0.1 reshape.179
  192.6 0.0 copy-done.6
  192.6 0.0 copy-done.14
  192.6 0.0 copy-done.15
  192.6 0.0 copy-done.16
  192.6 1.3 multiply_add_fusion.5
  194.0 0.0 copy-done.4
  194.0 0.0 copy-done.5
  194.0 0.0 copy-done.7
  194.0 0.0 copy-done.8
  194.0 1.0 multiply_add_fusion.2
  195.0 0.0 copy-done.3
  195.0 1.3 copy.68
  (34 shorter events, 0.4 us)
Async XLA Ops:
  55.4 2.6 %copy-start = (bf16[2,2,2,2,2,47,16,128]{7,6,5,4,3,2,1,0:T(8,128)(2,1)}, bf16[2,2,2,2,2,47,16,128]{7,6,5,4,3,2,1,0:T(8,128)(2,1)S(1)}, u32[]{:S(2)}) copy-start(bf16[2,2,2,2,2,47,16,128]{7,6,5,4,3,2,1,0:T(8,128)(2,1)S(1)} %gather.1) | copy-start | bytes 18481156
  138.0 52.1 %copy-start.17 = (f32[4,480]{1,0:T(4,128)S(1)}, f32[4,480]{1,0:T(4,128)}, u32[]{:S(2)}) copy-start(f32[4,480]{1,0:T(4,128)} %param.52) | copy-start | bytes 23044
  138.1 52.1 %copy-start.21 = (f32[4,480]{1,0:T(4,128)S(1)}, f32[4,480]{1,0:T(4,128)}, u32[]{:S(2)}) copy-start(f32[4,480]{1,0:T(4,128)} %param.55) | copy-start | bytes 23044
  138.1 52.1 %copy-start.22 = (f32[4,480]{1,0:T(4,128)S(1)}, f32[4,480]{1,0:T(4,128)}, u32[]{:S(2)}) copy-start(f32[4,480]{1,0:T(4,128)} %param.54) | copy-start | bytes 23044
  138.1 52.1 %copy-start.23 = (f32[4,480]{1,0:T(4,128)S(1)}, f32[4,480]{1,0:T(4,128)}, u32[]{:S(2)}) copy-start(f32[4,480]{1,0:T(4,128)} %param.53) | copy-start | bytes 23044
  138.1 52.9 %copy-start.13 = (f32[1,7200]{1,0:T(1,128)S(1)}, f32[1,7200]{1,0:T(1,128)}, u32[]{:S(2)}) copy-start(f32[1,7200]{1,0:T(1,128)} %param.40) | copy-start | bytes 86404
  138.1 52.8 %copy-start.18 = (f32[1,7200]{1,0:T(1,128)S(1)}, f32[1,7200]{1,0:T(1,128)}, u32[]{:S(2)}) copy-start(f32[1,7200]{1,0:T(1,128)} %param.43) | copy-start | bytes 86404
  138.1 52.8 %copy-start.19 = (f32[1,7200]{1,0:T(1,128)S(1)}, f32[1,7200]{1,0:T(1,128)}, u32[]{:S(2)}) copy-start(f32[1,7200]{1,0:T(1,128)} %param.42) | copy-start | bytes 86404
  138.1 52.8 %copy-start.20 = (f32[1,7200]{1,0:T(1,128)S(1)}, f32[1,7200]{1,0:T(1,128)}, u32[]{:S(2)}) copy-start(f32[1,7200]{1,0:T(1,128)} %param.41) | copy-start | bytes 86404
  138.1 54.4 %copy-start.6 = (f32[1,21600]{1,0:T(1,128)S(1)}, f32[1,21600]{1,0:T(1,128)}, u32[]{:S(2)}) copy-start(f32[1,21600]{1,0:T(1,128)} %param.36) | copy-start | bytes 259204
  138.1 54.4 %copy-start.14 = (f32[1,21600]{1,0:T(1,128)S(1)}, f32[1,21600]{1,0:T(1,128)}, u32[]{:S(2)}) copy-start(f32[1,21600]{1,0:T(1,128)} %param.39) | copy-start | bytes 259204
  138.2 54.4 %copy-start.15 = (f32[1,21600]{1,0:T(1,128)S(1)}, f32[1,21600]{1,0:T(1,128)}, u32[]{:S(2)}) copy-start(f32[1,21600]{1,0:T(1,128)} %param.38) | copy-start | bytes 259204
  138.2 54.4 %copy-start.16 = (f32[1,21600]{1,0:T(1,128)S(1)}, f32[1,21600]{1,0:T(1,128)}, u32[]{:S(2)}) copy-start(f32[1,21600]{1,0:T(1,128)} %param.37) | copy-start | bytes 259204
  138.2 55.8 %copy-start.4 = (f32[28800]{0:T(1024)S(1)}, f32[28800]{0:T(1024)}, u32[]{:S(2)}) copy-start(f32[28800]{0:T(1024)} %param.48) | copy-start | bytes 345604
  138.2 55.8 %copy-start.5 = (f32[28800]{0:T(1024)S(1)}, f32[28800]{0:T(1024)}, u32[]{:S(2)}) copy-start(f32[28800]{0:T(1024)} %param.44) | copy-start | bytes 345604
  138.2 55.7 %copy-start.7 = (f32[28800]{0:T(1024)S(1)}, f32[28800]{0:T(1024)}, u32[]{:S(2)}) copy-start(f32[28800]{0:T(1024)} %param.51) | copy-start | bytes 345604
  138.2 55.7 %copy-start.8 = (f32[28800]{0:T(1024)S(1)}, f32[28800]{0:T(1024)}, u32[]{:S(2)}) copy-start(f32[28800]{0:T(1024)} %param.50) | copy-start | bytes 345604
  138.2 55.7 %copy-start.9 = (f32[28800]{0:T(1024)S(1)}, f32[28800]{0:T(1024)}, u32[]{:S(2)}) copy-start(f32[28800]{0:T(1024)} %param.49) | copy-start | bytes 345604
  138.2 55.7 %copy-start.10 = (f32[28800]{0:T(1024)S(1)}, f32[28800]{0:T(1024)}, u32[]{:S(2)}) copy-start(f32[28800]{0:T(1024)} %param.46) | copy-start | bytes 345604
  138.3 55.7 %copy-start.11 = (f32[28800]{0:T(1024)S(1)}, f32[28800]{0:T(1024)}, u32[]{:S(2)}) copy-start(f32[28800]{0:T(1024)} %param.45) | copy-start | bytes 345604
  138.3 55.7 %copy-start.12 = (f32[28800]{0:T(1024)S(1)}, f32[28800]{0:T(1024)}, u32[]{:S(2)}) copy-start(f32[28800]{0:T(1024)} %param.47) | copy-start | bytes 345604
  141.0 2.7 %copy-start.1 = (bf16[8,4,47,16,128]{4,3,2,1,0:T(8,128)(2,1)S(1)}, bf16[8,4,47,16,128]{4,3,2,1,0:T(8,128)(2,1)}, u32[]{:S(2)}) copy-start(bf16[8,4,47,16,128]{4,3,2,1,0:T(8,128)(2,1)} %get-tuple-element.30) | copy-start | bytes 18481156
  143.7 0.7 copy-start.2
  144.4 50.6 %copy-start.3 = (f32[512,480]{1,0:T(8,128)S(1)}, f32[512,480]{1,0:T(8,128)}, u32[]{:S(2)}) copy-start(f32[512,480]{1,0:T(8,128)} %get-tuple-element.57) | copy-start | bytes 2949124

commit v2 on v1

v2 whole, which is shorter than its diff:
```python
import functools

import jax
import jax.numpy as jnp
import numpy as np
from jax import lax
from jax.experimental import pallas as pl
from jax.experimental.pallas import tpu as pltpu
from jax.sharding import PartitionSpec as P

D = 480
HEAD = 24
FF = 1920
MAXLEN = 512
NDP, NTEN = 8, 4
WIDE = 512
HEADS_DEV = 5
LANES = 128
TILES = 47
UP0, DOWN0, OUT0, QKV0 = 0, 15, 31, 35
CHUNK = 384
QB = 256

norm_eps = 1e-05
beta_one = 0.5
beta_two = 0.5
adam_eps = 1e-08
decay_rate = 0.01
average_keep = 0.75
masked_score = -1e30
MESH = pl.DeviceIdType.MESH
f32, bf16 = jnp.float32, jnp.bfloat16


def mm(a, b):
    return lax.dot_general(a, b, (((1,), (0,)), ((), ())), preferred_element_type=f32)


def mm_nt(a, b):
    return lax.dot_general(a, b, (((1,), (1,)), ((), ())), preferred_element_type=f32)


def constants():
    natural = np.arange(D)
    squeeze = np.zeros((WIDE, WIDE), np.float32)
    squeeze[natural, 16 * (natural // 15) + natural % 15] = 1.0
    spread = np.zeros((CHUNK, CHUNK), np.float32)
    for third in range(3):
        lane = np.arange(120)
        spread[third * 120 + lane, third * 128 + lane] = 1.0
    position = np.arange(MAXLEN, dtype=np.float32)
    exponent = np.arange(HEAD // 2, dtype=np.float32) * np.float32(2.0 / HEAD)
    inverse = np.float32(10000.0) ** (-exponent)
    angle = (position[:, None] * inverse[None, :]).astype(np.float32).astype(np.float64)
    lane = np.arange(120)
    place = lane % HEAD
    cosine = np.zeros((MAXLEN, LANES), np.float32)
    first = np.zeros((MAXLEN, LANES), np.float32)
    second = np.zeros((MAXLEN, LANES), np.float32)
    cosine[:, :120] = np.cos(angle)[:, place % 12]
    sines = np.sin(angle)[:, place % 12]
    first[:, :120] = np.where(place < 12, -sines, 0.0)
    second[:, :120] = np.where(place >= 12, sines, 0.0)
    low = lambda v: jnp.asarray(v.astype(jnp.bfloat16))
    return (low(squeeze), low(squeeze.T), low(spread), jnp.asarray(cosine), jnp.asarray(first), jnp.asarray(second))


LATE, EARLY = (0, 1, 2), (3, 4, 5)
ROUTES = (
    (0, 14, (0, 1, 3, 2, 4)),
    (14, 14, (0, 1, 2, 3, 4)),
    (28, 7, (2, 3, 0, 1, 4)),
    (35, 5, (0, 1, 3, 2, 4)),
    (40, 5, (0, 1, 2, 3, 4)),
    (45, 2, (2, 3, 0, 1, 4)),
)
GATHER_AT = (3, 14)
SCATTER_AT = (3, 12, 16, 19)


class Links:
    @staticmethod
    def scratch():
        n, tiles = len(ROUTES), (TILES, 16, LANES)
        bufs = [
            pltpu.VMEM((2,) * (4 - stage) + (count, 16, LANES), bf16)
            for begin, count, order in ROUTES
            for stage in range(5)
        ]
        return bufs + [
            pltpu.VMEM((2,) * 5 + tiles, bf16),
            pltpu.VMEM((2,) * 5 + tiles, bf16),
            pltpu.VMEM((5, 8, WIDE), f32),
            pltpu.VMEM((5, 8, WIDE), f32),
            pltpu.SemaphoreType.DMA,
            pltpu.SemaphoreType.DMA((n, 5)),
            pltpu.SemaphoreType.DMA((n, 5)),
            pltpu.SemaphoreType.DMA((n, 5)),
            pltpu.SemaphoreType.DMA((n, 5)),
            pltpu.SemaphoreType.DMA((5,)),
            pltpu.SemaphoreType.DMA((5,)),
        ]

    def __init__(self, shard, total, norm_total, *scratch):
        n = len(ROUTES)
        self.shard, self.total, self.norm_total = shard, total, norm_total
        self.bufs = [scratch[5 * r : 5 * r + 5] for r in range(n)]
        (
            self.whole, self.parts, self.norm_now, self.norm_in, self.own_sem,
            self.g_send, self.g_recv, self.s_send, self.s_recv, self.n_send, self.n_recv,
        ) = scratch[5 * n :]
        dp, tensor = lax.axis_index("dp"), lax.axis_index("tensor")
        self.coords = (dp // 4, (dp // 2) % 2, dp % 2, tensor // 2, tensor % 2)

    def partner(self, dim):
        c = list(self.coords)
        c[dim] = 1 - c[dim]
        return (c[0] * 4 + c[1] * 2 + c[2], c[3] * 2 + c[4])

    def greet(self):
        barrier = pltpu.get_barrier_semaphore()
        for dim in range(5):
            pl.semaphore_signal(barrier, inc=1, device_id=self.partner(dim), device_id_type=MESH)
        pl.semaphore_wait(barrier, 5)

    def keep_own(self):
        copy = pltpu.make_async_copy(self.shard, self.whole.at[self.coords], self.own_sem)
        copy.start()
        copy.wait()

    def gather_copy(self, r, stage):
        begin, count, order = ROUTES[r]
        done, dim = order[:stage], order[stage]
        where = tuple(slice(None) if d in done else self.coords[d] for d in range(5)) + (pl.ds(begin, count),)
        return pltpu.make_async_remote_copy(
            src_ref=self.whole.at[where],
            dst_ref=self.whole.at[where],
            send_sem=self.g_send.at[r, stage],
            recv_sem=self.g_recv.at[r, stage],
            device_id=self.partner(dim),
            device_id_type=MESH,
        )

    def gather_step(self, group, stage):
        for r in group:
            if stage > 0:
                self.gather_copy(r, stage - 1).wait_recv()
            if stage < 5:
                self.gather_copy(r, stage).start()

    def sums(self, r, stage, coordinate):
        begin, count, order = ROUTES[r]
        order = order[::-1]
        left = [d for d in range(5) if d not in order[:stage]]
        where = tuple(coordinate if d == order[stage] else slice(None) for d in left)
        if stage == 0:
            return self.parts.at[where + (pl.ds(begin, count),)]
        return self.bufs[r][stage - 1].at[where]

    def scatter_copy(self, r, stage):
        dim = ROUTES[r][2][4 - stage]
        return pltpu.make_async_remote_copy(
            src_ref=self.sums(r, stage, 1 - self.coords[dim]),
            dst_ref=self.bufs[r][stage],
            send_sem=self.s_send.at[r, stage],
            recv_sem=self.s_recv.at[r, stage],
            device_id=self.partner(dim),
            device_id_type=MESH,
        )

    def scatter_step(self, group, stage):
        for r in group:
            begin, count, order = ROUTES[r]
            if stage > 0:
                self.scatter_copy(r, stage - 1).wait_recv()
                buf = self.bufs[r][stage - 1]
                mine = self.sums(r, stage - 1, self.coords[order[5 - stage]])[...]
                if stage < 5:
                    buf[...] = buf[...] + mine
                else:
                    self.total[begin : begin + count] = buf[...].astype(f32) + mine.astype(f32)
            if stage < 5:
                self.scatter_copy(r, stage).start()

    def norm_copy(self, stage):
        return pltpu.make_async_remote_copy(
            src_ref=self.norm_now.at[stage],
            dst_ref=self.norm_in.at[stage],
            send_sem=self.n_send.at[stage],
            recv_sem=self.n_recv.at[stage],
            device_id=self.partner(stage),
            device_id_type=MESH,
        )

    def norm_start(self, values):
        self.norm_now[0] = values
        self.norm_copy(0).start()

    def norm_step(self, stage):
        self.norm_copy(stage).wait_recv()
        now = self.norm_now[stage] + self.norm_in[stage]
        if stage < 4:
            self.norm_now[stage + 1] = now
            self.norm_copy(stage + 1).start()
        else:
            self.norm_total[...] = now

    def finish(self):
        for stage in range(5):
            for r in range(len(ROUTES)):
                self.gather_copy(r, stage).wait_send()
                self.scatter_copy(r, stage).wait_send()
            self.norm_copy(stage).wait_send()


def gelu_parts(u):
    half = 0.5 * (1.0 + lax.erf(u * 0.7071067811865476))
    return u * half, half + u * jnp.exp(-0.5 * u * u) * 0.3989422804014327


def layer_kernel(remote, *refs):
    lengths, clusters, weights_of, source, tok, cot, norm, squeeze, widen, spread, cosine, first, second = refs[:13]
    layer_out, tokens_grad, G_out, norm_out = refs[13:17]
    (
        up_s, down_s, qkv_s, out_s, q_s, k_s, v_s, kT_s, vT_s, P_s, OT_s, att_s, dA_s, dqT_s, dk_s, dv_s,
        act1_s, act2_s, act_pad, plain1, plain2, res_s, y_s, dn_s, dres_s, dlow_s, eye_s, gdown_s, x_s,
    ) = refs[17:46]
    if remote:
        links = Links(source, G_out, norm_out, *refs[46:])
        W, G = links.whole, links.parts
        links.greet()
        links.keep_own()
        links.gather_step(EARLY, 0)
    else:
        links, W, G = None, source, G_out
    me = lax.axis_index("tensor")
    length = lengths[me]
    scale_row = weights_of[clusters[me]]
    scale = HEAD ** -0.5

    lane = lax.broadcasted_iota(jnp.int32, (1, WIDE), 1)
    real = jnp.where(lane < D, 1.0, 0.0)
    gains = norm[...]

    def norm_rows(values, gain, shift):
        middle = jnp.sum(values, axis=-1, keepdims=True) * (1.0 / D)
        centered = (values - middle) * real
        spread_ = jnp.sum(centered * centered, axis=-1, keepdims=True) * (1.0 / D)
        inverse = lax.rsqrt(spread_ + norm_eps)
        plain = centered * inverse
        return plain * gain + shift, plain, inverse

    def norm_back(dz, plain, inverse, gain):
        dg = jnp.sum(dz * plain, axis=0, keepdims=True)
        db = jnp.sum(dz, axis=0, keepdims=True)
        scaled = dz * gain
        one = jnp.sum(scaled, axis=-1, keepdims=True) * (1.0 / D)
        two = jnp.sum(scaled * plain, axis=-1, keepdims=True) * (1.0 / D)
        return inverse * (scaled - one - plain * two) * real, dg, db

    x_s[...] = jnp.zeros_like(x_s)
    x_s[:D, :] = tok[...].astype(f32)
    dres_s[...] = jnp.zeros_like(dres_s)
    dres_s[:D, :] = cot[...].astype(f32)
    x_s[...] = x_s[...].T
    normed, plain, inverse1 = norm_rows(x_s[...], gains[0:1], gains[1:2])
    plain1[...] = plain
    act1_s[...] = normed.astype(bf16)
    if remote:
        links.gather_step(EARLY, 1)
    row = lax.broadcasted_iota(jnp.int32, (MAXLEN, 1), 0)
    row_scale = jnp.where(row < length, scale_row, 0.0)
    dres_s[...] = dres_s[...].T * row_scale
    dlow_s[...] = dres_s[...].astype(bf16)
    if remote:
        links.gather_step(EARLY, 2)
        links.gather_step(LATE, 0)
        links.gather_step(EARLY, 3)
        links.gather_step(EARLY, 4)
        links.gather_step(LATE, 1)
        links.gather_step(EARLY, 5)
        links.gather_step(LATE, 2)

    for t in range(NTEN):
        mine = (slice(None),) * 3 + (t // 2, t % 2)
        pieces = [W[mine + (slice(QKV0 + 4 * c, QKV0 + 4 * c + 4),)].reshape(WIDE, LANES) for c in range(3)]
        plain = mm(squeeze[...], jnp.concatenate(pieces, 1)).astype(bf16)
        qkv_s[t] = mm(plain, spread[...]).astype(bf16)
    cosv, firstv, secondv = cosine[...], first[...], second[...]
    for t in range(NTEN):
        joined = mm(act1_s[...], qkv_s[t])
        for number in range(2):
            u = joined[:, number * LANES : (number + 1) * LANES]
            r = u * cosv + pltpu.roll(u, LANES - 12, 1) * firstv + pltpu.roll(u, 12, 1) * secondv
            if number == 0:
                q_s[t] = r.astype(bf16)
            else:
                k_s[t] = r.astype(bf16)
                kT_s[t] = r.T.astype(bf16)
        v = joined[:, 2 * LANES :]
        v_s[t] = v.astype(bf16)
        vT_s[t] = v.T.astype(bf16)

    lane_id = lax.broadcasted_iota(jnp.int32, (1, LANES), 1)
    row_id = lax.broadcasted_iota(jnp.int32, (LANES, 1), 0)
    key_id = lax.broadcasted_iota(jnp.int32, (MAXLEN, 1), 0)
    usable = key_id < length

    OT_s[...] = jnp.zeros_like(OT_s)

    def forward_head(h, carry):
        t = h // HEADS_DEV
        begin = (h - t * HEADS_DEV) * HEAD
        lanes = jnp.where((lane_id >= begin) & (lane_id < begin + HEAD), 1.0, 0.0).astype(bf16)
        rows = jnp.where((row_id >= begin) & (row_id < begin + HEAD), 1.0, 0.0).astype(bf16)
        keys = k_s[t] * lanes
        values = vT_s[t] * rows
        for b in range(MAXLEN // QB):
            cols = slice(b * QB, (b + 1) * QB)
            s = mm_nt(keys, q_s[t, cols, :])
            s = jnp.where(usable, s * scale, masked_score)
            top = jnp.max(s, axis=0, keepdims=True)
            e = jnp.exp(s - top)
            total = jnp.sum(e, axis=0, keepdims=True)
            p = (e * (1.0 / total)).astype(bf16)
            P_s[h, :, cols] = p
            OT_s[t, :, cols] += mm(values, p)
        if remote:
            for number, when in enumerate(GATHER_AT):
                pl.when(h == when)(functools.partial(links.gather_step, LATE, 3 + number))
        return carry

    lax.fori_loop(0, NTEN * HEADS_DEV, forward_head, 0)

    if remote:
        links.gather_step(LATE, 5)
    res = x_s[...]
    for t in range(NTEN):
        mine = (slice(None),) * 3 + (t // 2, t % 2)
        pieces = [W[mine + (OUT0 + c,)].reshape(LANES, LANES) for c in range(4)]
        out_s[t] = mm(squeeze[:LANES, :LANES], jnp.concatenate(pieces, 1)).astype(bf16)
        att_s[t] = OT_s[t].T.astype(bf16)
        res = res + mm(att_s[t], out_s[t])
    res_s[...] = res
    normed, plain, inverse2 = norm_rows(res, gains[2:3], gains[3:4])
    plain2[...] = plain
    act2_s[...] = normed.astype(bf16)
    act_pad[...] = mm_nt(widen[...], act2_s[...]).astype(bf16)

    for c in range(15):
        part = mm(squeeze[...], W[:, :, :, :, :, UP0 + c].reshape(WIDE, LANES)).astype(bf16)
        up_s[:, c * LANES : (c + 1) * LANES] = part

    def down_rows(k, carry):
        mine = (k // 4, (k // 2) % 2, k % 2)
        pieces = [W[mine + (slice(None),) * 2 + (slice(DOWN0 + 4 * c, DOWN0 + 4 * c + 4),)].reshape(256, LANES) for c in range(4)]
        part = mm(squeeze[:240, :256], jnp.concatenate(pieces, 1)).astype(bf16)
        down_s[pl.ds(pl.multiple_of(k * 240, 16), 240), :] = part
        return carry

    lax.fori_loop(0, NDP, down_rows, 0)

    y_s[...] = res_s[...]
    dn_s[...] = jnp.zeros_like(dn_s)
    eye_row = lax.broadcasted_iota(jnp.int32, (CHUNK, CHUNK), 0)
    eye_col = lax.broadcasted_iota(jnp.int32, (CHUNK, CHUNK), 1)
    eye = jnp.where(eye_row == eye_col, 1.0, 0.0).astype(bf16)
    eye_s[...] = eye

    def hidden_chunk(c, carry):
        cols = pl.ds(pl.multiple_of(c * CHUNK, LANES), CHUNK)
        u = mm(act2_s[...], up_s[:, cols])
        value, slope = gelu_parts(u)
        a = value.astype(bf16)
        y_s[...] += mm(a, down_s[cols, :])
        d_active = mm_nt(dlow_s[...], down_s[cols, :])
        d_upper = (d_active * slope).astype(bf16)
        dn_s[...] += mm_nt(d_upper, up_s[:, cols])
        g_up = mm(act_pad[...], d_upper).astype(bf16)
        for part in range(3):
            G[:, :, :, :, :, UP0 + 3 * c + part] = g_up[:, part * LANES : (part + 1) * LANES].reshape(2, 2, 2, 2, 2, 16, LANES)
        aT = mm_nt(eye_s[...], a).astype(bf16)
        gdown_s[cols, :] = mm(aT, dlow_s[...]).astype(bf16)
        return carry

    lax.fori_loop(0, FF // CHUNK, hidden_chunk, 0)
    y_s[...] = y_s[...].T
    layer_out[...] = y_s[:D, :]

    def down_groups(k, carry):
        part = mm(widen[:256, :240], gdown_s[pl.ds(pl.multiple_of(k * 240, 16), 240), :]).astype(bf16)
        mine = (k // 4, (k // 2) % 2, k % 2)
        for c in range(4):
            where = mine + (slice(None),) * 2 + (slice(DOWN0 + 4 * c, DOWN0 + 4 * c + 4),)
            G[where] = part[:, c * LANES : (c + 1) * LANES].reshape(2, 2, 4, 16, LANES)
        return carry

    lax.fori_loop(0, 8, down_groups, 0)

    d_from, dg2, db2 = norm_back(dn_s[...], plain2[...], inverse2, gains[2:3])
    d_res = dres_s[...] + d_from
    dres_s[...] = d_res
    dlow_s[...] = d_res.astype(bf16)

    for t in range(NTEN):
        dA_s[t] = mm_nt(dlow_s[...], out_s[t]).astype(bf16)
        attT = mm_nt(widen[:LANES, :LANES], att_s[t]).astype(bf16)
        part = mm(attT, dlow_s[...]).astype(bf16)
        mine = (slice(None),) * 3 + (t // 2, t % 2)
        for c in range(4):
            G[mine + (OUT0 + c,)] = part[:, c * LANES : (c + 1) * LANES].reshape(2, 2, 2, 16, LANES)
    if remote:
        links.scatter_step(LATE, 0)

    dqT_s[...] = jnp.zeros_like(dqT_s)
    dk_s[...] = jnp.zeros_like(dk_s)
    dv_s[...] = jnp.zeros_like(dv_s)

    def backward_head(h, carry):
        t = h // HEADS_DEV
        begin = (h - t * HEADS_DEV) * HEAD
        lanes = jnp.where((lane_id >= begin) & (lane_id < begin + HEAD), 1.0, 0.0).astype(bf16)
        rows = jnp.where((row_id >= begin) & (row_id < begin + HEAD), 1.0, 0.0).astype(bf16)
        values = v_s[t]
        keysT = kT_s[t] * rows
        for b in range(MAXLEN // QB):
            cols = slice(b * QB, (b + 1) * QB)
            dA = dA_s[t, cols, :] * lanes
            dP = mm_nt(values, dA)
            low = P_s[h, :, cols]
            p = low.astype(f32)
            centre = jnp.sum(p * dP, axis=0, keepdims=True)
            ds = (p * (dP - centre)).astype(bf16)
            dv_s[t] += mm(low, dA)
            dk_s[t] += mm(ds, q_s[t, cols, :] * lanes)
            dqT_s[t, :, cols] += mm(keysT, ds)
        if remote:
            for number, when in enumerate(SCATTER_AT):
                pl.when(h == when)(functools.partial(links.scatter_step, LATE, 1 + number))
        return carry

    lax.fori_loop(0, NTEN * HEADS_DEV, backward_head, 0)

    act_pad[...] = mm_nt(widen[...], act1_s[...]).astype(bf16)
    for t in range(NTEN):
        pieces = []
        for number in range(2):
            g = (dqT_s[t].T if number == 0 else dk_s[t]) * scale
            r = g * cosv - pltpu.roll(g, LANES - 12, 1) * firstv - pltpu.roll(g, 12, 1) * secondv
            pieces.append(r.astype(bf16))
        pieces.append(dv_s[t].astype(bf16))
        d_joined = jnp.concatenate(pieces, 1)
        q_s[t], k_s[t], v_s[t] = pieces
        natural = mm_nt(d_joined, spread[...]).astype(bf16)
        part = mm(act_pad[...], natural).astype(bf16)
        mine = (slice(None),) * 3 + (t // 2, t % 2)
        for c in range(3):
            where = mine + (slice(QKV0 + 4 * c, QKV0 + 4 * c + 4),)
            G[where] = part[:, c * LANES : (c + 1) * LANES].reshape(2, 2, 2, 4, 16, LANES)
    if remote:
        links.scatter_step(EARLY, 0)
        links.scatter_step(LATE, 5)
    dz = jnp.zeros((MAXLEN, WIDE), f32)
    for t in range(NTEN):
        for number, ref in enumerate((q_s, k_s, v_s)):
            dz = dz + mm_nt(ref[t], qkv_s[t, :, number * LANES : (number + 1) * LANES])
    d_from, dg1, db1 = norm_back(dz, plain1[...], inverse1, gains[0:1])
    norm_parts = jnp.concatenate([dg1, db1, dg2, db2, jnp.zeros((4, WIDE), f32)], 0)
    if remote:
        links.norm_start(norm_parts)
        links.scatter_step(EARLY, 1)
    else:
        norm_out[...] = norm_parts
    x_s[...] = (dres_s[...] + d_from).T
    tokens_grad[...] = x_s[:D, :]
    if remote:
        for stage in range(5):
            if stage > 0:
                links.scatter_step(EARLY, stage + 1)
            links.norm_step(stage)
        links.finish()


def run_layer(lengths, clusters, cluster_weight, source, tokens, cotangent, norm_master, remote):
    rows = MAXLEN
    wide_norm = jnp.pad(norm_master, ((0, 0), (0, WIDE - D)))
    smem = pl.BlockSpec(memory_space=pltpu.SMEM)
    vmem = pl.BlockSpec(memory_space=pltpu.VMEM)
    head_set = (NTEN, MAXLEN, LANES)
    turned = (NTEN, LANES, MAXLEN)
    wide = (rows, WIDE)
    scratch = [
        pltpu.VMEM((WIDE, FF), bf16),
        pltpu.VMEM((FF, WIDE), bf16),
        pltpu.VMEM((NTEN, WIDE, CHUNK), bf16),
        pltpu.VMEM((NTEN, LANES, WIDE), bf16),
        pltpu.VMEM(head_set, bf16),
        pltpu.VMEM(head_set, bf16),
        pltpu.VMEM(head_set, bf16),
        pltpu.VMEM(turned, bf16),
        pltpu.VMEM(turned, bf16),
        pltpu.VMEM((NTEN * HEADS_DEV, MAXLEN, MAXLEN), bf16),
        pltpu.VMEM(turned, f32),
        pltpu.VMEM(head_set, bf16),
        pltpu.VMEM(head_set, bf16),
        pltpu.VMEM(turned, f32),
        pltpu.VMEM(head_set, f32),
        pltpu.VMEM(head_set, f32),
        pltpu.VMEM(wide, bf16),
        pltpu.VMEM(wide, bf16),
        pltpu.VMEM(wide, bf16),
        pltpu.VMEM(wide, f32),
        pltpu.VMEM(wide, f32),
        pltpu.VMEM(wide, f32),
        pltpu.VMEM(wide, f32),
        pltpu.VMEM(wide, f32),
        pltpu.VMEM(wide, f32),
        pltpu.VMEM(wide, bf16),
        pltpu.VMEM((CHUNK, CHUNK), bf16),
        pltpu.VMEM((FF, WIDE), bf16),
        pltpu.VMEM(wide, f32),
    ]
    tiles = (TILES, 16, LANES)
    params = dict(vmem_limit_bytes=66_900_000)
    if remote:
        result = jax.ShapeDtypeStruct(tiles, f32)
        scratch += Links.scratch()
        params.update(collective_id=0, has_side_effects=True)
    else:
        result = jax.ShapeDtypeStruct((2,) * 5 + tiles, bf16)
        source = source.reshape((2,) * 5 + tiles)
    turned_out, turned_grad, grads, norm_grad = pl.pallas_call(
        functools.partial(layer_kernel, remote),
        out_shape=(
            jax.ShapeDtypeStruct((D, rows), f32),
            jax.ShapeDtypeStruct((D, rows), f32),
            result,
            jax.ShapeDtypeStruct((8, WIDE), f32),
        ),
        in_specs=[smem] * 3 + [vmem] * 10,
        out_specs=[vmem] * 4,
        scratch_shapes=scratch,
        compiler_params=pltpu.CompilerParams(**params),
        name="layer",
    )(lengths, clusters, cluster_weight, source, tokens.T, cotangent.T, wide_norm, *constants())
    if not remote:
        grads = grads.reshape(NDP, NTEN, *tiles)
    return turned_out.T, turned_grad.T, grads, norm_grad


def shard_tiles(up, down, qkv, out):
    up = jnp.pad(up.reshape(15, 15, LANES), ((0, 1), (0, 0), (0, 0))).transpose(1, 0, 2)
    down = jnp.pad(down.reshape(4, 15, D), ((0, 0), (0, 1), (0, WIDE - D)))
    down = down.reshape(4, 16, 4, LANES).transpose(2, 0, 1, 3).reshape(16, 16, LANES)
    qkv = jnp.pad(qkv.reshape(4, 15, 360), ((0, 0), (0, 1), (0, CHUNK - 360)))
    qkv = qkv.reshape(4, 16, 3, LANES).transpose(2, 0, 1, 3).reshape(12, 16, LANES)
    out = jnp.pad(out.reshape(15, D), ((0, 1), (0, WIDE - D)))
    out = out.reshape(16, 4, LANES).transpose(1, 0, 2)
    return jnp.concatenate([up, down, out, qkv], 0)


def tiles_shard(tiles):
    up = tiles[UP0:DOWN0, :15].transpose(1, 0, 2).reshape(-1)
    down = tiles[DOWN0:OUT0].reshape(4, 4, 16, LANES).transpose(1, 2, 0, 3)[:, :15].reshape(60, WIDE)[:, :D].reshape(-1)
    qkv = tiles[QKV0:].reshape(3, 4, 16, LANES).transpose(1, 2, 0, 3)[:, :15].reshape(60, CHUNK)[:, :360].reshape(1, -1)
    out = tiles[OUT0:QKV0].transpose(1, 0, 2)[:15].reshape(15, WIDE)[:, :D].reshape(1, -1)
    return up, down, qkv, out


def adam_step(master, moment, square, average, grad, rate):
    moment_new = beta_one * moment + (1.0 - beta_one) * grad
    square_new = beta_two * square + (1.0 - beta_two) * grad * grad
    update = moment_new / (jnp.sqrt(square_new) + adam_eps) + decay_rate * master
    fresh = master - rate * update
    average_new = average_keep * average + (1.0 - average_keep) * fresh
    return (fresh, moment_new, square_new, average_new)


def to_groups(up, down, qkv, out):
    up, down = up.reshape(NDP, NTEN, -1), down.reshape(NDP, NTEN, -1)
    qkv = qkv.reshape(NTEN, NDP, -1).transpose(1, 0, 2)
    out = out.reshape(NTEN, NDP, -1).transpose(1, 0, 2)
    return jax.vmap(jax.vmap(shard_tiles))(up, down, qkv, out)


def from_groups(tiles):
    up, down, qkv, out = jax.vmap(jax.vmap(tiles_shard))(tiles.astype(f32))
    qkv = qkv.reshape(NDP, NTEN, -1).transpose(1, 0, 2).reshape(NTEN, -1)
    out = out.reshape(NDP, NTEN, -1).transpose(1, 0, 2).reshape(NTEN, -1)
    return up.reshape(-1), down.reshape(-1), qkv, out


def on_device(tokens, cotangent, lengths, clusters, cluster_weight, *state):
    qkv, out, up, down, norm = (state[4 * k : 4 * k + 4] for k in range(5))
    ends = ("dp", "tensor")
    low = tuple(w[0].astype(bf16) for w in (up, down, qkv, out))
    grid = (lax.axis_size("dp"), lax.axis_size("tensor")) == (NDP, NTEN)
    if grid:
        source = shard_tiles(*low)
    else:
        whole = [lax.all_gather(w, ends, axis=0, tiled=True) for w in low[:2]]
        for w in low[2:]:
            block = lax.all_gather(w, "dp", axis=1, tiled=True)
            whole.append(lax.all_gather(block, "tensor", axis=0, tiled=True))
        source = to_groups(*whole)
    layer_out, tokens_grad, total, norm_total = run_layer(
        lengths, clusters, cluster_weight, source, tokens, cotangent, norm[0], grid
    )
    if grid:
        grads = tiles_shard(total)
    else:
        whole = from_groups(total)
        grads = [lax.psum_scatter(g, ends, scatter_dimension=0, tiled=True) for g in whole[:2]]
        for g in whole[2:]:
            block = lax.psum_scatter(g, "tensor", scatter_dimension=0, tiled=True)
            grads.append(lax.psum_scatter(block, "dp", scatter_dimension=1, tiled=True))
        norm_total = lax.psum(norm_total, ends)
    up_grad, down_grad, qkv_grad, out_grad = grads
    results = (layer_out, tokens_grad)
    results += adam_step(*qkv, qkv_grad, D ** (-0.5))
    results += adam_step(*out, out_grad, (D // 32) ** (-0.5))
    results += adam_step(*up, up_grad, D ** (-0.5))
    results += adam_step(*down, down_grad, FF ** (-0.5))
    results += adam_step(*norm, norm_total[:4, :D], 0.2)
    return results


def solution(mesh):
    rows, both, flat = P(("dp", "tensor"), None), P("tensor", "dp"), P(("dp", "tensor"))
    state = (both,) * 8 + (flat,) * 8 + (P(),) * 4
    return jax.shard_map(
        on_device,
        mesh=mesh,
        in_specs=(rows, rows, P("dp"), P("dp"), P()) + state,
        out_specs=(rows, rows) + state,
        check_vma=False,
    )
```

time: 197 us -> 148 us (0.75)
  Pallas kernels: 171 us -> 131 us
  local copies, waits for them, and re-layouts: 16.9 us -> 9.13 us
    pallas_call x3 -> x1, Pallas kernels: 171 us -> 131 us  [run_layer(): pl.pallas_call(functools.partial(layer_kernel, remote), out_shape=(jax.Sh...]
    unnamed x58 -> x48, local copies, waits for them, and re-layouts: 14.3 us -> 5.73 us
    convert_element_type x4, other arithmetic: 3.77 us -> 1.07 us  [on_device(): low = tuple((w[0].astype(bf16) for w in (up, down, qkv, out)))]
where the time goes in v2:
time: 148 us
  Pallas kernels  131 us (89%)
  local copies, waits for them, and re-layouts  9.13 us (6%)
  other arithmetic  7.08 us (5%)
    pallas_call x1, Pallas kernels, run_layer(): pl.pallas_call(functools.partial(layer_kernel, remote), out_shape=(jax.Sh...  131 us
    unnamed x48, local copies, waits for them, and re-layouts  5.73 us
    add x4, other arithmetic, adam_step(): average_new = average_keep * average + (1.0 - average_keep) * fresh  5.3 us

profile of v2, /device:TPU:0, one launch (start us, length us, event | category | flops | bytes accessed | tf_op | source)
XLA Modules:
  0.0 147.9 jit_solution(13795597977309300789)
XLA Ops:
  0.7 0.0 copy-start.6
  0.7 1.3 pad.24.refs_6_
  2.0 0.8 convert_reduce_fusion.1
  2.8 0.1 reshape.158
  2.9 0.0 copy-done.6
  3.0 0.2 convert_reduce_fusion
  3.2 0.1 reshape.160
  3.4 0.0 copy-start.3
  3.4 0.8 copy-done.3
  4.3 0.0 copy-start.2
  4.4 0.8 copy-done.2
  5.2 0.1 reshape.155
  5.4 0.7 pad_maximum_fusion.refs_3_
  6.1 0.0 copy-start.18
  6.1 0.0 copy-start.19
  6.1 130.6 %layer.1 = (f32[480,512]{1,0:T(8,128)}, f32[480,512]{1,0:T(8,128)}, f32[47,16,128]{2,1,0:T(8,128)}, f32[8,512]{1,0:T(8,128)}) custom-call(s32[4]{0:T(128)} %refs_0_.1, s32[4]{0:T(128)} %refs_1_.1, f32[64]{0:T(128)} %refs_2_.1, bf16[47,16,128]{2,1,0:T(8,128)(2,1)} %pad_maximum_fusion.refs_3_, bf16[480,512]{1,0:T(8,128)(2,1)} %bitcast.52, ...), custom_call_target="tpu_custom_call" | custom-call | tf_op jit(solution)/shard_map/layer/pallas_call | solution.py:532
  136.7 0.0 copy-start.5
  136.8 0.8 slice_bitcast_fusion.1
  137.6 0.1 reshape.167
  137.7 0.0 copy-done.18
  137.7 0.0 copy-done.19
  137.8 0.0 copy-start.14
  137.8 1.4 multiply_add_fusion.9
  139.1 0.0 copy-done.14
  139.1 1.6 %multiply_add_fusion.7 = (f32[1,7200]{1,0:T(1,128)}, f32[1,7200]{1,0:T(1,128)}, f32[1,7200]{1,0:T(1,128)}, f32[1,7200]{1,0:T(1,128)}) fusion(f32[1,7200]{1,0:T(1,128)} %param.43, f32[1,7200]{1,0:T(1,128)S(1)} %copy-done.14, f32[1,7200]{1,0:T(1,128)S(1)} %reshape.167, f32[1,7200]{1,0:T(1,128)} %param.42, f32[1,7200]{1,0:T(1,128)} %param.41), kind=kLoop, calls=%fused_computation.25 | loop fusion | flops 108000 | bytes 259200 | tf_op jit(solution)/shard_map/add | solution.py:575
  140.8 0.0 copy-done.5
  140.8 0.1 copy.69
  140.9 0.2 reshape.165
  141.1 0.1 copy.68
  141.4 0.0 copy-start.15
  141.4 0.0 copy-start.16
  141.4 0.0 copy-start.17
  141.4 0.0 copy-start.7
  141.4 0.0 copy-start.13
  141.4 0.1 reshape.171
  141.6 0.7 copy-done.15
  142.3 0.0 copy-done.16
  142.3 0.0 copy-done.17
  142.3 0.0 copy-done.7
  142.4 0.0 copy-start.4
  142.4 0.0 copy-start.8
  142.4 0.0 copy-start.9
  142.4 0.0 copy-start.10
  142.4 0.0 copy-start.11
  142.4 0.0 copy-start.12
  142.4 1.3 multiply_add_fusion.5
  143.8 0.0 copy-done.13
  143.8 0.0 copy-done.4
  143.8 0.0 copy-done.8
  143.8 0.0 copy-done.9
  143.8 0.0 copy-done.10
  143.8 0.0 copy-done.11
  143.8 0.0 copy-done.12
  143.8 0.0 copy-start.1
  143.8 1.0 multiply_add_fusion.2
  144.8 0.6 copy-done.1
  145.4 0.0 copy-start
  145.4 0.9 copy.72
  146.3 0.6 copy-done
  146.9 0.9 copy.73
  (26 shorter events, 0.4 us)
Async XLA Ops:
  0.7 2.3 %copy-start.6 = (f32[1,21600]{1,0:T(1,128)S(1)}, f32[1,21600]{1,0:T(1,128)}, u32[]{:S(2)}) copy-start(f32[1,21600]{1,0:T(1,128)} %param.36) | copy-start | bytes 259204
  3.4 0.9 copy-start.3
  4.3 0.9 copy-start.2
  6.1 131.6 %copy-start.18 = (f32[4,480]{1,0:T(4,128)S(1)}, f32[4,480]{1,0:T(4,128)}, u32[]{:S(2)}) copy-start(f32[4,480]{1,0:T(4,128)} %param.52) | copy-start | bytes 23044
  6.1 131.6 %copy-start.19 = (f32[4,480]{1,0:T(4,128)S(1)}, f32[4,480]{1,0:T(4,128)}, u32[]{:S(2)}) copy-start(f32[4,480]{1,0:T(4,128)} %param.55) | copy-start | bytes 23044
  136.7 4.0 %copy-start.5 = (f32[47,16,128]{2,1,0:T(8,128)S(1)}, f32[47,16,128]{2,1,0:T(8,128)}, u32[]{:S(2)}) copy-start(f32[47,16,128]{2,1,0:T(8,128)} %get-tuple-element.28) | copy-start | bytes 1155076
  137.8 1.4 copy-start.14
  141.4 0.9 copy-start.15
  141.4 0.9 copy-start.16
  141.4 1.0 copy-start.17
  141.4 1.0 copy-start.7
  141.4 2.3 %copy-start.13 = (f32[28800]{0:T(1024)S(1)}, f32[28800]{0:T(1024)}, u32[]{:S(2)}) copy-start(f32[28800]{0:T(1024)} %param.47) | copy-start | bytes 345604
  142.4 1.4 copy-start.4
  142.4 1.4 copy-start.8
  142.4 1.4 copy-start.9
  142.4 1.4 copy-start.10
  142.4 1.4 copy-start.11
  142.4 1.4 copy-start.12
  143.8 1.5 %copy-start.1 = (f32[480,512]{1,0:T(8,128)S(1)}, f32[480,512]{1,0:T(8,128)}, u32[]{:S(2)}) copy-start(f32[480,512]{1,0:T(8,128)} %get-tuple-element.26) | copy-start | bytes 2949124
  145.4 1.6 %copy-start = (f32[480,512]{1,0:T(8,128)S(1)}, f32[480,512]{1,0:T(8,128)}, u32[]{:S(2)}) copy-start(f32[480,512]{1,0:T(8,128)} %get-tuple-element.27) | copy-start | bytes 2949124

commit v3 on v2

--- a/solution.py
+++ b/solution.py
@@ -17,9 +17,11 @@
 HEADS_DEV = 5
 LANES = 128
 TILES = 47
-UP0, DOWN0, OUT0, QKV0 = 0, 15, 31, 35
+JOINED = 1536
+UP0, OUT0, DOWN0, QKV0 = 0, 15, 19, 35
 CHUNK = 384
-QB = 256
+QB = 512
+SPARE = 120
 
 norm_eps = 1e-05
 beta_one = 0.5
@@ -27,7 +29,7 @@
 adam_eps = 1e-08
 decay_rate = 0.01
 average_keep = 0.75
-masked_score = -1e30
+hidden_score = -1e38
 MESH = pl.DeviceIdType.MESH
 f32, bf16 = jnp.float32, jnp.bfloat16
 
@@ -44,10 +46,6 @@
     natural = np.arange(D)
     squeeze = np.zeros((WIDE, WIDE), np.float32)
     squeeze[natural, 16 * (natural // 15) + natural % 15] = 1.0
-    spread = np.zeros((CHUNK, CHUNK), np.float32)
-    for third in range(3):
-        lane = np.arange(120)
-        spread[third * 120 + lane, third * 128 + lane] = 1.0
     position = np.arange(MAXLEN, dtype=np.float32)
     exponent = np.arange(HEAD // 2, dtype=np.float32) * np.float32(2.0 / HEAD)
     inverse = np.float32(10000.0) ** (-exponent)
@@ -62,47 +60,50 @@
     first[:, :120] = np.where(place < 12, -sines, 0.0)
     second[:, :120] = np.where(place >= 12, sines, 0.0)
     low = lambda v: jnp.asarray(v.astype(jnp.bfloat16))
-    return (low(squeeze), low(squeeze.T), low(spread), jnp.asarray(cosine), jnp.asarray(first), jnp.asarray(second))
-
-
-LATE, EARLY = (0, 1, 2), (3, 4, 5)
-ROUTES = (
-    (0, 14, (0, 1, 3, 2, 4)),
-    (14, 14, (0, 1, 2, 3, 4)),
-    (28, 7, (2, 3, 0, 1, 4)),
-    (35, 5, (0, 1, 3, 2, 4)),
-    (40, 5, (0, 1, 2, 3, 4)),
-    (45, 2, (2, 3, 0, 1, 4)),
+    return (low(squeeze), low(squeeze.T), jnp.asarray(cosine), jnp.asarray(first), jnp.asarray(second))
+
+
+UP, DOWN, EARLY = (0, 1, 2), (3, 4, 5), (6, 7, 8)
+WAY_A, WAY_B, WAY_C = (0, 1, 3, 2, 4), (0, 1, 2, 3, 4), (2, 3, 0, 1, 4)
+GATHER_ROUTES = (
+    (0, 8, WAY_A), (8, 8, WAY_B), (16, 3, WAY_C),
+    (19, 6, WAY_A), (25, 7, WAY_B), (32, 3, WAY_C),
+    (35, 5, WAY_A), (40, 5, WAY_B), (45, 2, WAY_C),
 )
-GATHER_AT = (3, 14)
-SCATTER_AT = (3, 12, 16, 19)
+SCATTER_ROUTES = (
+    (0, 6, WAY_A), (6, 6, WAY_B), (12, 3, WAY_C),
+    (15, 8, WAY_A), (23, 8, WAY_B), (31, 4, WAY_C),
+    (35, 5, WAY_A), (40, 5, WAY_B), (45, 2, WAY_C),
+)
+GATHER_AT = ((1, DOWN, 1), (3, UP, 3), (5, DOWN, 2), (10, UP, 4), (11, DOWN, 3), (18, DOWN, 4))
+SCATTER_AT = ((3, UP, 2), (4, DOWN, 1), (8, UP, 3), (10, DOWN, 2), (11, UP, 4), (14, DOWN, 3), (17, DOWN, 4))
 
 
 class Links:
     @staticmethod
     def scratch():
-        n, tiles = len(ROUTES), (TILES, 16, LANES)
+        n, tiles = len(SCATTER_ROUTES), (TILES, 16, LANES)
         bufs = [
             pltpu.VMEM((2,) * (4 - stage) + (count, 16, LANES), bf16)
-            for begin, count, order in ROUTES
+            for begin, count, order in SCATTER_ROUTES
             for stage in range(5)
         ]
         return bufs + [
             pltpu.VMEM((2,) * 5 + tiles, bf16),
             pltpu.VMEM((2,) * 5 + tiles, bf16),
-            pltpu.VMEM((5, 8, WIDE), f32),
-            pltpu.VMEM((5, 8, WIDE), f32),
+            pltpu.VMEM((3, 8, WIDE), f32),
+            pltpu.VMEM((3, 4, 8, WIDE), f32),
             pltpu.SemaphoreType.DMA,
             pltpu.SemaphoreType.DMA((n, 5)),
             pltpu.SemaphoreType.DMA((n, 5)),
             pltpu.SemaphoreType.DMA((n, 5)),
             pltpu.SemaphoreType.DMA((n, 5)),
-            pltpu.SemaphoreType.DMA((5,)),
-            pltpu.SemaphoreType.DMA((5,)),
+            pltpu.SemaphoreType.DMA((3, 3)),
+            pltpu.SemaphoreType.DMA((3, 3)),
         ]
 
     def __init__(self, shard, total, norm_total, *scratch):
-        n = len(ROUTES)
+        n = len(SCATTER_ROUTES)
         self.shard, self.total, self.norm_total = shard, total, norm_total
         self.bufs = [scratch[5 * r : 5 * r + 5] for r in range(n)]
         (
@@ -117,11 +118,30 @@
         c[dim] = 1 - c[dim]
         return (c[0] * 4 + c[1] * 2 + c[2], c[3] * 2 + c[4])
 
+    def peers(self, group):
+        z0, z1, x, y, core = self.coords
+        found = []
+        if group == 0:
+            mine = z0 * 2 + z1
+            for step in range(1, 4):
+                z = (mine + step) % 4
+                found.append(((z * 2 + x, y * 2 + core), z))
+        elif group == 1:
+            mine = x * 2 + y
+            for dx, dy in ((0, 1), (1, 0), (1, 1)):
+                px, py = (x + dx) % 2, (y + dy) % 2
+                found.append((((z0 * 2 + z1) * 2 + px, py * 2 + core), px * 2 + py))
+        else:
+            mine = core
+            found.append((((z0 * 2 + z1) * 2 + x, y * 2 + 1 - core), 1 - core))
+        return found, mine
+
     def greet(self):
         barrier = pltpu.get_barrier_semaphore()
-        for dim in range(5):
-            pl.semaphore_signal(barrier, inc=1, device_id=self.partner(dim), device_id_type=MESH)
-        pl.semaphore_wait(barrier, 5)
+        others = [device for group in range(3) for device, slot in self.peers(group)[0]]
+        for device in others:
+            pl.semaphore_signal(barrier, inc=1, device_id=device, device_id_type=MESH)
+        pl.semaphore_wait(barrier, len(others))
 
     def keep_own(self):
         copy = pltpu.make_async_copy(self.shard, self.whole.at[self.coords], self.own_sem)
@@ -129,7 +149,7 @@
         copy.wait()
 
     def gather_copy(self, r, stage):
-        begin, count, order = ROUTES[r]
+        begin, count, order = GATHER_ROUTES[r]
         done, dim = order[:stage], order[stage]
         where = tuple(slice(None) if d in done else self.coords[d] for d in range(5)) + (pl.ds(begin, count),)
         return pltpu.make_async_remote_copy(
@@ -149,7 +169,7 @@
                 self.gather_copy(r, stage).start()
 
     def sums(self, r, stage, coordinate):
-        begin, count, order = ROUTES[r]
+        begin, count, order = SCATTER_ROUTES[r]
         order = order[::-1]
         left = [d for d in range(5) if d not in order[:stage]]
         where = tuple(coordinate if d == order[stage] else slice(None) for d in left)
@@ -158,7 +178,7 @@
         return self.bufs[r][stage - 1].at[where]
 
     def scatter_copy(self, r, stage):
-        dim = ROUTES[r][2][4 - stage]
+        dim = SCATTER_ROUTES[r][2][4 - stage]
         return pltpu.make_async_remote_copy(
             src_ref=self.sums(r, stage, 1 - self.coords[dim]),
             dst_ref=self.bufs[r][stage],
@@ -170,7 +190,7 @@
 
     def scatter_step(self, group, stage):
         for r in group:
-            begin, count, order = ROUTES[r]
+            begin, count, order = SCATTER_ROUTES[r]
             if stage > 0:
                 self.scatter_copy(r, stage - 1).wait_recv()
                 buf = self.bufs[r][stage - 1]
@@ -182,35 +202,46 @@
             if stage < 5:
                 self.scatter_copy(r, stage).start()
 
-    def norm_copy(self, stage):
-        return pltpu.make_async_remote_copy(
-            src_ref=self.norm_now.at[stage],
-            dst_ref=self.norm_in.at[stage],
-            send_sem=self.n_send.at[stage],
-            recv_sem=self.n_recv.at[stage],
-            device_id=self.partner(stage),
-            device_id_type=MESH,
-        )
-
-    def norm_start(self, values):
-        self.norm_now[0] = values
-        self.norm_copy(0).start()
-
-    def norm_step(self, stage):
-        self.norm_copy(stage).wait_recv()
-        now = self.norm_now[stage] + self.norm_in[stage]
-        if stage < 4:
-            self.norm_now[stage + 1] = now
-            self.norm_copy(stage + 1).start()
+    def norm_copies(self, group):
+        found, mine = self.peers(group)
+        return [
+            pltpu.make_async_remote_copy(
+                src_ref=self.norm_now.at[group],
+                dst_ref=self.norm_in.at[group, mine],
+                send_sem=self.n_send.at[group, k],
+                recv_sem=self.n_recv.at[group, k],
+                device_id=device,
+                device_id_type=MESH,
+            )
+            for k, (device, slot) in enumerate(found)
+        ]
+
+    def norm_start(self, values, group=0):
+        self.norm_now[group] = values
+        self.norm_in[group, self.peers(group)[1]] = values
+        for copy in self.norm_copies(group):
+            copy.start()
+
+    def norm_step(self, group):
+        for copy in self.norm_copies(group):
+            copy.wait_recv()
+        now = self.norm_in[group, 0]
+        for slot in range(1, 2 if group == 2 else 4):
+            now = now + self.norm_in[group, slot]
+        if group < 2:
+            self.norm_start(now, group + 1)
         else:
             self.norm_total[...] = now
 
     def finish(self):
         for stage in range(5):
-            for r in range(len(ROUTES)):
+            for r in range(len(GATHER_ROUTES)):
                 self.gather_copy(r, stage).wait_send()
+            for r in range(len(SCATTER_ROUTES)):
                 self.scatter_copy(r, stage).wait_send()
-            self.norm_copy(stage).wait_send()
+        for group in range(3):
+            for copy in self.norm_copies(group):
+                copy.wait_send()
 
 
 def gelu_parts(u):
@@ -219,14 +250,14 @@
 
 
 def layer_kernel(remote, *refs):
-    lengths, clusters, weights_of, source, tok, cot, norm, squeeze, widen, spread, cosine, first, second = refs[:13]
-    layer_out, tokens_grad, G_out, norm_out = refs[13:17]
+    lengths, clusters, weights_of, source, tok, cot, norm, squeeze, widen, cosine, first, second = refs[:12]
+    layer_out, tokens_grad, G_out, norm_out = refs[12:16]
     (
-        up_s, down_s, qkv_s, out_s, q_s, k_s, v_s, kT_s, vT_s, P_s, OT_s, att_s, dA_s, dqT_s, dk_s, dv_s,
-        act1_s, act2_s, act_pad, plain1, plain2, res_s, y_s, dn_s, dres_s, dlow_s, eye_s, gdown_s, x_s,
-    ) = refs[17:46]
-    if remote:
-        links = Links(source, G_out, norm_out, *refs[46:])
+        up_s, down_s, qkv_s, dj_s, out_s, q_s, k_s, v_s, kT_s, vT_s, P_s, OT_s, att_s, dA_s, dqT_s, dk_s, dv_s,
+        act1_s, act2_s, act_pad, plain1, plain2, res_s, y_s, dn_s, dres_s, dlow_s, eye_s, x_s, centre_s, ds_s, act_pad1,
+    ) = refs[16:48]
+    if remote:
+        links = Links(source, G_out, norm_out, *refs[48:])
         W, G = links.whole, links.parts
         links.greet()
         links.keep_own()
@@ -272,74 +303,88 @@
     row_scale = jnp.where(row < length, scale_row, 0.0)
     dres_s[...] = dres_s[...].T * row_scale
     dlow_s[...] = dres_s[...].astype(bf16)
+    act_pad1[...] = mm_nt(widen[...], act1_s[...]).astype(bf16)
     if remote:
         links.gather_step(EARLY, 2)
-        links.gather_step(LATE, 0)
+        links.gather_step(UP, 0)
         links.gather_step(EARLY, 3)
         links.gather_step(EARLY, 4)
-        links.gather_step(LATE, 1)
+        links.gather_step(UP, 1)
         links.gather_step(EARLY, 5)
-        links.gather_step(LATE, 2)
+        links.gather_step(UP, 2)
+        links.gather_step(DOWN, 0)
+
+    for pair in range(2):
+        pieces = []
+        for t in (2 * pair, 2 * pair + 1):
+            mine = (slice(None),) * 3 + (t // 2, t % 2)
+            pieces += [W[mine + (slice(QKV0 + 4 * c, QKV0 + 4 * c + 4),)].reshape(WIDE, LANES) for c in range(3)]
+        half = slice(pair * (JOINED // 2), (pair + 1) * (JOINED // 2))
+        qkv_s[:, half] = mm(squeeze[...], jnp.concatenate(pieces, 1)).astype(bf16)
+    cosv, firstv, secondv = cosine[...], first[...], second[...]
+    lane_id = lax.broadcasted_iota(jnp.int32, (1, LANES), 1)
+    key_id = lax.broadcasted_iota(jnp.int32, (MAXLEN, 1), 0)
+    spare = jnp.where(lane_id == SPARE, 1.0, 0.0)
+    key_bias = jnp.where(key_id < length, 0.0, hidden_score) * spare
+
+    def strided(block):
+        gap = jnp.zeros((8, MAXLEN), f32)
+        return jnp.concatenate([x for j in range(HEADS_DEV) for x in (block[j * HEAD : (j + 1) * HEAD], gap)], 0)
+
+    def dense(block):
+        rows = [block[j * 32 : j * 32 + HEAD] for j in range(HEADS_DEV)]
+        return jnp.concatenate(rows + [jnp.zeros((8, MAXLEN), f32)], 0)
 
     for t in range(NTEN):
-        mine = (slice(None),) * 3 + (t // 2, t % 2)
-        pieces = [W[mine + (slice(QKV0 + 4 * c, QKV0 + 4 * c + 4),)].reshape(WIDE, LANES) for c in range(3)]
-        plain = mm(squeeze[...], jnp.concatenate(pieces, 1)).astype(bf16)
-        qkv_s[t] = mm(plain, spread[...]).astype(bf16)
-    cosv, firstv, secondv = cosine[...], first[...], second[...]
-    for t in range(NTEN):
-        joined = mm(act1_s[...], qkv_s[t])
+        if t % 2 == 0:
+            both = mm(act1_s[...], qkv_s[:, t * 3 * LANES : (t + 2) * 3 * LANES])
+        joined = both[:, (t % 2) * 3 * LANES : (t % 2 + 1) * 3 * LANES]
         for number in range(2):
             u = joined[:, number * LANES : (number + 1) * LANES]
             r = u * cosv + pltpu.roll(u, LANES - 12, 1) * firstv + pltpu.roll(u, 12, 1) * secondv
             if number == 0:
-                q_s[t] = r.astype(bf16)
+                q_s[t] = (r + spare).astype(bf16)
             else:
-                k_s[t] = r.astype(bf16)
-                kT_s[t] = r.T.astype(bf16)
+                k_s[t] = (r + key_bias).astype(bf16)
+                kT_s[t] = strided(r.T).astype(bf16)
         v = joined[:, 2 * LANES :]
         v_s[t] = v.astype(bf16)
-        vT_s[t] = v.T.astype(bf16)
-
-    lane_id = lax.broadcasted_iota(jnp.int32, (1, LANES), 1)
-    row_id = lax.broadcasted_iota(jnp.int32, (LANES, 1), 0)
-    key_id = lax.broadcasted_iota(jnp.int32, (MAXLEN, 1), 0)
-    usable = key_id < length
-
-    OT_s[...] = jnp.zeros_like(OT_s)
+        vT_s[t] = strided(v.T).astype(bf16)
+
+    fold = HEAD ** -0.5 * 1.4426950408889634
 
     def forward_head(h, carry):
         t = h // HEADS_DEV
-        begin = (h - t * HEADS_DEV) * HEAD
-        lanes = jnp.where((lane_id >= begin) & (lane_id < begin + HEAD), 1.0, 0.0).astype(bf16)
-        rows = jnp.where((row_id >= begin) & (row_id < begin + HEAD), 1.0, 0.0).astype(bf16)
-        keys = k_s[t] * lanes
-        values = vT_s[t] * rows
+        j = h - t * HEADS_DEV
+        begin = j * HEAD
+        kept = ((lane_id >= begin) & (lane_id < begin + HEAD)) | (lane_id == SPARE)
+        keys = k_s[t] * jnp.where(kept, 1.0, 0.0).astype(bf16)
+        rows = pl.ds(pl.multiple_of(j * 32, 32), 32)
+        values = vT_s[t, rows, :]
         for b in range(MAXLEN // QB):
             cols = slice(b * QB, (b + 1) * QB)
             s = mm_nt(keys, q_s[t, cols, :])
-            s = jnp.where(usable, s * scale, masked_score)
             top = jnp.max(s, axis=0, keepdims=True)
-            e = jnp.exp(s - top)
+            e = jnp.exp2(s * fold - top * fold)
             total = jnp.sum(e, axis=0, keepdims=True)
             p = (e * (1.0 / total)).astype(bf16)
             P_s[h, :, cols] = p
-            OT_s[t, :, cols] += mm(values, p)
+            OT_s[t, rows, cols] = mm(values, p)
         if remote:
-            for number, when in enumerate(GATHER_AT):
-                pl.when(h == when)(functools.partial(links.gather_step, LATE, 3 + number))
+            for when, group, number in GATHER_AT:
+                pl.when(h == when)(functools.partial(links.gather_step, group, number))
         return carry
 
     lax.fori_loop(0, NTEN * HEADS_DEV, forward_head, 0)
 
     if remote:
-        links.gather_step(LATE, 5)
+        links.gather_step(UP, 5)
     res = x_s[...]
     for t in range(NTEN):
         mine = (slice(None),) * 3 + (t // 2, t % 2)
         pieces = [W[mine + (OUT0 + c,)].reshape(LANES, LANES) for c in range(4)]
         out_s[t] = mm(squeeze[:LANES, :LANES], jnp.concatenate(pieces, 1)).astype(bf16)
-        att_s[t] = OT_s[t].T.astype(bf16)
+        att_s[t] = dense(OT_s[t]).T.astype(bf16)
         res = res + mm(att_s[t], out_s[t])
     res_s[...] = res
     normed, plain, inverse2 = norm_rows(res, gains[2:3], gains[3:4])
@@ -347,9 +392,12 @@
     act2_s[...] = normed.astype(bf16)
     act_pad[...] = mm_nt(widen[...], act2_s[...]).astype(bf16)
 
-    for c in range(15):
-        part = mm(squeeze[...], W[:, :, :, :, :, UP0 + c].reshape(WIDE, LANES)).astype(bf16)
-        up_s[:, c * LANES : (c + 1) * LANES] = part
+    for c in range(8):
+        pieces = [W[:, :, :, :, :, UP0 + n].reshape(WIDE, LANES) for n in range(2 * c, min(2 * c + 2, 15))]
+        up_s[:, 2 * c * LANES : (2 * c + len(pieces)) * LANES] = mm(squeeze[...], jnp.concatenate(pieces, 1)).astype(bf16)
+
+    if remote:
+        links.gather_step(DOWN, 5)
 
     def down_rows(k, carry):
         mine = (k // 4, (k // 2) % 2, k % 2)
@@ -380,22 +428,24 @@
         for part in range(3):
             G[:, :, :, :, :, UP0 + 3 * c + part] = g_up[:, part * LANES : (part + 1) * LANES].reshape(2, 2, 2, 2, 2, 16, LANES)
         aT = mm_nt(eye_s[...], a).astype(bf16)
-        gdown_s[cols, :] = mm(aT, dlow_s[...]).astype(bf16)
+        down_s[cols, :] = mm(aT, dlow_s[...]).astype(bf16)
         return carry
 
     lax.fori_loop(0, FF // CHUNK, hidden_chunk, 0)
+    if remote:
+        links.scatter_step(UP, 0)
     y_s[...] = y_s[...].T
     layer_out[...] = y_s[:D, :]
 
     def down_groups(k, carry):
-        part = mm(widen[:256, :240], gdown_s[pl.ds(pl.multiple_of(k * 240, 16), 240), :]).astype(bf16)
+        part = mm(widen[:256, :240], down_s[pl.ds(pl.multiple_of(k * 240, 16), 240), :]).astype(bf16)
         mine = (k // 4, (k // 2) % 2, k % 2)
         for c in range(4):
             where = mine + (slice(None),) * 2 + (slice(DOWN0 + 4 * c, DOWN0 + 4 * c + 4),)
             G[where] = part[:, c * LANES : (c + 1) * LANES].reshape(2, 2, 4, 16, LANES)
         return carry
 
-    lax.fori_loop(0, 8, down_groups, 0)
+    lax.fori_loop(0, NDP, down_groups, 0)
 
     d_from, dg2, db2 = norm_back(dn_s[...], plain2[...], inverse2, gains[2:3])
     d_res = dres_s[...] + d_from
@@ -404,66 +454,64 @@
 
     for t in range(NTEN):
         dA_s[t] = mm_nt(dlow_s[...], out_s[t]).astype(bf16)
+        dAT = mm_nt(out_s[t], dlow_s[...]).astype(bf16).astype(f32)
+        product = OT_s[t] * strided(dAT)
+        for j in range(HEADS_DEV):
+            centre_s[t, j : j + 1, :] = jnp.sum(product[j * 32 : j * 32 + HEAD], axis=0, keepdims=True)
         attT = mm_nt(widen[:LANES, :LANES], att_s[t]).astype(bf16)
         part = mm(attT, dlow_s[...]).astype(bf16)
         mine = (slice(None),) * 3 + (t // 2, t % 2)
         for c in range(4):
             G[mine + (OUT0 + c,)] = part[:, c * LANES : (c + 1) * LANES].reshape(2, 2, 2, 16, LANES)
     if remote:
-        links.scatter_step(LATE, 0)
-
-    dqT_s[...] = jnp.zeros_like(dqT_s)
+        links.scatter_step(DOWN, 0)
+        links.scatter_step(UP, 1)
+
     dk_s[...] = jnp.zeros_like(dk_s)
     dv_s[...] = jnp.zeros_like(dv_s)
 
     def backward_head(h, carry):
         t = h // HEADS_DEV
-        begin = (h - t * HEADS_DEV) * HEAD
+        j = h - t * HEADS_DEV
+        begin = j * HEAD
         lanes = jnp.where((lane_id >= begin) & (lane_id < begin + HEAD), 1.0, 0.0).astype(bf16)
-        rows = jnp.where((row_id >= begin) & (row_id < begin + HEAD), 1.0, 0.0).astype(bf16)
+        rows = pl.ds(pl.multiple_of(j * 32, 32), 32)
         values = v_s[t]
-        keysT = kT_s[t] * rows
+        keysT = kT_s[t, rows, :]
+        dA = dA_s[t] * lanes
         for b in range(MAXLEN // QB):
             cols = slice(b * QB, (b + 1) * QB)
-            dA = dA_s[t, cols, :] * lanes
-            dP = mm_nt(values, dA)
-            low = P_s[h, :, cols]
-            p = low.astype(f32)
-            centre = jnp.sum(p * dP, axis=0, keepdims=True)
-            ds = (p * (dP - centre)).astype(bf16)
-            dv_s[t] += mm(low, dA)
-            dk_s[t] += mm(ds, q_s[t, cols, :] * lanes)
-            dqT_s[t, :, cols] += mm(keysT, ds)
+            dP = mm_nt(values, dA[cols])
+            ds = (P_s[h, :, cols].astype(f32) * (dP - centre_s[t, pl.ds(j, 1), cols])).astype(bf16)
+            ds_s[:, cols] = ds
+            dqT_s[t, rows, cols] = mm(keysT, ds)
+        dv_s[t] += mm(P_s[h], dA)
+        dk_s[t] += mm(ds_s[...], q_s[t] * lanes)
         if remote:
-            for number, when in enumerate(SCATTER_AT):
-                pl.when(h == when)(functools.partial(links.scatter_step, LATE, 1 + number))
+            for when, group, number in SCATTER_AT:
+                pl.when(h == when)(functools.partial(links.scatter_step, group, number))
         return carry
 
     lax.fori_loop(0, NTEN * HEADS_DEV, backward_head, 0)
 
-    act_pad[...] = mm_nt(widen[...], act1_s[...]).astype(bf16)
     for t in range(NTEN):
-        pieces = []
+        first_lane = t * 3 * LANES
         for number in range(2):
-            g = (dqT_s[t].T if number == 0 else dk_s[t]) * scale
+            g = (dense(dqT_s[t]).T if number == 0 else dk_s[t]) * scale
             r = g * cosv - pltpu.roll(g, LANES - 12, 1) * firstv - pltpu.roll(g, 12, 1) * secondv
-            pieces.append(r.astype(bf16))
-        pieces.append(dv_s[t].astype(bf16))
-        d_joined = jnp.concatenate(pieces, 1)
-        q_s[t], k_s[t], v_s[t] = pieces
-        natural = mm_nt(d_joined, spread[...]).astype(bf16)
-        part = mm(act_pad[...], natural).astype(bf16)
-        mine = (slice(None),) * 3 + (t // 2, t % 2)
-        for c in range(3):
-            where = mine + (slice(QKV0 + 4 * c, QKV0 + 4 * c + 4),)
-            G[where] = part[:, c * LANES : (c + 1) * LANES].reshape(2, 2, 2, 4, 16, LANES)
+            dj_s[:, first_lane + number * LANES : first_lane + (number + 1) * LANES] = r.astype(bf16)
+        dj_s[:, first_lane + 2 * LANES : first_lane + 3 * LANES] = dv_s[t].astype(bf16)
+    for pair in range(2):
+        part = mm(act_pad1[...], dj_s[:, pair * (JOINED // 2) : (pair + 1) * (JOINED // 2)]).astype(bf16)
+        for number in range(6):
+            t, c = 2 * pair + number // 3, number % 3
+            where = (slice(None),) * 3 + (t // 2, t % 2) + (slice(QKV0 + 4 * c, QKV0 + 4 * c + 4),)
+            G[where] = part[:, number * LANES : (number + 1) * LANES].reshape(2, 2, 2, 4, 16, LANES)
     if remote:
         links.scatter_step(EARLY, 0)
-        links.scatter_step(LATE, 5)
-    dz = jnp.zeros((MAXLEN, WIDE), f32)
-    for t in range(NTEN):
-        for number, ref in enumerate((q_s, k_s, v_s)):
-            dz = dz + mm_nt(ref[t], qkv_s[t, :, number * LANES : (number + 1) * LANES])
+        links.scatter_step(UP, 5)
+        links.scatter_step(DOWN, 5)
+    dz = mm_nt(dj_s[...], qkv_s[...])
     d_from, dg1, db1 = norm_back(dz, plain1[...], inverse1, gains[0:1])
     norm_parts = jnp.concatenate([dg1, db1, dg2, db2, jnp.zeros((4, WIDE), f32)], 0)
     if remote:
@@ -474,10 +522,13 @@
     x_s[...] = (dres_s[...] + d_from).T
     tokens_grad[...] = x_s[:D, :]
     if remote:
-        for stage in range(5):
-            if stage > 0:
-                links.scatter_step(EARLY, stage + 1)
-            links.norm_step(stage)
+        links.norm_step(0)
+        links.scatter_step(EARLY, 2)
+        links.norm_step(1)
+        links.scatter_step(EARLY, 3)
+        links.norm_step(2)
+        links.scatter_step(EARLY, 4)
+        links.scatter_step(EARLY, 5)
         links.finish()
 
 
@@ -487,12 +538,13 @@
     smem = pl.BlockSpec(memory_space=pltpu.SMEM)
     vmem = pl.BlockSpec(memory_space=pltpu.VMEM)
     head_set = (NTEN, MAXLEN, LANES)
-    turned = (NTEN, LANES, MAXLEN)
+    turned = (NTEN, HEADS_DEV * 32, MAXLEN)
     wide = (rows, WIDE)
     scratch = [
         pltpu.VMEM((WIDE, FF), bf16),
         pltpu.VMEM((FF, WIDE), bf16),
-        pltpu.VMEM((NTEN, WIDE, CHUNK), bf16),
+        pltpu.VMEM((WIDE, JOINED), bf16),
+        pltpu.VMEM((WIDE, JOINED), bf16),
         pltpu.VMEM((NTEN, LANES, WIDE), bf16),
         pltpu.VMEM(head_set, bf16),
         pltpu.VMEM(head_set, bf16),
@@ -517,8 +569,10 @@
         pltpu.VMEM(wide, f32),
         pltpu.VMEM(wide, bf16),
         pltpu.VMEM((CHUNK, CHUNK), bf16),
-        pltpu.VMEM((FF, WIDE), bf16),
         pltpu.VMEM(wide, f32),
+        pltpu.VMEM((NTEN, 8, MAXLEN), f32),
+        pltpu.VMEM((MAXLEN, MAXLEN), bf16),
+        pltpu.VMEM(wide, bf16),
     ]
     tiles = (TILES, 16, LANES)
     params = dict(vmem_limit_bytes=66_900_000)
@@ -537,7 +591,7 @@
             result,
             jax.ShapeDtypeStruct((8, WIDE), f32),
         ),
-        in_specs=[smem] * 3 + [vmem] * 10,
+        in_specs=[smem] * 3 + [vmem] * 9,
         out_specs=[vmem] * 4,
         scratch_shapes=scratch,
         compiler_params=pltpu.CompilerParams(**params),
@@ -552,18 +606,18 @@
     up = jnp.pad(up.reshape(15, 15, LANES), ((0, 1), (0, 0), (0, 0))).transpose(1, 0, 2)
     down = jnp.pad(down.reshape(4, 15, D), ((0, 0), (0, 1), (0, WIDE - D)))
     down = down.reshape(4, 16, 4, LANES).transpose(2, 0, 1, 3).reshape(16, 16, LANES)
-    qkv = jnp.pad(qkv.reshape(4, 15, 360), ((0, 0), (0, 1), (0, CHUNK - 360)))
-    qkv = qkv.reshape(4, 16, 3, LANES).transpose(2, 0, 1, 3).reshape(12, 16, LANES)
+    qkv = jnp.pad(qkv.reshape(4, 15, 3, 120), ((0, 0), (0, 1), (0, 0), (0, LANES - 120)))
+    qkv = qkv.transpose(2, 0, 1, 3).reshape(12, 16, LANES)
     out = jnp.pad(out.reshape(15, D), ((0, 1), (0, WIDE - D)))
     out = out.reshape(16, 4, LANES).transpose(1, 0, 2)
-    return jnp.concatenate([up, down, out, qkv], 0)
+    return jnp.concatenate([up, out, down, qkv], 0)
 
 
 def tiles_shard(tiles):
-    up = tiles[UP0:DOWN0, :15].transpose(1, 0, 2).reshape(-1)
-    down = tiles[DOWN0:OUT0].reshape(4, 4, 16, LANES).transpose(1, 2, 0, 3)[:, :15].reshape(60, WIDE)[:, :D].reshape(-1)
-    qkv = tiles[QKV0:].reshape(3, 4, 16, LANES).transpose(1, 2, 0, 3)[:, :15].reshape(60, CHUNK)[:, :360].reshape(1, -1)
-    out = tiles[OUT0:QKV0].transpose(1, 0, 2)[:15].reshape(15, WIDE)[:, :D].reshape(1, -1)
+    up = tiles[UP0:OUT0, :15].transpose(1, 0, 2).reshape(-1)
+    down = tiles[DOWN0:QKV0].reshape(4, 4, 16, LANES).transpose(1, 2, 0, 3)[:, :15].reshape(60, WIDE)[:, :D].reshape(-1)
+    qkv = tiles[QKV0:].reshape(3, 4, 16, LANES).transpose(1, 2, 0, 3)[:, :15, :, :120].reshape(1, -1)
+    out = tiles[OUT0:DOWN0].transpose(1, 0, 2)[:15].reshape(15, WIDE)[:, :D].reshape(1, -1)
     return up, down, qkv, out
 
 

time: 148 us -> 134 us (0.905)
  Pallas kernels: 131 us -> 116 us
    pallas_call x1, Pallas kernels: 131 us -> 116 us  [run_layer(): pl.pallas_call(functools.partial(layer_kernel, remote), out_shape=(jax.Sh...]
    unnamed x48 -> x46, local copies, waits for them, and re-layouts: 5.73 us -> 5.67 us
where the time goes in v3:
time: 134 us
  Pallas kernels  116 us (87%)
  local copies, waits for them, and re-layouts  9.1 us (7%)
  other arithmetic  7.07 us (5%)
    pallas_call x1, Pallas kernels, run_layer(): pl.pallas_call(functools.partial(layer_kernel, remote), out_shape=(jax.Sh...  116 us
    unnamed x46, local copies, waits for them, and re-layouts  5.67 us
    add x4, other arithmetic, adam_step(): average_new = average_keep * average + (1.0 - average_keep) * fresh  5.29 us

profile of v3, /device:TPU:0, one launch (start us, length us, event | category | flops | bytes accessed | tf_op | source)
XLA Modules:
  0.0 133.5 jit_solution(2663703882926098089)
XLA Ops:
  0.7 0.0 copy-start.6
  0.7 1.3 pad.24.refs_6_
  2.0 0.8 convert_reduce_fusion.1
  2.8 0.1 reshape.149
  2.9 0.0 copy-done.6
  3.0 0.2 convert_reduce_fusion
  3.2 0.1 reshape.154
  3.3 0.0 copy-start.3
  3.4 0.8 copy-done.3
  4.3 0.0 copy-start.2
  4.4 0.8 copy-done.2
  5.2 0.1 reshape.151
  5.4 0.7 pad_maximum_fusion.refs_3_
  6.1 0.0 copy-start.18
  6.1 0.0 copy-start.19
  6.1 116.3 %layer.1 = (f32[480,512]{1,0:T(8,128)}, f32[480,512]{1,0:T(8,128)}, f32[47,16,128]{2,1,0:T(8,128)}, f32[8,512]{1,0:T(8,128)}) custom-call(s32[4]{0:T(128)} %refs_0_.1, s32[4]{0:T(128)} %refs_1_.1, f32[64]{0:T(128)} %refs_2_.1, bf16[47,16,128]{2,1,0:T(8,128)(2,1)} %pad_maximum_fusion.refs_3_, bf16[480,512]{1,0:T(8,128)(2,1)} %bitcast.47, ...), custom_call_target="tpu_custom_call" | custom-call | tf_op jit(solution)/shard_map/layer/pallas_call | solution.py:586
  122.4 0.0 copy-start.5
  122.4 0.8 slice_bitcast_fusion.1
  123.3 0.1 reshape.159
  123.4 0.0 copy-done.18
  123.4 0.0 copy-done.19
  123.4 0.0 copy-start.14
  123.5 1.4 %multiply_add_fusion.9 = (f32[4,480]{1,0:T(4,128)}, f32[4,480]{1,0:T(4,128)}, f32[4,480]{1,0:T(4,128)}, f32[4,480]{1,0:T(4,128)}) fusion(f32[4,480]{1,0:T(4,128)S(1)} %copy-done.19, f32[4,480]{1,0:T(4,128)S(1)} %copy-done.18, f32[8,512]{1,0:T(8,128)} %get-tuple-element.29, f32[4,480]{1,0:T(4,128)} %param.53, f32[4,480]{1,0:T(4,128)} %param.52), kind=kLoop, calls=%fused_computation.34 | loop fusion | flops 28800 | bytes 69120 | tf_op jit(solution)/shard_map/add | solution.py:629
  124.8 0.0 copy-done.14
  124.8 1.6 %multiply_add_fusion.7 = (f32[1,7200]{1,0:T(1,128)}, f32[1,7200]{1,0:T(1,128)}, f32[1,7200]{1,0:T(1,128)}, f32[1,7200]{1,0:T(1,128)}) fusion(f32[1,7200]{1,0:T(1,128)} %param.42, f32[1,7200]{1,0:T(1,128)S(1)} %copy-done.14, f32[1,7200]{1,0:T(1,128)S(1)} %reshape.159, f32[1,7200]{1,0:T(1,128)} %param.41, f32[1,7200]{1,0:T(1,128)} %param.40), kind=kLoop, calls=%fused_computation.26 | loop fusion | flops 108000 | bytes 259200 | tf_op jit(solution)/shard_map/add | solution.py:629
  126.4 0.0 copy-done.5
  126.5 0.1 copy.69
  126.6 0.2 reshape.157
  126.8 0.1 copy.68
  127.0 0.0 copy-start.15
  127.0 0.0 copy-start.16
  127.0 0.0 copy-start.17
  127.1 0.0 copy-start.7
  127.1 0.0 copy-start.13
  127.1 0.1 reshape.163
  127.2 0.7 copy-done.15
  127.9 0.0 copy-done.16
  128.0 0.0 copy-done.17
  128.0 0.0 copy-done.7
  128.1 0.0 copy-start.4
  128.1 0.0 copy-start.8
  128.1 0.0 copy-start.9
  128.1 0.0 copy-start.10
  128.1 0.0 copy-start.11
  128.1 0.0 copy-start.12
  128.1 1.3 multiply_add_fusion.5
  129.4 0.0 copy-done.13
  129.4 0.0 copy-done.4
  129.4 0.0 copy-done.8
  129.4 0.0 copy-done.9
  129.4 0.0 copy-done.10
  129.4 0.0 copy-done.11
  129.5 0.0 copy-done.12
  129.5 0.0 copy-start.1
  129.5 1.0 multiply_add_fusion.2
  130.5 0.5 copy-done.1
  131.0 0.0 copy-start
  131.0 0.9 copy.72
  132.0 0.6 copy-done
  132.6 0.9 copy.73
  (23 shorter events, 0.4 us)
Async XLA Ops:
  0.7 2.3 %copy-start.6 = (f32[1,21600]{1,0:T(1,128)S(1)}, f32[1,21600]{1,0:T(1,128)}, u32[]{:S(2)}) copy-start(f32[1,21600]{1,0:T(1,128)} %param.35) | copy-start | bytes 259204
  3.3 0.9 copy-start.3
  4.3 0.9 copy-start.2
  6.1 117.3 %copy-start.18 = (f32[4,480]{1,0:T(4,128)S(1)}, f32[4,480]{1,0:T(4,128)}, u32[]{:S(2)}) copy-start(f32[4,480]{1,0:T(4,128)} %param.51) | copy-start | bytes 23044
  6.1 117.3 %copy-start.19 = (f32[4,480]{1,0:T(4,128)S(1)}, f32[4,480]{1,0:T(4,128)}, u32[]{:S(2)}) copy-start(f32[4,480]{1,0:T(4,128)} %param.54) | copy-start | bytes 23044
  122.4 4.0 %copy-start.5 = (f32[47,16,128]{2,1,0:T(8,128)S(1)}, f32[47,16,128]{2,1,0:T(8,128)}, u32[]{:S(2)}) copy-start(f32[47,16,128]{2,1,0:T(8,128)} %get-tuple-element.28) | copy-start | bytes 1155076
  123.4 1.4 %copy-start.14 = (f32[1,7200]{1,0:T(1,128)S(1)}, f32[1,7200]{1,0:T(1,128)}, u32[]{:S(2)}) copy-start(f32[1,7200]{1,0:T(1,128)} %param.39) | copy-start | bytes 86404
  127.0 0.9 copy-start.15
  127.0 0.9 copy-start.16
  127.0 1.0 copy-start.17
  127.1 1.0 copy-start.7
  127.1 2.3 %copy-start.13 = (f32[28800]{0:T(1024)S(1)}, f32[28800]{0:T(1024)}, u32[]{:S(2)}) copy-start(f32[28800]{0:T(1024)} %param.46) | copy-start | bytes 345604
  128.1 1.4 %copy-start.4 = (f32[28800]{0:T(1024)S(1)}, f32[28800]{0:T(1024)}, u32[]{:S(2)}) copy-start(f32[28800]{0:T(1024)} %param.43) | copy-start | bytes 345604
  128.1 1.4 %copy-start.8 = (f32[28800]{0:T(1024)S(1)}, f32[28800]{0:T(1024)}, u32[]{:S(2)}) copy-start(f32[28800]{0:T(1024)} %param.50) | copy-start | bytes 345604
  128.1 1.4 %copy-start.9 = (f32[28800]{0:T(1024)S(1)}, f32[28800]{0:T(1024)}, u32[]{:S(2)}) copy-start(f32[28800]{0:T(1024)} %param.49) | copy-start | bytes 345604
  128.1 1.4 %copy-start.10 = (f32[28800]{0:T(1024)S(1)}, f32[28800]{0:T(1024)}, u32[]{:S(2)}) copy-start(f32[28800]{0:T(1024)} %param.48) | copy-start | bytes 345604
  128.1 1.4 %copy-start.11 = (f32[28800]{0:T(1024)S(1)}, f32[28800]{0:T(1024)}, u32[]{:S(2)}) copy-start(f32[28800]{0:T(1024)} %param.45) | copy-start | bytes 345604
  128.1 1.4 %copy-start.12 = (f32[28800]{0:T(1024)S(1)}, f32[28800]{0:T(1024)}, u32[]{:S(2)}) copy-start(f32[28800]{0:T(1024)} %param.44) | copy-start | bytes 345604
  129.5 1.5 %copy-start.1 = (f32[480,512]{1,0:T(8,128)S(1)}, f32[480,512]{1,0:T(8,128)}, u32[]{:S(2)}) copy-start(f32[480,512]{1,0:T(8,128)} %get-tuple-element.26) | copy-start | bytes 2949124
  131.0 1.6 %copy-start = (f32[480,512]{1,0:T(8,128)S(1)}, f32[480,512]{1,0:T(8,128)}, u32[]{:S(2)}) copy-start(f32[480,512]{1,0:T(8,128)} %get-tuple-element.27) | copy-start | bytes 2949124

commit v4 on v3

--- a/solution.py
+++ b/solution.py
@@ -63,7 +63,7 @@
     return (low(squeeze), low(squeeze.T), jnp.asarray(cosine), jnp.asarray(first), jnp.asarray(second))
 
 
-UP, DOWN, EARLY = (0, 1, 2), (3, 4, 5), (6, 7, 8)
+UP, DOWN, EARLY, OUT = (0, 1, 2), (3, 4, 5), (6, 7, 8), (9, 10)
 WAY_A, WAY_B, WAY_C = (0, 1, 3, 2, 4), (0, 1, 2, 3, 4), (2, 3, 0, 1, 4)
 GATHER_ROUTES = (
     (0, 8, WAY_A), (8, 8, WAY_B), (16, 3, WAY_C),
@@ -72,11 +72,12 @@
 )
 SCATTER_ROUTES = (
     (0, 6, WAY_A), (6, 6, WAY_B), (12, 3, WAY_C),
-    (15, 8, WAY_A), (23, 8, WAY_B), (31, 4, WAY_C),
+    (19, 6, WAY_A), (25, 7, WAY_B), (32, 3, WAY_C),
     (35, 5, WAY_A), (40, 5, WAY_B), (45, 2, WAY_C),
+    (15, 2, WAY_A), (17, 2, WAY_B),
 )
 GATHER_AT = ((1, DOWN, 1), (3, UP, 3), (5, DOWN, 2), (10, UP, 4), (11, DOWN, 3), (18, DOWN, 4))
-SCATTER_AT = ((3, UP, 2), (4, DOWN, 1), (8, UP, 3), (10, DOWN, 2), (11, UP, 4), (14, DOWN, 3), (17, DOWN, 4))
+SCATTER_AT = ((2, OUT, 1), (5, UP, 2), (11, DOWN, 2), (13, OUT, 2), (14, UP, 3), (16, DOWN, 3), (17, OUT, 3), (18, UP, 4))
 
 
 class Links:
@@ -254,10 +255,10 @@
     layer_out, tokens_grad, G_out, norm_out = refs[12:16]
     (
         up_s, down_s, qkv_s, dj_s, out_s, q_s, k_s, v_s, kT_s, vT_s, P_s, OT_s, att_s, dA_s, dqT_s, dk_s, dv_s,
-        act1_s, act2_s, act_pad, plain1, plain2, res_s, y_s, dn_s, dres_s, dlow_s, eye_s, x_s, centre_s, ds_s, act_pad1,
-    ) = refs[16:48]
-    if remote:
-        links = Links(source, G_out, norm_out, *refs[48:])
+        act1_s, act2_s, act_pad, plain1, plain2, res_s, y_s, dn_s, dres_s, dlow_s, eye_s, x_s, centre_s, ds_s, act_pad1, norm_s, rows_s, read_sem,
+    ) = refs[16:51]
+    if remote:
+        links = Links(source, G_out, norm_out, *refs[51:])
         W, G = links.whole, links.parts
         links.greet()
         links.keep_own()
@@ -271,7 +272,9 @@
 
     lane = lax.broadcasted_iota(jnp.int32, (1, WIDE), 1)
     real = jnp.where(lane < D, 1.0, 0.0)
-    gains = norm[...]
+    norm_s[...] = jnp.zeros_like(norm_s)
+    norm_s[:4, :D] = norm[...]
+    gains = norm_s[...]
 
     def norm_rows(values, gain, shift):
         middle = jnp.sum(values, axis=-1, keepdims=True) * (1.0 / D)
@@ -289,10 +292,15 @@
         two = jnp.sum(scaled * plain, axis=-1, keepdims=True) * (1.0 / D)
         return inverse * (scaled - one - plain * two) * real, dg, db
 
+    reads = [pltpu.make_async_copy(ref, rows_s.at[k], read_sem.at[k]) for k, ref in enumerate((tok, cot))]
+    for read in reads:
+        read.start()
     x_s[...] = jnp.zeros_like(x_s)
-    x_s[:D, :] = tok[...].astype(f32)
     dres_s[...] = jnp.zeros_like(dres_s)
-    dres_s[:D, :] = cot[...].astype(f32)
+    for read in reads:
+        read.wait()
+    x_s[:D, :] = rows_s[0].astype(f32)
+    dres_s[:D, :] = rows_s[1].astype(f32)
     x_s[...] = x_s[...].T
     normed, plain, inverse1 = norm_rows(x_s[...], gains[0:1], gains[1:2])
     plain1[...] = plain
@@ -446,12 +454,16 @@
         return carry
 
     lax.fori_loop(0, NDP, down_groups, 0)
+    if remote:
+        links.scatter_step(DOWN, 0)
 
     d_from, dg2, db2 = norm_back(dn_s[...], plain2[...], inverse2, gains[2:3])
     d_res = dres_s[...] + d_from
     dres_s[...] = d_res
     dlow_s[...] = d_res.astype(bf16)
 
+    if remote:
+        links.scatter_step(UP, 1)
     for t in range(NTEN):
         dA_s[t] = mm_nt(dlow_s[...], out_s[t]).astype(bf16)
         dAT = mm_nt(out_s[t], dlow_s[...]).astype(bf16).astype(f32)
@@ -464,8 +476,8 @@
         for c in range(4):
             G[mine + (OUT0 + c,)] = part[:, c * LANES : (c + 1) * LANES].reshape(2, 2, 2, 16, LANES)
     if remote:
-        links.scatter_step(DOWN, 0)
-        links.scatter_step(UP, 1)
+        links.scatter_step(OUT, 0)
+        links.scatter_step(DOWN, 1)
 
     dk_s[...] = jnp.zeros_like(dk_s)
     dv_s[...] = jnp.zeros_like(dv_s)
@@ -510,7 +522,8 @@
     if remote:
         links.scatter_step(EARLY, 0)
         links.scatter_step(UP, 5)
-        links.scatter_step(DOWN, 5)
+        links.scatter_step(DOWN, 4)
+        links.scatter_step(OUT, 4)
     dz = mm_nt(dj_s[...], qkv_s[...])
     d_from, dg1, db1 = norm_back(dz, plain1[...], inverse1, gains[0:1])
     norm_parts = jnp.concatenate([dg1, db1, dg2, db2, jnp.zeros((4, WIDE), f32)], 0)
@@ -523,6 +536,8 @@
     tokens_grad[...] = x_s[:D, :]
     if remote:
         links.norm_step(0)
+        links.scatter_step(DOWN, 5)
+        links.scatter_step(OUT, 5)
         links.scatter_step(EARLY, 2)
         links.norm_step(1)
         links.scatter_step(EARLY, 3)
@@ -534,9 +549,9 @@
 
 def run_layer(lengths, clusters, cluster_weight, source, tokens, cotangent, norm_master, remote):
     rows = MAXLEN
-    wide_norm = jnp.pad(norm_master, ((0, 0), (0, WIDE - D)))
     smem = pl.BlockSpec(memory_space=pltpu.SMEM)
     vmem = pl.BlockSpec(memory_space=pltpu.VMEM)
+    hbm = pl.BlockSpec(memory_space=pl.ANY)
     head_set = (NTEN, MAXLEN, LANES)
     turned = (NTEN, HEADS_DEV * 32, MAXLEN)
     wide = (rows, WIDE)
@@ -573,6 +588,9 @@
         pltpu.VMEM((NTEN, 8, MAXLEN), f32),
         pltpu.VMEM((MAXLEN, MAXLEN), bf16),
         pltpu.VMEM(wide, bf16),
+        pltpu.VMEM((8, WIDE), f32),
+        pltpu.VMEM((2, D, MAXLEN), bf16),
+        pltpu.SemaphoreType.DMA((2,)),
     ]
     tiles = (TILES, 16, LANES)
     params = dict(vmem_limit_bytes=66_900_000)
@@ -591,12 +609,12 @@
             result,
             jax.ShapeDtypeStruct((8, WIDE), f32),
         ),
-        in_specs=[smem] * 3 + [vmem] * 9,
+        in_specs=[smem] * 3 + [vmem, hbm, hbm] + [vmem] * 6,
         out_specs=[vmem] * 4,
         scratch_shapes=scratch,
         compiler_params=pltpu.CompilerParams(**params),
         name="layer",
-    )(lengths, clusters, cluster_weight, source, tokens.T, cotangent.T, wide_norm, *constants())
+    )(lengths, clusters, cluster_weight, source, tokens.T, cotangent.T, norm_master, *constants())
     if not remote:
         grads = grads.reshape(NDP, NTEN, *tiles)
     return turned_out.T, turned_grad.T, grads, norm_grad

time: 134 us -> 128 us (0.955)
  Pallas kernels: 116 us -> 112 us
    pallas_call x1, Pallas kernels: 116 us -> 112 us  [run_layer(): pl.pallas_call(functools.partial(layer_kernel, remote), out_shape=(jax.Sh...]
where the time goes in v4:
time: 128 us
  Pallas kernels  112 us (88%)
  local copies, waits for them, and re-layouts  7.77 us (6%)
  other arithmetic  7.1 us (6%)
    pallas_call x1, Pallas kernels, run_layer(): pl.pallas_call(functools.partial(layer_kernel, remote), out_shape=(jax.Sh...  112 us
    unnamed x46, local copies, waits for them, and re-layouts  5.67 us
    add x4, other arithmetic, adam_step(): average_new = average_keep * average + (1.0 - average_keep) * fresh  5.29 us

profile of v4, /device:TPU:0, one launch (start us, length us, event | category | flops | bytes accessed | tf_op | source)
XLA Modules:
  0.0 127.5 jit_solution(18001869207023121260)
XLA Ops:
  0.7 0.0 copy-start.6
  0.7 0.9 convert_reduce_fusion.1
  1.5 0.1 reshape.149
  1.6 0.0 copy-done.6
  1.7 0.2 convert_reduce_fusion
  1.9 0.1 reshape.154
  2.0 0.0 copy-start.3
  2.1 0.8 copy-done.3
  3.0 0.0 copy-start.2
  3.1 0.8 copy-done.2
  3.9 0.1 reshape.151
  4.1 0.7 pad_maximum_fusion.refs_3_
  4.8 0.0 copy-start.18
  4.8 0.0 copy-start.19
  4.8 111.6 %layer.1 = (f32[480,512]{1,0:T(8,128)}, f32[480,512]{1,0:T(8,128)}, f32[47,16,128]{2,1,0:T(8,128)}, f32[8,512]{1,0:T(8,128)}) custom-call(s32[4]{0:T(128)} %refs_0_.1, s32[4]{0:T(128)} %refs_1_.1, f32[64]{0:T(128)} %refs_2_.1, bf16[47,16,128]{2,1,0:T(8,128)(2,1)} %pad_maximum_fusion.refs_3_, bf16[480,512]{1,0:T(8,128)(2,1)} %bitcast.47, ...), custom_call_target="tpu_custom_call" | custom-call | tf_op jit(solution)/shard_map/layer/pallas_call | solution.py:604
  116.4 0.0 copy-start.5
  116.4 0.8 slice_bitcast_fusion.1
  117.3 0.1 reshape.159
  117.4 0.0 copy-done.18
  117.4 0.0 copy-done.19
  117.4 0.0 copy-start.14
  117.5 1.4 %multiply_add_fusion.9 = (f32[4,480]{1,0:T(4,128)}, f32[4,480]{1,0:T(4,128)}, f32[4,480]{1,0:T(4,128)}, f32[4,480]{1,0:T(4,128)}) fusion(f32[4,480]{1,0:T(4,128)S(1)} %copy-done.19, f32[4,480]{1,0:T(4,128)S(1)} %copy-done.18, f32[8,512]{1,0:T(8,128)} %get-tuple-element.29, f32[4,480]{1,0:T(4,128)} %param.53, f32[4,480]{1,0:T(4,128)} %param.52), kind=kLoop, calls=%fused_computation.34 | loop fusion | flops 28800 | bytes 69120 | tf_op jit(solution)/shard_map/add | solution.py:647
  118.8 0.0 copy-done.14
  118.8 1.6 %multiply_add_fusion.7 = (f32[1,7200]{1,0:T(1,128)}, f32[1,7200]{1,0:T(1,128)}, f32[1,7200]{1,0:T(1,128)}, f32[1,7200]{1,0:T(1,128)}) fusion(f32[1,7200]{1,0:T(1,128)} %param.42, f32[1,7200]{1,0:T(1,128)S(1)} %copy-done.14, f32[1,7200]{1,0:T(1,128)S(1)} %reshape.159, f32[1,7200]{1,0:T(1,128)} %param.41, f32[1,7200]{1,0:T(1,128)} %param.40), kind=kLoop, calls=%fused_computation.26 | loop fusion | flops 108000 | bytes 259200 | tf_op jit(solution)/shard_map/add | solution.py:647
  120.4 0.0 copy-done.5
  120.5 0.1 copy.69
  120.6 0.2 reshape.157
  120.8 0.1 copy.68
  121.0 0.0 copy-start.15
  121.0 0.0 copy-start.16
  121.1 0.0 copy-start.17
  121.1 0.0 copy-start.7
  121.1 0.0 copy-start.13
  121.1 0.1 reshape.163
  121.2 0.7 copy-done.15
  121.9 0.0 copy-done.16
  122.0 0.0 copy-done.17
  122.0 0.0 copy-done.7
  122.1 0.0 copy-start.4
  122.1 0.0 copy-start.8
  122.1 0.0 copy-start.9
  122.1 0.0 copy-start.10
  122.1 0.0 copy-start.11
  122.1 0.0 copy-start.12
  122.1 1.3 %multiply_add_fusion.5 = (f32[1,21600]{1,0:T(1,128)}, f32[1,21600]{1,0:T(1,128)}, f32[1,21600]{1,0:T(1,128)}, f32[1,21600]{1,0:T(1,128)}) fusion(f32[1,21600]{1,0:T(1,128)S(1)} %copy-done.15, f32[1,21600]{1,0:T(1,128)S(1)} %copy-done.7, f32[1,21600]{1,0:T(1,128)S(1)} %reshape.157, f32[1,21600]{1,0:T(1,128)S(1)} %copy-done.16, f32[1,21600]{1,0:T(1,128)S(1)} %copy-done.17), kind=kLoop, calls=%fused_computation.17 | loop fusion | flops 324000 | bytes 777600 | tf_op jit(solution)/shard_map/add | solution.py:647
  123.4 0.0 copy-done.13
  123.4 0.0 copy-done.4
  123.4 0.0 copy-done.8
  123.4 0.0 copy-done.9
  123.4 0.0 copy-done.10
  123.4 0.0 copy-done.11
  123.5 0.0 copy-done.12
  123.5 0.0 copy-start.1
  123.5 1.0 multiply_add_fusion.2
  124.5 0.6 copy-done.1
  125.0 0.0 copy-start
  125.0 0.9 copy.72
  126.0 0.6 copy-done
  126.6 0.9 copy.73
  (23 shorter events, 0.4 us)
Async XLA Ops:
  0.7 1.0 copy-start.6
  2.0 0.9 copy-start.3
  3.0 0.9 copy-start.2
  4.8 112.6 %copy-start.18 = (f32[4,480]{1,0:T(4,128)S(1)}, f32[4,480]{1,0:T(4,128)}, u32[]{:S(2)}) copy-start(f32[4,480]{1,0:T(4,128)} %refs_6_.1) | copy-start | bytes 23044
  4.8 112.6 %copy-start.19 = (f32[4,480]{1,0:T(4,128)S(1)}, f32[4,480]{1,0:T(4,128)}, u32[]{:S(2)}) copy-start(f32[4,480]{1,0:T(4,128)} %param.54) | copy-start | bytes 23044
  116.4 4.0 %copy-start.5 = (f32[47,16,128]{2,1,0:T(8,128)S(1)}, f32[47,16,128]{2,1,0:T(8,128)}, u32[]{:S(2)}) copy-start(f32[47,16,128]{2,1,0:T(8,128)} %get-tuple-element.28) | copy-start | bytes 1155076
  117.4 1.4 %copy-start.14 = (f32[1,7200]{1,0:T(1,128)S(1)}, f32[1,7200]{1,0:T(1,128)}, u32[]{:S(2)}) copy-start(f32[1,7200]{1,0:T(1,128)} %param.39) | copy-start | bytes 86404
  121.0 0.9 copy-start.15
  121.0 0.9 copy-start.16
  121.1 1.0 copy-start.17
  121.1 1.0 copy-start.7
  121.1 2.3 %copy-start.13 = (f32[28800]{0:T(1024)S(1)}, f32[28800]{0:T(1024)}, u32[]{:S(2)}) copy-start(f32[28800]{0:T(1024)} %param.46) | copy-start | bytes 345604
  122.1 1.4 %copy-start.4 = (f32[28800]{0:T(1024)S(1)}, f32[28800]{0:T(1024)}, u32[]{:S(2)}) copy-start(f32[28800]{0:T(1024)} %param.43) | copy-start | bytes 345604
  122.1 1.4 %copy-start.8 = (f32[28800]{0:T(1024)S(1)}, f32[28800]{0:T(1024)}, u32[]{:S(2)}) copy-start(f32[28800]{0:T(1024)} %param.50) | copy-start | bytes 345604
  122.1 1.4 %copy-start.9 = (f32[28800]{0:T(1024)S(1)}, f32[28800]{0:T(1024)}, u32[]{:S(2)}) copy-start(f32[28800]{0:T(1024)} %param.49) | copy-start | bytes 345604
  122.1 1.4 %copy-start.10 = (f32[28800]{0:T(1024)S(1)}, f32[28800]{0:T(1024)}, u32[]{:S(2)}) copy-start(f32[28800]{0:T(1024)} %param.48) | copy-start | bytes 345604
  122.1 1.4 %copy-start.11 = (f32[28800]{0:T(1024)S(1)}, f32[28800]{0:T(1024)}, u32[]{:S(2)}) copy-start(f32[28800]{0:T(1024)} %param.45) | copy-start | bytes 345604
  122.1 1.4 %copy-start.12 = (f32[28800]{0:T(1024)S(1)}, f32[28800]{0:T(1024)}, u32[]{:S(2)}) copy-start(f32[28800]{0:T(1024)} %param.44) | copy-start | bytes 345604
  123.5 1.5 %copy-start.1 = (f32[480,512]{1,0:T(8,128)S(1)}, f32[480,512]{1,0:T(8,128)}, u32[]{:S(2)}) copy-start(f32[480,512]{1,0:T(8,128)} %get-tuple-element.26) | copy-start | bytes 2949124
  125.0 1.6 %copy-start = (f32[480,512]{1,0:T(8,128)S(1)}, f32[480,512]{1,0:T(8,128)}, u32[]{:S(2)}) copy-start(f32[480,512]{1,0:T(8,128)} %get-tuple-element.27) | copy-start | bytes 2949124

commit v5 on v4

--- a/solution.py
+++ b/solution.py
@@ -53,27 +53,26 @@
     lane = np.arange(120)
     place = lane % HEAD
     cosine = np.zeros((MAXLEN, LANES), np.float32)
-    first = np.zeros((MAXLEN, LANES), np.float32)
-    second = np.zeros((MAXLEN, LANES), np.float32)
+    signed = np.zeros((MAXLEN, LANES), np.float32)
     cosine[:, :120] = np.cos(angle)[:, place % 12]
-    sines = np.sin(angle)[:, place % 12]
-    first[:, :120] = np.where(place < 12, -sines, 0.0)
-    second[:, :120] = np.where(place >= 12, sines, 0.0)
+    signed[:, :120] = np.sin(angle)[:, place % 12] * np.where(place < 12, -1.0, 1.0)
     low = lambda v: jnp.asarray(v.astype(jnp.bfloat16))
-    return (low(squeeze), low(squeeze.T), jnp.asarray(cosine), jnp.asarray(first), jnp.asarray(second))
-
-
-UP, DOWN, EARLY, OUT = (0, 1, 2), (3, 4, 5), (6, 7, 8), (9, 10)
+    return (low(squeeze), jnp.asarray(cosine), jnp.asarray(signed))
+
+
+UP, DOWN, EARLY, VALUES, OUT = (0, 1, 2), (3, 4, 5), (6, 7, 8), (9, 10), (11, 12)
 WAY_A, WAY_B, WAY_C = (0, 1, 3, 2, 4), (0, 1, 2, 3, 4), (2, 3, 0, 1, 4)
 GATHER_ROUTES = (
     (0, 8, WAY_A), (8, 8, WAY_B), (16, 3, WAY_C),
     (19, 6, WAY_A), (25, 7, WAY_B), (32, 3, WAY_C),
-    (35, 5, WAY_A), (40, 5, WAY_B), (45, 2, WAY_C),
+    (35, 3, WAY_A), (38, 3, WAY_B), (41, 2, WAY_C),
+    (43, 2, WAY_A), (45, 2, WAY_B),
 )
 SCATTER_ROUTES = (
     (0, 6, WAY_A), (6, 6, WAY_B), (12, 3, WAY_C),
     (19, 6, WAY_A), (25, 7, WAY_B), (32, 3, WAY_C),
-    (35, 5, WAY_A), (40, 5, WAY_B), (45, 2, WAY_C),
+    (35, 3, WAY_A), (38, 3, WAY_B), (41, 2, WAY_C),
+    (43, 2, WAY_A), (45, 2, WAY_B),
     (15, 2, WAY_A), (17, 2, WAY_B),
 )
 GATHER_AT = ((1, DOWN, 1), (3, UP, 3), (5, DOWN, 2), (10, UP, 4), (11, DOWN, 3), (18, DOWN, 4))
@@ -251,18 +250,20 @@
 
 
 def layer_kernel(remote, *refs):
-    lengths, clusters, weights_of, source, tok, cot, norm, squeeze, widen, cosine, first, second = refs[:12]
-    layer_out, tokens_grad, G_out, norm_out = refs[12:16]
+    lengths, clusters, weights_of, source, tok, cot, norm, *tables = refs[:10]
+    layer_out, tokens_grad, G_out, norm_out = refs[10:14]
     (
         up_s, down_s, qkv_s, dj_s, out_s, q_s, k_s, v_s, kT_s, vT_s, P_s, OT_s, att_s, dA_s, dqT_s, dk_s, dv_s,
         act1_s, act2_s, act_pad, plain1, plain2, res_s, y_s, dn_s, dres_s, dlow_s, eye_s, x_s, centre_s, ds_s, act_pad1, norm_s, rows_s, read_sem,
-    ) = refs[16:51]
-    if remote:
-        links = Links(source, G_out, norm_out, *refs[51:])
+        widen, squeeze, cosine, signed,
+    ) = refs[14:53]
+    if remote:
+        links = Links(source, G_out, norm_out, *refs[53:])
         W, G = links.whole, links.parts
         links.greet()
         links.keep_own()
         links.gather_step(EARLY, 0)
+        links.gather_step(VALUES, 0)
     else:
         links, W, G = None, source, G_out
     me = lax.axis_index("tensor")
@@ -292,7 +293,8 @@
         two = jnp.sum(scaled * plain, axis=-1, keepdims=True) * (1.0 / D)
         return inverse * (scaled - one - plain * two) * real, dg, db
 
-    reads = [pltpu.make_async_copy(ref, rows_s.at[k], read_sem.at[k]) for k, ref in enumerate((tok, cot))]
+    places = (rows_s.at[0], rows_s.at[1], squeeze, cosine, signed)
+    reads = [pltpu.make_async_copy(ref, to, read_sem.at[k]) for k, (ref, to) in enumerate(zip((tok, cot, *tables), places))]
     for read in reads:
         read.start()
     x_s[...] = jnp.zeros_like(x_s)
@@ -300,6 +302,7 @@
     for read in reads:
         read.wait()
     x_s[:D, :] = rows_s[0].astype(f32)
+    widen[...] = squeeze[...].astype(f32).T.astype(bf16)
     dres_s[:D, :] = rows_s[1].astype(f32)
     x_s[...] = x_s[...].T
     normed, plain, inverse1 = norm_rows(x_s[...], gains[0:1], gains[1:2])
@@ -307,6 +310,7 @@
     act1_s[...] = normed.astype(bf16)
     if remote:
         links.gather_step(EARLY, 1)
+        links.gather_step(VALUES, 1)
     row = lax.broadcasted_iota(jnp.int32, (MAXLEN, 1), 0)
     row_scale = jnp.where(row < length, scale_row, 0.0)
     dres_s[...] = dres_s[...].T * row_scale
@@ -314,23 +318,33 @@
     act_pad1[...] = mm_nt(widen[...], act1_s[...]).astype(bf16)
     if remote:
         links.gather_step(EARLY, 2)
+        links.gather_step(VALUES, 2)
         links.gather_step(UP, 0)
         links.gather_step(EARLY, 3)
+        links.gather_step(VALUES, 3)
         links.gather_step(EARLY, 4)
+        links.gather_step(VALUES, 4)
         links.gather_step(UP, 1)
         links.gather_step(EARLY, 5)
         links.gather_step(UP, 2)
         links.gather_step(DOWN, 0)
 
-    for pair in range(2):
+    def joined_third(c):
         pieces = []
-        for t in (2 * pair, 2 * pair + 1):
+        for t in range(NTEN):
             mine = (slice(None),) * 3 + (t // 2, t % 2)
-            pieces += [W[mine + (slice(QKV0 + 4 * c, QKV0 + 4 * c + 4),)].reshape(WIDE, LANES) for c in range(3)]
-        half = slice(pair * (JOINED // 2), (pair + 1) * (JOINED // 2))
-        qkv_s[:, half] = mm(squeeze[...], jnp.concatenate(pieces, 1)).astype(bf16)
-    cosv, firstv, secondv = cosine[...], first[...], second[...]
+            pieces.append(W[mine + (slice(QKV0 + 4 * c, QKV0 + 4 * c + 4),)].reshape(WIDE, LANES))
+        third = slice(c * WIDE, (c + 1) * WIDE)
+        qkv_s[:, third] = mm(squeeze[...], jnp.concatenate(pieces, 1)).astype(bf16)
+        return mm(act1_s[...], qkv_s[:, third])
+
+    cosv, signv = cosine[...], signed[...]
     lane_id = lax.broadcasted_iota(jnp.int32, (1, LANES), 1)
+    ahead = functools.reduce(jnp.logical_or, [(lane_id >= j * HEAD) & (lane_id < j * HEAD + HEAD // 2) for j in range(HEADS_DEV)])
+
+    def partners(u):
+        return jnp.where(ahead, pltpu.roll(u, LANES - HEAD // 2, 1), pltpu.roll(u, HEAD // 2, 1))
+
     key_id = lax.broadcasted_iota(jnp.int32, (MAXLEN, 1), 0)
     spare = jnp.where(lane_id == SPARE, 1.0, 0.0)
     key_bias = jnp.where(key_id < length, 0.0, hidden_score) * spare
@@ -343,22 +357,25 @@
         rows = [block[j * 32 : j * 32 + HEAD] for j in range(HEADS_DEV)]
         return jnp.concatenate(rows + [jnp.zeros((8, MAXLEN), f32)], 0)
 
-    for t in range(NTEN):
-        if t % 2 == 0:
-            both = mm(act1_s[...], qkv_s[:, t * 3 * LANES : (t + 2) * 3 * LANES])
-        joined = both[:, (t % 2) * 3 * LANES : (t % 2 + 1) * 3 * LANES]
-        for number in range(2):
-            u = joined[:, number * LANES : (number + 1) * LANES]
-            r = u * cosv + pltpu.roll(u, LANES - 12, 1) * firstv + pltpu.roll(u, 12, 1) * secondv
+    for number in range(2):
+        joined = joined_third(number)
+        for t in range(NTEN):
+            u = joined[:, t * LANES : (t + 1) * LANES]
+            r = u * cosv + partners(u) * signv
             if number == 0:
                 q_s[t] = (r + spare).astype(bf16)
             else:
                 k_s[t] = (r + key_bias).astype(bf16)
                 kT_s[t] = strided(r.T).astype(bf16)
-        v = joined[:, 2 * LANES :]
+    if remote:
+        links.gather_step(VALUES, 5)
+    joined = joined_third(2)
+    for t in range(NTEN):
+        v = joined[:, t * LANES : (t + 1) * LANES]
         v_s[t] = v.astype(bf16)
         vT_s[t] = strided(v.T).astype(bf16)
 
+    OT_s[...] = jnp.zeros_like(OT_s)
     fold = HEAD ** -0.5 * 1.4426950408889634
 
     def forward_head(h, carry):
@@ -506,21 +523,26 @@
 
     lax.fori_loop(0, NTEN * HEADS_DEV, backward_head, 0)
 
+    def scatter_third(c):
+        part = mm(act_pad1[...], dj_s[:, c * WIDE : (c + 1) * WIDE]).astype(bf16)
+        for t in range(NTEN):
+            where = (slice(None),) * 3 + (t // 2, t % 2) + (slice(QKV0 + 4 * c, QKV0 + 4 * c + 4),)
+            G[where] = part[:, t * LANES : (t + 1) * LANES].reshape(2, 2, 2, 4, 16, LANES)
+
     for t in range(NTEN):
-        first_lane = t * 3 * LANES
-        for number in range(2):
+        dj_s[:, 2 * WIDE + t * LANES : 2 * WIDE + (t + 1) * LANES] = dv_s[t].astype(bf16)
+    scatter_third(2)
+    if remote:
+        links.scatter_step(VALUES, 0)
+    for number in (1, 0):
+        for t in range(NTEN):
             g = (dense(dqT_s[t]).T if number == 0 else dk_s[t]) * scale
-            r = g * cosv - pltpu.roll(g, LANES - 12, 1) * firstv - pltpu.roll(g, 12, 1) * secondv
-            dj_s[:, first_lane + number * LANES : first_lane + (number + 1) * LANES] = r.astype(bf16)
-        dj_s[:, first_lane + 2 * LANES : first_lane + 3 * LANES] = dv_s[t].astype(bf16)
-    for pair in range(2):
-        part = mm(act_pad1[...], dj_s[:, pair * (JOINED // 2) : (pair + 1) * (JOINED // 2)]).astype(bf16)
-        for number in range(6):
-            t, c = 2 * pair + number // 3, number % 3
-            where = (slice(None),) * 3 + (t // 2, t % 2) + (slice(QKV0 + 4 * c, QKV0 + 4 * c + 4),)
-            G[where] = part[:, number * LANES : (number + 1) * LANES].reshape(2, 2, 2, 4, 16, LANES)
+            r = g * cosv - partners(g) * signv
+            dj_s[:, number * WIDE + t * LANES : number * WIDE + (t + 1) * LANES] = r.astype(bf16)
+        scatter_third(number)
     if remote:
         links.scatter_step(EARLY, 0)
+        links.scatter_step(VALUES, 1)
         links.scatter_step(UP, 5)
         links.scatter_step(DOWN, 4)
         links.scatter_step(OUT, 4)
@@ -538,11 +560,15 @@
         links.norm_step(0)
         links.scatter_step(DOWN, 5)
         links.scatter_step(OUT, 5)
+        links.scatter_step(VALUES, 2)
         links.scatter_step(EARLY, 2)
         links.norm_step(1)
+        links.scatter_step(VALUES, 3)
         links.scatter_step(EARLY, 3)
         links.norm_step(2)
+        links.scatter_step(VALUES, 4)
         links.scatter_step(EARLY, 4)
+        links.scatter_step(VALUES, 5)
         links.scatter_step(EARLY, 5)
         links.finish()
 
@@ -590,7 +616,11 @@
         pltpu.VMEM(wide, bf16),
         pltpu.VMEM((8, WIDE), f32),
         pltpu.VMEM((2, D, MAXLEN), bf16),
-        pltpu.SemaphoreType.DMA((2,)),
+        pltpu.SemaphoreType.DMA((5,)),
+        pltpu.VMEM((WIDE, WIDE), bf16),
+        pltpu.VMEM((WIDE, WIDE), bf16),
+        pltpu.VMEM((MAXLEN, LANES), f32),
+        pltpu.VMEM((MAXLEN, LANES), f32),
     ]
     tiles = (TILES, 16, LANES)
     params = dict(vmem_limit_bytes=66_900_000)
@@ -609,7 +639,7 @@
             result,
             jax.ShapeDtypeStruct((8, WIDE), f32),
         ),
-        in_specs=[smem] * 3 + [vmem, hbm, hbm] + [vmem] * 6,
+        in_specs=[smem] * 3 + [vmem, hbm, hbm, vmem] + [hbm] * 3,
         out_specs=[vmem] * 4,
         scratch_shapes=scratch,
         compiler_params=pltpu.CompilerParams(**params),

time: 128 us -> 127 us (level)
  no operation moved by 1% of the time
where the time goes in v5:
time: 127 us
  Pallas kernels  111 us (87%)
  local copies, waits for them, and re-layouts  7.77 us (6%)
  other arithmetic  7.1 us (6%)
    pallas_call x1, Pallas kernels, run_layer(): pl.pallas_call(functools.partial(layer_kernel, remote), out_shape=(jax.Sh...  111 us
    unnamed x46, local copies, waits for them, and re-layouts  5.67 us
    add x4, other arithmetic, adam_step(): average_new = average_keep * average + (1.0 - average_keep) * fresh  5.29 us

profile of v5, /device:TPU:0, one launch (start us, length us, event | category | flops | bytes accessed | tf_op | source)
XLA Modules:
  0.0 126.7 jit_solution(16104340721226052758)
XLA Ops:
  0.7 0.0 copy-start.6
  0.7 0.9 convert_reduce_fusion.1
  1.5 0.1 reshape.149
  1.6 0.0 copy-done.6
  1.7 0.2 convert_reduce_fusion
  1.9 0.1 reshape.154
  2.0 0.0 copy-start.3
  2.1 0.8 copy-done.3
  3.0 0.0 copy-start.2
  3.1 0.8 copy-done.2
  3.9 0.1 reshape.151
  4.1 0.7 pad_maximum_fusion.refs_3_
  4.8 0.0 copy-start.18
  4.8 0.0 copy-start.19
  4.8 110.8 %layer.1 = (f32[480,512]{1,0:T(8,128)}, f32[480,512]{1,0:T(8,128)}, f32[47,16,128]{2,1,0:T(8,128)}, f32[8,512]{1,0:T(8,128)}) custom-call(s32[4]{0:T(128)} %refs_0_.1, s32[4]{0:T(128)} %refs_1_.1, f32[64]{0:T(128)} %refs_2_.1, bf16[47,16,128]{2,1,0:T(8,128)(2,1)} %pad_maximum_fusion.refs_3_, bf16[480,512]{1,0:T(8,128)(2,1)} %bitcast.47, ...), custom_call_target="tpu_custom_call" | custom-call | tf_op jit(solution)/shard_map/layer/pallas_call | solution.py:634
  115.6 0.0 copy-start.5
  115.6 0.8 slice_bitcast_fusion.1
  116.5 0.1 reshape.159
  116.6 0.0 copy-done.18
  116.6 0.0 copy-done.19
  116.6 0.0 copy-start.14
  116.6 1.4 %multiply_add_fusion.9 = (f32[4,480]{1,0:T(4,128)}, f32[4,480]{1,0:T(4,128)}, f32[4,480]{1,0:T(4,128)}, f32[4,480]{1,0:T(4,128)}) fusion(f32[4,480]{1,0:T(4,128)S(1)} %copy-done.19, f32[4,480]{1,0:T(4,128)S(1)} %copy-done.18, f32[8,512]{1,0:T(8,128)} %get-tuple-element.29, f32[4,480]{1,0:T(4,128)} %param.51, f32[4,480]{1,0:T(4,128)} %param.50), kind=kLoop, calls=%fused_computation.34 | loop fusion | flops 28800 | bytes 69120 | tf_op jit(solution)/shard_map/add | solution.py:677
  118.0 0.0 copy-done.14
  118.0 1.6 %multiply_add_fusion.7 = (f32[1,7200]{1,0:T(1,128)}, f32[1,7200]{1,0:T(1,128)}, f32[1,7200]{1,0:T(1,128)}, f32[1,7200]{1,0:T(1,128)}) fusion(f32[1,7200]{1,0:T(1,128)} %param.40, f32[1,7200]{1,0:T(1,128)S(1)} %copy-done.14, f32[1,7200]{1,0:T(1,128)S(1)} %reshape.159, f32[1,7200]{1,0:T(1,128)} %param.39, f32[1,7200]{1,0:T(1,128)} %param.38), kind=kLoop, calls=%fused_computation.26 | loop fusion | flops 108000 | bytes 259200 | tf_op jit(solution)/shard_map/add | solution.py:677
  119.6 0.0 copy-done.5
  119.6 0.1 copy.67
  119.8 0.2 reshape.157
  120.0 0.1 copy.66
  120.2 0.0 copy-start.15
  120.2 0.0 copy-start.16
  120.2 0.0 copy-start.17
  120.3 0.0 copy-start.7
  120.3 0.0 copy-start.13
  120.3 0.1 reshape.163
  120.4 0.7 copy-done.15
  121.1 0.0 copy-done.16
  121.2 0.0 copy-done.17
  121.2 0.0 copy-done.7
  121.2 0.0 copy-start.4
  121.3 0.0 copy-start.8
  121.3 0.0 copy-start.9
  121.3 0.0 copy-start.10
  121.3 0.0 copy-start.11
  121.3 0.0 copy-start.12
  121.3 1.3 %multiply_add_fusion.5 = (f32[1,21600]{1,0:T(1,128)}, f32[1,21600]{1,0:T(1,128)}, f32[1,21600]{1,0:T(1,128)}, f32[1,21600]{1,0:T(1,128)}) fusion(f32[1,21600]{1,0:T(1,128)S(1)} %copy-done.15, f32[1,21600]{1,0:T(1,128)S(1)} %copy-done.7, f32[1,21600]{1,0:T(1,128)S(1)} %reshape.157, f32[1,21600]{1,0:T(1,128)S(1)} %copy-done.16, f32[1,21600]{1,0:T(1,128)S(1)} %copy-done.17), kind=kLoop, calls=%fused_computation.17 | loop fusion | flops 324000 | bytes 777600 | tf_op jit(solution)/shard_map/add | solution.py:677
  122.6 0.0 copy-done.13
  122.6 0.0 copy-done.4
  122.6 0.0 copy-done.8
  122.6 0.0 copy-done.9
  122.6 0.0 copy-done.10
  122.6 0.0 copy-done.11
  122.6 0.0 copy-done.12
  122.7 0.0 copy-start.1
  122.7 1.0 multiply_add_fusion.2
  123.6 0.6 copy-done.1
  124.2 0.0 copy-start
  124.2 0.9 copy.70
  125.1 0.6 copy-done
  125.8 0.9 copy.71
  (23 shorter events, 0.4 us)
Async XLA Ops:
  0.7 1.0 copy-start.6
  2.0 0.9 copy-start.3
  3.0 0.9 copy-start.2
  4.8 111.8 %copy-start.18 = (f32[4,480]{1,0:T(4,128)S(1)}, f32[4,480]{1,0:T(4,128)}, u32[]{:S(2)}) copy-start(f32[4,480]{1,0:T(4,128)} %refs_6_.1) | copy-start | bytes 23044
  4.8 111.8 %copy-start.19 = (f32[4,480]{1,0:T(4,128)S(1)}, f32[4,480]{1,0:T(4,128)}, u32[]{:S(2)}) copy-start(f32[4,480]{1,0:T(4,128)} %param.52) | copy-start | bytes 23044
  115.6 4.0 %copy-start.5 = (f32[47,16,128]{2,1,0:T(8,128)S(1)}, f32[47,16,128]{2,1,0:T(8,128)}, u32[]{:S(2)}) copy-start(f32[47,16,128]{2,1,0:T(8,128)} %get-tuple-element.28) | copy-start | bytes 1155076
  116.6 1.4 %copy-start.14 = (f32[1,7200]{1,0:T(1,128)S(1)}, f32[1,7200]{1,0:T(1,128)}, u32[]{:S(2)}) copy-start(f32[1,7200]{1,0:T(1,128)} %param.37) | copy-start | bytes 86404
  120.2 0.9 copy-start.15
  120.2 0.9 copy-start.16
  120.2 1.0 copy-start.17
  120.3 1.0 copy-start.7
  120.3 2.3 %copy-start.13 = (f32[28800]{0:T(1024)S(1)}, f32[28800]{0:T(1024)}, u32[]{:S(2)}) copy-start(f32[28800]{0:T(1024)} %param.44) | copy-start | bytes 345604
  121.2 1.4 %copy-start.4 = (f32[28800]{0:T(1024)S(1)}, f32[28800]{0:T(1024)}, u32[]{:S(2)}) copy-start(f32[28800]{0:T(1024)} %param.41) | copy-start | bytes 345604
  121.3 1.4 %copy-start.8 = (f32[28800]{0:T(1024)S(1)}, f32[28800]{0:T(1024)}, u32[]{:S(2)}) copy-start(f32[28800]{0:T(1024)} %param.48) | copy-start | bytes 345604
  121.3 1.4 %copy-start.9 = (f32[28800]{0:T(1024)S(1)}, f32[28800]{0:T(1024)}, u32[]{:S(2)}) copy-start(f32[28800]{0:T(1024)} %param.47) | copy-start | bytes 345604
  121.3 1.4 %copy-start.10 = (f32[28800]{0:T(1024)S(1)}, f32[28800]{0:T(1024)}, u32[]{:S(2)}) copy-start(f32[28800]{0:T(1024)} %param.46) | copy-start | bytes 345604
  121.3 1.4 %copy-start.11 = (f32[28800]{0:T(1024)S(1)}, f32[28800]{0:T(1024)}, u32[]{:S(2)}) copy-start(f32[28800]{0:T(1024)} %param.43) | copy-start | bytes 345604
  121.3 1.4 %copy-start.12 = (f32[28800]{0:T(1024)S(1)}, f32[28800]{0:T(1024)}, u32[]{:S(2)}) copy-start(f32[28800]{0:T(1024)} %param.42) | copy-start | bytes 345604
  122.7 1.5 %copy-start.1 = (f32[480,512]{1,0:T(8,128)S(1)}, f32[480,512]{1,0:T(8,128)}, u32[]{:S(2)}) copy-start(f32[480,512]{1,0:T(8,128)} %get-tuple-element.26) | copy-start | bytes 2949124
  124.2 1.6 %copy-start = (f32[480,512]{1,0:T(8,128)S(1)}, f32[480,512]{1,0:T(8,128)}, u32[]{:S(2)}) copy-start(f32[480,512]{1,0:T(8,128)} %get-tuple-element.27) | copy-start | bytes 2949124
